TPU v7x, 32 devices: a whole 2x2x4 slice. The times are simulated.
32 devices in a mesh: row: 8 (over y, x, core), col: 4 (over z).
Axes of the slice: x: 2, y: 2, z: 4, core: 2. Of those that a mesh axis runs over, the one named last changes fastest.
Arguments:
- inverse_blocks: bfloat16 [8, 384, 256, 256], P('row', 'col'), may hold values from -6 to 6
- inverse_rows: int32 [8, 384], P('row', 'col'), may hold values from 0 to 95, as said below
- inverse_cols: int32 [8, 384], P('row', 'col'), may hold values from 0 to 95, as said below
- inverse_count: int32 [8, 4], P('row', 'col'), may hold values from 1 to 96, as said below
- panel_rows: int32 [16], replicated, may hold values from -1 to 95, as said below
- lower_old: bfloat16 [3, 16, 256, 256], P(None, 'row'), may hold values from -0.038085938 to 0.038085938
- lower_new: bfloat16 [3, 3, 256, 256], replicated, may hold values from -0.375 to 0.375
- diag_inverse: float32 [3, 256, 256], replicated, may hold values from -6 to 6
Outputs:
- panel_inverse: bfloat16 [3, 16, 256, 256], P(None, 'row', 'col')
- supernode_inverse: float32 [3, 3, 256, 256], replicated
Inputs may be any that keep to these rules, and one draw needn't show every extreme that they name: `panel_rows`: for each row index r in order, 2 entries: distinct block rows congruent to r modulo the number of row indices, at least one, then -1 in the empty slots; some row index fills all 2 in every draw. `inverse_rows`: on row index r every slot names one of the panel rows of r, padding slots too. `inverse_cols`: on column index c every slot names a block column congruent to c modulo the number of column indices; positions may repeat, and repeated blocks add. `inverse_count`: slots 0 to count - 1 of a device's lists are live, the rest padding; one device reaches 96 in every draw.
All inputs are finite; a program needn't handle non-finite values.
Results may differ from a plain program's by a relative error of at most 0.0045.
Values may be sent and summed in bfloat16 or wider, within the bound.
No kernel may reach another device: no remote copies, remote signals or barrier semaphores. Data moves between devices by JAX's collectives and lax.ppermute only.
A program may use at most 128 MiB of HBM per device.

v0:
```python
import functools

import jax
import jax.numpy as jnp
from jax import lax
from jax.experimental import pallas as pl
from jax.experimental.pallas import tpu as pltpu
from jax.sharding import PartitionSpec as P


BF16 = jnp.bfloat16
F32 = jnp.float32
VMEM = pl.BlockSpec(memory_space=pltpu.VMEM)
ANY = pl.BlockSpec(memory_space=pl.ANY)
SMEM = pl.BlockSpec(memory_space=pltpu.SMEM)
DEPTH = 8


def permute(value, pairs):
    return lax.ppermute(value, ("row", "col"), pairs)


def gather_kernel(groups, slots, me, count, rows_in, cols_in, panel_in, blocks, *refs):
    w_outs = refs[:groups]
    acc, w, order, code, buf, rows_ref, cols_ref, panel, sem, out_sem, in_sem = refs[groups:]
    width = buf.shape[-1]
    n_cand = groups * slots
    row_me = me[0]
    tables = ((rows_in, rows_ref), (cols_in, cols_ref), (panel_in, panel))
    brought = [pltpu.make_async_copy(*pair, in_sem.at[i]) for i, pair in enumerate(tables)]
    for copy in brought:
        copy.start()
    acc[...] = jnp.zeros_like(acc)
    for copy in brought:
        copy.wait()
    own = [panel[row_me * slots + s] for s in range(slots)]
    cand = [panel[me[1 + g] * slots + s] for g in range(groups) for s in range(slots)]
    step_size = 8 if rows_ref.shape[1] % 8 == 0 else 1

    def scan(step, n):
        for u in range(step_size):
            k = step * step_size + u
            row, col = rows_ref[0, k], cols_ref[0, k]
            where = jnp.int32(-1)
            for p in range(n_cand):
                where = jnp.where(col == cand[p], p, where)
            slot = jnp.int32(-1)
            for s in range(slots):
                slot = jnp.where(row == own[s], s, slot)
            order[n] = k
            code[n] = slot * n_cand + where
            used = (where >= 0) & (slot >= 0) & (k < count[0, 0])
            n = n + used.astype(jnp.int32)
        return n

    n_steps = (count[0, 0] + step_size - 1) // step_size
    n_used = lax.fori_loop(0, n_steps, scan, jnp.int32(0))

    def fetch(i):
        slot = lax.rem(i, DEPTH)
        return pltpu.make_async_copy(blocks.at[order[i]], buf.at[slot], sem.at[slot])

    for i in range(DEPTH):

        @pl.when(i < n_used)
        def _():
            fetch(jnp.int32(i)).start()

    def step(i, carry):
        fetch(i).wait()
        target = code[i]
        slot = lax.rem(i, DEPTH)
        acc[target] += buf[slot].astype(F32)

        @pl.when(i + DEPTH < n_used)
        def _():
            fetch(i + DEPTH).start()

        return carry

    lax.fori_loop(0, n_used, step, 0)
    for g in range(groups):
        for s in range(slots):
            for p in range(slots):
                rows = pl.ds(s * width, width)
                cols = pl.ds(p * width, width)
                value = acc[s * n_cand + g * slots + p]
                high = value.astype(BF16)
                w[g, 0, rows, cols] = high
                w[g, 1, rows, cols] = (value - high.astype(F32)).astype(BF16)
        pltpu.make_async_copy(w.at[g], w_outs[g], out_sem.at[g]).start()
    for g in range(groups):
        pltpu.make_async_copy(w.at[g], w_outs[g], out_sem.at[g]).wait()


def fill(where, options, lo, sems):
    count, slots, width = options[0].shape[:3]

    def copies(part, t):
        return [
            pltpu.make_async_copy(
                part.at[t, p], lo.at[t, pl.ds(p * width, width), :], sems.at[t, p]
            )
            for p in range(slots)
        ]

    for case, part in enumerate(options):

        @pl.when(where[0] == case)
        def _():
            for t in range(count):
                for copy in copies(part, t):
                    copy.start()

    def wait(t):
        for copy in copies(options[0], t):
            copy.wait()

    return wait


def own_kernel(where, w_in, *refs):
    options, (p_out, w, lo, w_sem, sems) = refs[:-5], refs[-5:]
    w_copy = pltpu.make_async_copy(w_in, w, w_sem)
    w_copy.start()
    wait = fill(where, options, lo, sems)
    w_copy.wait()
    for t in range(lo.shape[0]):
        wait(t)
        lo_t = lo[t]
        running = jnp.dot(w[0], lo_t, preferred_element_type=F32)
        p_out[t] = running + jnp.dot(w[1], lo_t, preferred_element_type=F32)


def piece_index(core, value, j, count):
    return jnp.where(core == 0, 2 * j + value, value * count + j)


def main_kernel(n_high, n_col, where, p_own, old, new, *refs):
    t_count = new.shape[0]
    slots = old.shape[1]
    n_far = n_high - 1
    w_ins, parts = refs[:n_far], refs[n_far:-8]
    u_keep, u_send, g_keep, g_send, lo, u_all, g_all, sems = refs[-8:]
    width = new.shape[-1]
    part_rows = slots * width
    cases = len(parts) // max(n_far, 1)
    waits = [
        fill(where, parts[g * cases : (g + 1) * cases], lo.at[g], sems.at[g]) for g in range(n_far)
    ]
    panels = []
    index = 0
    for t in range(t_count):
        running = p_own[t]
        for g in range(n_high - 1):
            waits[g](t)
            lo_t = lo[g, t]
            running += jnp.dot(w_ins[g][0], lo_t, preferred_element_type=F32)
            running += jnp.dot(w_ins[g][1], lo_t, preferred_element_type=F32)
        for s in range(t):
            running += jnp.dot(panels[s], new[t, s], preferred_element_type=F32)
        current = -running
        u_all[t] = current
        panels.append(current.astype(BF16))
        own = old[t].reshape(part_rows, width)
        for s in range(t + 1):
            left, right = (own, panels[t]) if s == t else (panels[s], own)
            g_all[pl.ds(index * width, width), :] = lax.dot_general(
                left, right, (((0,), (0,)), ((), ())), preferred_element_type=F32
            )
            index += 1
    half = g_keep.shape[0]
    g_keep[...] = g_all[pl.ds(pl.multiple_of(where[1] * half, 16), half), :]
    g_send[...] = g_all[pl.ds(pl.multiple_of((1 - where[1]) * half, 16), half), :].astype(BF16)
    share = width // n_col
    count = n_col // 2
    for value, out in ((where[4], u_keep), (1 - where[4], u_send)):
        for j in range(count):
            start = piece_index(where[1], value, j, count) * share
            for t in range(t_count):
                for s in range(slots):
                    window = pl.ds(pl.multiple_of(s * width + start, 16), share)
                    out[j, t, s] = u_all[t, window, :].astype(out.dtype)


def halving_kernel(bit, where, keep, received, keep_out, send_out):
    count = keep_out.shape[0]
    for value, out in ((where[bit], keep_out), (1 - where[bit], send_out)):
        for j in range(count):
            index = piece_index(where[1], value, j, count)
            out[j] = (keep[index] + received[index].astype(F32)).astype(out.dtype)


def split_kernel(where, keep, received, own, *sends):
    def piece(m):
        index = where[3] ^ m
        return keep[index] + received[index].astype(F32)

    own[...] = piece(0)
    for m, send in enumerate(sends):
        send[...] = piece(m + 1).astype(BF16)


def tree(values):
    while len(values) > 1:
        values = [a + b for a, b in zip(values[::2], values[1::2])]
    return values[0]


def add_kernel(*refs):
    out = refs[-1]
    out[...] = tree([ref[...].astype(F32) for ref in refs[:-1]]).astype(out.dtype)


def wide_dot(left, right, dims):
    dims = (dims, ((), ()))
    if left.dtype == F32:
        high = left.astype(BF16)
        low = (left - high.astype(F32)).astype(BF16)
        return lax.dot_general(high, right, dims, preferred_element_type=F32) + lax.dot_general(
            low, right, dims, preferred_element_type=F32
        )
    high = right.astype(BF16)
    low = (right - high.astype(F32)).astype(BF16)
    return lax.dot_general(left, high, dims, preferred_element_type=F32) + lax.dot_general(
        left, low, dims, preferred_element_type=F32
    )


def final_kernel(where, new, diag, *refs):
    pieces, (out, g_all, y, zero, sems) = refs[:-5], refs[-5:]
    t_count = new.shape[0]
    width = new.shape[-1]
    n_plane = len(pieces) // 2
    rows = pieces[0].shape[0]
    for i, piece in enumerate(pieces):
        core, chip = where[1] ^ i // n_plane, where[3] ^ i % n_plane
        place = (core * n_plane + chip) * rows
        g_all[pl.ds(pl.multiple_of(place, 16), rows), :] = piece[...]

    def g(t, s):
        index = t * (t + 1) // 2 + s
        return g_all[pl.ds(index * width, width), :].astype(F32)

    def give(source, t, s):
        copy = pltpu.make_async_copy(source, out.at[t, s], sems.at[t, s])
        copy.start()
        sent.append(copy)

    sent = []
    zero[...] = jnp.zeros_like(zero)
    for t in range(t_count):
        for s in range(t + 1, t_count):
            give(zero, t, s)
    blocks = {}
    for t in range(t_count):
        for s in range(t):
            crossed = g(t, s)
            for u in range(t):
                if u >= s:
                    crossed += wide_dot(blocks[u, s], new[t, u], ((1,), (0,)))
                else:
                    crossed += wide_dot(blocks[s, u], new[t, u], ((0,), (0,)))
            blocks[t, s] = -crossed
            y[t, s] = blocks[t, s]
            give(y.at[t, s], t, s)
        diagonal = diag[t] - g(t, t)
        for s in range(t):
            diagonal -= wide_dot(new[t, s], blocks[t, s], ((0,), (0,)))
        blocks[t, t] = diagonal
        y[t, t] = diagonal
        give(y.at[t, t], t, t)
    for copy in sent:
        copy.wait()


def call(kernel, shapes, in_specs, scratch=(), flops=0, moved=0, limit=8):
    def place(shape):
        if not isinstance(shape, jax.ShapeDtypeStruct):
            return ANY
        return SMEM if shape.dtype == jnp.int32 else VMEM

    return pl.pallas_call(
        kernel,
        out_shape=shapes,
        in_specs=in_specs,
        out_specs=tuple(map(place, shapes)) if isinstance(shapes, tuple) else place(shapes),
        scratch_shapes=list(scratch),
        cost_estimate=pl.CostEstimate(flops=flops, bytes_accessed=moved, transcendentals=0),
        compiler_params=pltpu.CompilerParams(vmem_limit_bytes=limit << 20),
    )


def per_device(
    inverse_blocks,
    inverse_rows,
    inverse_cols,
    inverse_count,
    panel_rows,
    lower_old,
    lower_new,
    diag_inverse,
):
    blocks = inverse_blocks[0]
    kmax = blocks.shape[0]
    width = blocks.shape[-1]
    t_count, slots = lower_old.shape[:2]
    n_row = lax.axis_size("row")
    n_col = lax.axis_size("col")
    row_me = lax.axis_index("row")
    col_me = lax.axis_index("col")
    devices = [(r, c) for r in range(n_row) for c in range(n_col)]
    n_high = n_row // n_col
    n_plane = n_row // 2

    def pairs(active, partner):
        return [
            (r * n_col + c, pr * n_col + pc)
            for r, c in devices
            if active(r, c)
            for pr, pc in [partner(r, c)]
        ]

    high_me = row_me // n_col
    groups = [((high_me ^ g) * n_col + col_me) for g in range(n_high)]
    n_cand = n_high * slots
    me = jnp.stack([row_me, *groups]).astype(jnp.int32)
    source = (row_me ^ col_me) & (n_col - 1)
    core_me = row_me & 1
    chip_me = row_me >> 1
    col_bits = n_col.bit_length() - 1

    def bit_of(value, bits, i):
        return jnp.where(core_me == 0, value >> i, value >> bits - 1 - i) & 1

    where = jnp.stack(
        [source, core_me, col_me, chip_me] + [bit_of(col_me, col_bits, i) for i in range(col_bits)]
    ).astype(jnp.int32)

    block = width * width
    anyone = lambda r, c: True

    def core_swap(value):
        return permute(value, pairs(anyone, lambda r, c: (r ^ 1, c)))

    def spread(group, offset, core, land=0):
        table = {}
        for r, c in devices:
            if r % n_col == c:
                table[r ^ core, c] = ((r // n_col ^ group) * n_col + (c ^ offset) ^ land, c)
        targets = set(table.values())
        for r, c in devices:
            if (r ^ c) & 1 == 0:
                for taker in (r, r ^ 1):
                    for giver in (taker ^ 1, taker) if core else (taker ^ 1,):
                        if (giver, c) not in table and (taker, c) not in targets:
                            table[giver, c] = (taker, c)
                            targets.add((taker, c))
        return [(r * n_col + c, pr * n_col + pc) for (r, c), (pr, pc) in table.items()]

    offsets = list(range(0, n_col, 2))
    sibling = core_swap(lower_old)
    own_parts = [lower_old, sibling]
    for o in offsets[1:]:
        part = permute(lower_old, spread(0, o, 0))
        own_parts += [part, core_swap(part)]
    far = {}
    for g in range(1, n_high):
        far[g, 0] = permute(lower_old, spread(g, 0, 0, 1))
    for g in range(1, n_high):
        for o in offsets[1:]:
            far[g, o] = permute(sibling, spread(g, o, 1))
    far_parts = []
    for g in range(1, n_high):
        for o in offsets:
            both = [far[g, o], core_swap(far[g, o])]
            far_parts += both if o else both[::-1]

    w_shape = (2, slots * width, slots * width)
    ws = call(
        functools.partial(gather_kernel, n_high, slots),
        (pltpu.MemorySpace.HBM(w_shape, BF16),) * n_high,
        [SMEM, SMEM] + [ANY] * 4,
        [
            pltpu.VMEM((slots * n_cand, width, width), F32),
            pltpu.VMEM((n_high, *w_shape), BF16),
            pltpu.SMEM((kmax,), jnp.int32),
            pltpu.SMEM((kmax,), jnp.int32),
            pltpu.VMEM((DEPTH, width, width), BF16),
            pltpu.SMEM(inverse_rows.shape, jnp.int32),
            pltpu.SMEM(inverse_cols.shape, jnp.int32),
            pltpu.SMEM(panel_rows.shape, jnp.int32),
            pltpu.SemaphoreType.DMA((DEPTH,)),
            pltpu.SemaphoreType.DMA((n_high,)),
            pltpu.SemaphoreType.DMA((3,)),
        ],
        flops=block * 16,
        moved=16 * block * 2 + 16 * n_cand * slots * block,
        limit=6 + (slots * n_cand * 8 * block + DEPTH * 2 * block) // 2**20,
    )(
        me,
        inverse_count,
        *[
            pltpu.with_memory_space_constraint(value, pltpu.MemorySpace.HBM)
            for value in (inverse_rows, inverse_cols, panel_rows, blocks)
        ],
    )
    p_shape = (t_count, slots * width, width)
    p_own = call(
        own_kernel,
        jax.ShapeDtypeStruct(p_shape, F32),
        [SMEM, ANY] + [ANY] * len(own_parts),
        [
            pltpu.VMEM(w_shape, BF16),
            pltpu.VMEM(p_shape, BF16),
            pltpu.SemaphoreType.DMA,
            pltpu.SemaphoreType.DMA((t_count, slots)),
        ],
        flops=4 * block * width * slots * slots * t_count,
        moved=8 * block * t_count * slots,
        limit=12,
    )(
        where,
        pltpu.with_memory_space_constraint(ws[0], pltpu.MemorySpace.HBM),
        *own_parts,
    )

    share = width // n_col
    n_blocks = t_count * (t_count + 1) // 2
    half = n_blocks * width // 2
    piece = half // n_plane
    u_shape = (n_col // 2, t_count, slots, share, width)
    u_keep, u_send, g_keep, g_send = call(
        functools.partial(main_kernel, n_high, n_col),
        (
            jax.ShapeDtypeStruct(u_shape, F32),
            jax.ShapeDtypeStruct(u_shape, BF16),
            jax.ShapeDtypeStruct((half, width), F32),
            jax.ShapeDtypeStruct((half, width), BF16),
        ),
        [SMEM, VMEM, VMEM, VMEM] + [VMEM] * (n_high - 1) + [ANY] * len(far_parts),
        [
            pltpu.VMEM((n_high - 1, t_count, slots * width, width), BF16),
            pltpu.VMEM((t_count, slots * width, width), F32),
            pltpu.VMEM((n_blocks * width, width), F32),
            pltpu.SemaphoreType.DMA((n_high - 1, t_count, slots)),
        ],
        flops=2 * block * width * slots * t_count * (2 * n_cand + 4),
        moved=4 * block * t_count * n_cand,
        limit=12 + 2 * n_high,
    )(where, p_own, lower_old, lower_new, *ws[1:], *far_parts)

    def step(index):
        return pairs(
            anyone, lambda r, c: (r, c ^ 1 << (index if r & 1 == 0 else col_bits - 1 - index))
        )

    def halve(position, keep, received):
        shape = (keep.shape[0] // 2, *keep.shape[1:])
        return call(
            functools.partial(halving_kernel, position),
            (jax.ShapeDtypeStruct(shape, F32), jax.ShapeDtypeStruct(shape, BF16)),
            [SMEM, VMEM, VMEM],
            flops=keep.size,
            moved=keep.size * 6,
        )(where, keep, received)

    def add(dtype, values):
        return call(
            add_kernel,
            jax.ShapeDtypeStruct(values[0].shape, dtype),
            [VMEM] * len(values),
            flops=len(values) * values[0].size,
            moved=values[0].size * 2 * len(values),
        )(*values)

    keep = g_keep.reshape(n_plane, piece, width)
    received = core_swap(g_send)
    u_received = permute(u_send, step(0))
    shape = (piece, width)
    own, *sends = call(
        split_kernel,
        (jax.ShapeDtypeStruct(shape, F32), *[jax.ShapeDtypeStruct(shape, BF16)] * (n_plane - 1)),
        [SMEM, VMEM, VMEM],
        flops=half * width,
        moved=half * width * 8,
    )(where, keep, received.reshape(keep.shape))
    arrived = [
        permute(send, pairs(anyone, lambda r, c: (r ^ 2 * (m + 1), c)))
        for m, send in enumerate(sends)
    ]
    in_plane = add(BF16, [own, *arrived])
    level = [in_plane] + [
        permute(in_plane, pairs(anyone, lambda r, c: (r, c ^ m))) for m in range(1, n_col)
    ]
    for i in range(1, col_bits):
        u_keep, u_send = halve(5 + i - 1, u_keep, u_received)
        u_received = permute(u_send, step(i))
    total = add(BF16, level)
    pieces = [total] + [
        permute(total, pairs(anyone, lambda r, c: (r ^ 2 * m, c))) for m in range(1, n_plane)
    ]
    pieces += [core_swap(value) for value in pieces]
    supernode_inverse = call(
        final_kernel,
        pltpu.MemorySpace.HBM((t_count, t_count, width, width), F32),
        [SMEM] + [VMEM] * (2 + len(pieces)),
        [
            pltpu.VMEM((n_blocks * width, width), BF16),
            pltpu.VMEM((t_count, t_count, width, width), F32),
            pltpu.VMEM((width, width), F32),
            pltpu.SemaphoreType.DMA((t_count, t_count)),
        ],
        flops=2 * block * width * 16,
        moved=block * t_count * t_count * 6,
    )(where, lower_new, diag_inverse, *pieces)
    panel_inverse = add(BF16, [u_keep, u_received])[0]
    return (panel_inverse, supernode_inverse)


def solution(mesh):
    placed = (
        P("row", "col", None, None),
        P("row", "col"),
        P("row", "col"),
        P("row", "col"),
        P(),
        P(None, "row", None, None),
        P(),
        P(),
    )
    return jax.shard_map(
        per_device,
        mesh=mesh,
        in_specs=placed,
        out_specs=(P(None, "row", "col", None), P()),
        check_vma=False,
    )
```

profile of v0, /device:TPU:0, one launch (start us, length us, event | category | flops | bytes accessed | tf_op | source)
XLA Modules:
  0.0 74.2 jit_solution(4668881446757873815)
XLA Ops:
  0.6 0.6 collective-permute-start
  1.2 4.4 %collective-permute-start.1 = (bf16[3,2,256,256]{3,2,1,0:T(8,128)(2,1)}, bf16[3,2,256,256]{3,2,1,0:T(8,128)(2,1)S(1)}, u32[]{:S(2)}, u32[]{:S(2)}) collective-permute-start(bf16[3,2,256,256]{3,2,1,0:T(8,128)(2,1)} %old.1), channel_id=1, source_target_pairs={{0,8},{5,13},{10,2},{15,7},{16,24},{21,29},{26,18},{31,23},{4,0},{... | collective-permute-start | bytes 2359304 | tf_op jit(solution)/shard_map/ppermute | solution.py:20
  5.6 0.2 collective-permute-start.3
  5.8 0.0 collective-permute-done.refs_1_
  5.8 1.5 %collective-permute-start.5 = (bf16[3,2,256,256]{3,2,1,0:T(8,128)(2,1)S(1)}, bf16[3,2,256,256]{3,2,1,0:T(8,128)(2,1)}, u32[]{:S(2)}, u32[]{:S(2)}) collective-permute-start(bf16[3,2,256,256]{3,2,1,0:T(8,128)(2,1)S(1)} %collective-permute-done.refs_1_), channel_id=1, source_target_pairs={{4,24},{1,29},{14,18},{11,23},{20,8},{17,13},{30,2},{27,7},{0,0},{... | collective-permute-start | bytes 2359304 | tf_op jit(solution)/shard_map/ppermute | solution.py:20
  7.4 13.8 %collective-permute-done.1.refs_2_ = bf16[3,2,256,256]{3,2,1,0:T(8,128)(2,1)S(1)} collective-permute-done((bf16[3,2,256,256]{3,2,1,0:T(8,128)(2,1)}, bf16[3,2,256,256]{3,2,1,0:T(8,128)(2,1)S(1)}, u32[]{:S(2)}, u32[]{:S(2)}) %collective-permute-start.1) | collective-permute-done | bytes 786464 | tf_op jit(solution)/shard_map/ppermute | solution.py:20
  21.2 0.0 collective-permute-start.2
  21.2 0.0 collective-permute-done.3.refs_2_
  21.2 0.5 collective-permute-start.4
  21.7 0.0 collective-permute-done.5.refs_3_
  21.7 2.1 %collective-permute-start.6 = (bf16[3,2,256,256]{3,2,1,0:T(8,128)(2,1)}, bf16[3,2,256,256]{3,2,1,0:T(8,128)(2,1)}, u32[]{:S(2)}, u32[]{:S(2)}) collective-permute-start(bf16[3,2,256,256]{3,2,1,0:T(8,128)(2,1)} %collective-permute-done.5.refs_3_), channel_id=1, source_target_pairs={{0,4},{1,5},{2,6},{3,7},{4,0},{5,1},{6,2},{7,3},{8,12},{9,13},{10,... | collective-permute-start | bytes 2359304 | tf_op jit(solution)/shard_map/ppermute | solution.py:20
  24.5 0.1 stack.39.where
  24.6 0.1 pad_add_fusion.me
  24.6 0.0 copy-start.1
  24.7 3.9 %shard_map.95 = (bf16[2,512,512]{2,1,0:T(8,128)(2,1)}, bf16[2,512,512]{2,1,0:T(8,128)(2,1)}) custom-call(s32[3]{0:T(128)S(1)} %pad_add_fusion.me, s32[1,1]{1,0:T(1,128)S(6)} %copy.10.count, s32[1,96]{1,0:T(1,128)} %rows_in.1, s32[1,96]{1,0:T(1,128)} %cols_in.1, s32[16]{0:T(128)} %panel_in.1, bf16[96,256,256]{2,1,0:T(8,128)(2,1)} %bitcast.15), custom_call_target="tpu_custom_call" | custom-call | flops 1048576 | bytes 10485760 | tf_op jit(solution)/shard_map/pallas_call | solution.py:380
  28.5 0.0 collective-permute-done.2.refs_3_
  28.6 0.0 copy-done.1
  28.6 0.0 copy-start
  28.6 0.0 copy-start.3
  28.6 3.8 %shard_map.96.p_own = f32[3,512,256]{2,1,0:T(8,128)S(1)} custom-call(s32[6]{0:T(128)S(1)} %stack.39.where, bf16[2,512,512]{2,1,0:T(8,128)(2,1)} %get-tuple-element.14.w_in, bf16[3,2,256,256]{3,2,1,0:T(8,128)(2,1)S(1)} %copy-done.1, bf16[3,2,256,256]{3,2,1,0:T(8,128)(2,1)S(1)} %collective-permute-done.refs_1_, ...), custom_call_target="tpu_custom_call" | custom-call | flops 805306368 | bytes 3145728 | tf_op jit(solution)/shard_map/pallas_call | solution.py:409
  32.4 0.0 collective-permute-done.4.refs_1_
  32.4 0.0 collective-permute-done.6.refs_4_
  32.4 0.0 copy-done
  32.4 0.0 copy-done.3
  32.4 4.6 %shard_map.97 = (f32[2,3,2,64,256]{4,3,2,1,0:T(8,128)S(1)}, bf16[2,3,2,64,256]{4,3,2,1,0:T(8,128)(2,1)S(1)}, f32[768,256]{1,0:T(8,128)S(1)}, bf16[768,256]{1,0:T(8,128)(2,1)S(1)}) custom-call(s32[6]{0:T(128)S(1)} %stack.39.where, f32[3,512,256]{2,1,0:T(8,128)S(1)} %shard_map.96.p_own, bf16[3,2,256,256]{3,2,1,0:T(8,128)(2,1)S(1)} %copy-done.1, ...), custom_call_target="tpu_custom_call" | custom-call | flops 2415919104 | bytes 3145728 | tf_op jit(solution)/shard_map/pallas_call | solution.py:433
  37.0 0.0 copy-start.2
  37.0 0.4 collective-permute-start.9
  37.4 2.5 %collective-permute-start.7 = (bf16[2,3,2,64,256]{4,3,2,1,0:T(8,128)(2,1)S(1)}, bf16[2,3,2,64,256]{4,3,2,1,0:T(8,128)(2,1)S(1)}, u32[]{:S(2)}, u32[]{:S(2)}) collective-permute-start(bf16[2,3,2,64,256]{4,3,2,1,0:T(8,128)(2,1)S(1)} %get-tuple-element.17), channel_id=1, source_target_pairs={{0,1},{1,0},{2,3},{3,2},{4,6},{5,7},{6,4},{7,5},{8,9},{9,8},{10,11... | collective-permute-start | bytes 1179656 | tf_op jit(solution)/shard_map/ppermute | solution.py:20
  40.0 0.0 collective-permute-done.9
  40.0 0.6 shard_map.100
  40.6 3.0 %collective-permute-start.10 = (bf16[192,256]{1,0:T(8,128)(2,1)S(1)}, bf16[192,256]{1,0:T(8,128)(2,1)S(1)}, u32[]{:S(2)}, u32[]{:S(2)}) collective-permute-start(bf16[192,256]{1,0:T(8,128)(2,1)S(1)} %get-tuple-element.23), channel_id=1, source_target_pairs={{0,8},{1,9},{2,10},{3,11},{4,12},{5,13},{6,14},{7,15},{8,0},{9,1},... | collective-permute-start | bytes 294920 | tf_op jit(solution)/shard_map/ppermute | solution.py:20
  43.6 1.0 %collective-permute-start.11 = (bf16[192,256]{1,0:T(8,128)(2,1)S(1)}, bf16[192,256]{1,0:T(8,128)(2,1)S(1)}, u32[]{:S(2)}, u32[]{:S(2)}) collective-permute-start(bf16[192,256]{1,0:T(8,128)(2,1)S(1)} %get-tuple-element.24), channel_id=1, source_target_pairs={{0,16},{1,17},{2,18},{3,19},{4,20},{5,21},{6,22},{7,23},{8,24},{9,... | collective-permute-start | bytes 294920 | tf_op jit(solution)/shard_map/ppermute | solution.py:20
  44.6 0.5 collective-permute-start.12
  45.1 1.6 %collective-permute-done.10.refs_1_ = bf16[192,256]{1,0:T(8,128)(2,1)S(1)} collective-permute-done((bf16[192,256]{1,0:T(8,128)(2,1)S(1)}, bf16[192,256]{1,0:T(8,128)(2,1)S(1)}, u32[]{:S(2)}, u32[]{:S(2)}) %collective-permute-start.10) | collective-permute-done | bytes 98336 | tf_op jit(solution)/shard_map/ppermute | solution.py:20
  46.7 4.4 %collective-permute-done.11.refs_2_ = bf16[192,256]{1,0:T(8,128)(2,1)S(1)} collective-permute-done((bf16[192,256]{1,0:T(8,128)(2,1)S(1)}, bf16[192,256]{1,0:T(8,128)(2,1)S(1)}, u32[]{:S(2)}, u32[]{:S(2)}) %collective-permute-start.11) | collective-permute-done | bytes 98336 | tf_op jit(solution)/shard_map/ppermute | solution.py:20
  51.1 0.0 collective-permute-done.12.refs_3_
  51.2 0.7 collective-permute-start.13
  51.9 1.5 %collective-permute-start.14 = (bf16[192,256]{1,0:T(8,128)(2,1)S(1)}, bf16[192,256]{1,0:T(8,128)(2,1)S(1)}, u32[]{:S(2)}, u32[]{:S(2)}) collective-permute-start(bf16[192,256]{1,0:T(8,128)(2,1)S(1)} %shard_map.101.refs_0_), channel_id=1, source_target_pairs={{0,2},{1,3},{2,0},{3,1},{4,6},{5,7},{6,4},{7,5},{8,10},{9,11},{10,... | collective-permute-start | bytes 294920 | tf_op jit(solution)/shard_map/ppermute | solution.py:20
  53.4 2.2 %collective-permute-start.15 = (bf16[192,256]{1,0:T(8,128)(2,1)S(1)}, bf16[192,256]{1,0:T(8,128)(2,1)S(1)}, u32[]{:S(2)}, u32[]{:S(2)}) collective-permute-start(bf16[192,256]{1,0:T(8,128)(2,1)S(1)} %shard_map.101.refs_0_), channel_id=1, source_target_pairs={{0,3},{1,2},{2,1},{3,0},{4,7},{5,6},{6,5},{7,4},{8,11},{9,10},{10,... | collective-permute-start | bytes 294920 | tf_op jit(solution)/shard_map/ppermute | solution.py:20
  55.6 0.0 collective-permute-done.7.received
  55.6 0.6 shard_map.98
  56.2 1.1 %collective-permute-start.8 = (bf16[1,3,2,64,256]{4,3,2,1,0:T(8,128)(2,1)S(1)}, bf16[1,3,2,64,256]{4,3,2,1,0:T(8,128)(2,1)S(1)}, u32[]{:S(2)}, u32[]{:S(2)}) collective-permute-start(bf16[1,3,2,64,256]{4,3,2,1,0:T(8,128)(2,1)S(1)} %get-tuple-element.19), channel_id=1, source_target_pairs={{0,2},{1,3},{2,0},{3,1},{4,5},{5,4},{6,7},{7,6},{8,10},{9,11},{10,... | collective-permute-start | bytes 589832 | tf_op jit(solution)/shard_map/ppermute | solution.py:20
  57.3 0.0 collective-permute-done.13.refs_1_
  57.3 4.4 %collective-permute-done.14.refs_2_ = bf16[192,256]{1,0:T(8,128)(2,1)S(1)} collective-permute-done((bf16[192,256]{1,0:T(8,128)(2,1)S(1)}, bf16[192,256]{1,0:T(8,128)(2,1)S(1)}, u32[]{:S(2)}, u32[]{:S(2)}) %collective-permute-start.14) | collective-permute-done | bytes 98336 | tf_op jit(solution)/shard_map/ppermute | solution.py:20
  61.7 0.8 %collective-permute-done.15.refs_3_ = bf16[192,256]{1,0:T(8,128)(2,1)S(1)} collective-permute-done((bf16[192,256]{1,0:T(8,128)(2,1)S(1)}, bf16[192,256]{1,0:T(8,128)(2,1)S(1)}, u32[]{:S(2)}, u32[]{:S(2)}) %collective-permute-start.15) | collective-permute-done | bytes 98336 | tf_op jit(solution)/shard_map/ppermute | solution.py:20
  62.5 0.1 shard_map.102.refs_0_
  62.5 1.7 %collective-permute-start.16 = (bf16[192,256]{1,0:T(8,128)(2,1)S(1)}, bf16[192,256]{1,0:T(8,128)(2,1)S(1)}, u32[]{:S(2)}, u32[]{:S(2)}) collective-permute-start(bf16[192,256]{1,0:T(8,128)(2,1)S(1)} %shard_map.102.refs_0_), channel_id=1, source_target_pairs={{0,8},{1,9},{2,10},{3,11},{4,12},{5,13},{6,14},{7,15},{8,0},{9,1},... | collective-permute-start | bytes 294920 | tf_op jit(solution)/shard_map/ppermute | solution.py:20
  64.3 0.6 collective-permute-start.17
  64.9 1.2 %collective-permute-start.18 = (bf16[192,256]{1,0:T(8,128)(2,1)S(1)}, bf16[192,256]{1,0:T(8,128)(2,1)S(1)}, u32[]{:S(2)}, u32[]{:S(2)}) collective-permute-start(bf16[192,256]{1,0:T(8,128)(2,1)S(1)} %shard_map.102.refs_0_), channel_id=1, source_target_pairs={{0,24},{1,25},{2,26},{3,27},{4,28},{5,29},{6,30},{7,31},{8,16},{9,... | collective-permute-start | bytes 294920 | tf_op jit(solution)/shard_map/ppermute | solution.py:20
  66.1 0.0 collective-permute-start.19
  66.1 1.1 %collective-permute-done.16.refs_1_ = bf16[192,256]{1,0:T(8,128)(2,1)S(1)} collective-permute-done((bf16[192,256]{1,0:T(8,128)(2,1)S(1)}, bf16[192,256]{1,0:T(8,128)(2,1)S(1)}, u32[]{:S(2)}, u32[]{:S(2)}) %collective-permute-start.16) | collective-permute-done | bytes 98336 | tf_op jit(solution)/shard_map/ppermute | solution.py:20
  67.2 0.0 collective-permute-start.20
  67.2 1.7 %collective-permute-done.17.refs_2_ = bf16[192,256]{1,0:T(8,128)(2,1)S(1)} collective-permute-done((bf16[192,256]{1,0:T(8,128)(2,1)S(1)}, bf16[192,256]{1,0:T(8,128)(2,1)S(1)}, u32[]{:S(2)}, u32[]{:S(2)}) %collective-permute-start.17) | collective-permute-done | bytes 98336 | tf_op jit(solution)/shard_map/ppermute | solution.py:20
  68.9 0.0 collective-permute-start.21
  68.9 1.5 %collective-permute-done.18.refs_3_ = bf16[192,256]{1,0:T(8,128)(2,1)S(1)} collective-permute-done((bf16[192,256]{1,0:T(8,128)(2,1)S(1)}, bf16[192,256]{1,0:T(8,128)(2,1)S(1)}, u32[]{:S(2)}, u32[]{:S(2)}) %collective-permute-start.18) | collective-permute-done | bytes 98336 | tf_op jit(solution)/shard_map/ppermute | solution.py:20
  70.4 0.0 collective-permute-start.22
  70.4 0.0 collective-permute-done.8.refs_1_
  70.4 0.7 shard_map.99
  71.1 0.0 collective-permute-done.19.refs_4_
  71.1 0.0 collective-permute-done.20.refs_5_
  71.1 0.0 collective-permute-done.21.refs_6_
  71.2 0.6 collective-permute-done.22.refs_7_
  71.7 0.0 copy-done.2
  71.7 2.5 %shard_map.103 = f32[3,3,256,256]{3,2,1,0:T(8,128)} custom-call(s32[6]{0:T(128)S(1)} %stack.39.where, bf16[3,3,256,256]{3,2,1,0:T(8,128)(2,1)S(1)} %copy-done, f32[3,256,256]{2,1,0:T(8,128)S(1)} %copy-done.2, bf16[192,256]{1,0:T(8,128)(2,1)S(1)} %shard_map.102.refs_0_, bf16[192,256]{1,0:T(8,128)(2,1)S(1)} %collective-permute-done.16.refs_1_, ...), custom_call_target="tpu_custom_call" | custom-call | flops 536870912 | bytes 3538944 | tf_op jit(solution)/shard_map/pallas_call | solution.py:504
  (1 shorter events, 0.0 us)
Async XLA Ops:
  0.6 5.2 %collective-permute-start = (bf16[3,2,256,256]{3,2,1,0:T(8,128)(2,1)}, bf16[3,2,256,256]{3,2,1,0:T(8,128)(2,1)S(1)}, u32[]{:S(2)}, u32[]{:S(2)}) collective-permute-start(bf16[3,2,256,256]{3,2,1,0:T(8,128)(2,1)} %old.1), channel_id=1, source_target_pairs={{0,4},{1,5},{2,6},{3,7},{4,0},{5,1},{6,2},{7,3},{8,12},{9,13},{10,... | collective-permute-start | bytes 2359304 | tf_op jit(solution)/shard_map/ppermute | solution.py:20
  1.2 20.0 %collective-permute-start.1 = (bf16[3,2,256,256]{3,2,1,0:T(8,128)(2,1)}, bf16[3,2,256,256]{3,2,1,0:T(8,128)(2,1)S(1)}, u32[]{:S(2)}, u32[]{:S(2)}) collective-permute-start(bf16[3,2,256,256]{3,2,1,0:T(8,128)(2,1)} %old.1), channel_id=1, source_target_pairs={{0,8},{5,13},{10,2},{15,7},{16,24},{21,29},{26,18},{31,23},{4,0},{... | collective-permute-start | bytes 2359304 | tf_op jit(solution)/shard_map/ppermute | solution.py:20
  5.6 15.6 %collective-permute-start.3 = (bf16[3,2,256,256]{3,2,1,0:T(8,128)(2,1)}, bf16[3,2,256,256]{3,2,1,0:T(8,128)(2,1)S(1)}, u32[]{:S(2)}, u32[]{:S(2)}) collective-permute-start(bf16[3,2,256,256]{3,2,1,0:T(8,128)(2,1)} %old.1), channel_id=1, source_target_pairs={{0,20},{5,17},{10,30},{15,27},{16,4},{21,1},{26,14},{31,11},{4,0},... | collective-permute-start | bytes 2359304 | tf_op jit(solution)/shard_map/ppermute | solution.py:20
  5.8 15.9 %collective-permute-start.5 = (bf16[3,2,256,256]{3,2,1,0:T(8,128)(2,1)S(1)}, bf16[3,2,256,256]{3,2,1,0:T(8,128)(2,1)}, u32[]{:S(2)}, u32[]{:S(2)}) collective-permute-start(bf16[3,2,256,256]{3,2,1,0:T(8,128)(2,1)S(1)} %collective-permute-done.refs_1_), channel_id=1, source_target_pairs={{4,24},{1,29},{14,18},{11,23},{20,8},{17,13},{30,2},{27,7},{0,0},{... | collective-permute-start | bytes 2359304 | tf_op jit(solution)/shard_map/ppermute | solution.py:20
  21.2 7.4 %collective-permute-start.2 = (bf16[3,2,256,256]{3,2,1,0:T(8,128)(2,1)S(1)}, bf16[3,2,256,256]{3,2,1,0:T(8,128)(2,1)S(1)}, u32[]{:S(2)}, u32[]{:S(2)}) collective-permute-start(bf16[3,2,256,256]{3,2,1,0:T(8,128)(2,1)S(1)} %collective-permute-done.1.refs_2_), channel_id=1, source_target_pairs={{0,4},{1,5},{2,6},{3,7},{4,0},{5,1},{6,2},{7,3},{8,12},{9,13},{10,... | collective-permute-start | bytes 2359304 | tf_op jit(solution)/shard_map/ppermute | solution.py:20
  21.2 11.2 %collective-permute-start.4 = (bf16[3,2,256,256]{3,2,1,0:T(8,128)(2,1)S(1)}, bf16[3,2,256,256]{3,2,1,0:T(8,128)(2,1)}, u32[]{:S(2)}, u32[]{:S(2)}) collective-permute-start(bf16[3,2,256,256]{3,2,1,0:T(8,128)(2,1)S(1)} %collective-permute-done.3.refs_2_), channel_id=1, source_target_pairs={{0,4},{1,5},{2,6},{3,7},{4,0},{5,1},{6,2},{7,3},{8,12},{9,13},{10,... | collective-permute-start | bytes 2359304 | tf_op jit(solution)/shard_map/ppermute | solution.py:20
  21.7 10.7 %collective-permute-start.6 = (bf16[3,2,256,256]{3,2,1,0:T(8,128)(2,1)}, bf16[3,2,256,256]{3,2,1,0:T(8,128)(2,1)}, u32[]{:S(2)}, u32[]{:S(2)}) collective-permute-start(bf16[3,2,256,256]{3,2,1,0:T(8,128)(2,1)} %collective-permute-done.5.refs_3_), channel_id=1, source_target_pairs={{0,4},{1,5},{2,6},{3,7},{4,0},{5,1},{6,2},{7,3},{8,12},{9,13},{10,... | collective-permute-start | bytes 2359304 | tf_op jit(solution)/shard_map/ppermute | solution.py:20
  24.6 3.9 %copy-start.1 = (bf16[3,2,256,256]{3,2,1,0:T(8,128)(2,1)S(1)}, bf16[3,2,256,256]{3,2,1,0:T(8,128)(2,1)}, u32[]{:S(2)}) copy-start(bf16[3,2,256,256]{3,2,1,0:T(8,128)(2,1)} %old.1) | copy-start | bytes 2359300
  28.6 3.8 %copy-start = (bf16[3,3,256,256]{3,2,1,0:T(8,128)(2,1)S(1)}, bf16[3,3,256,256]{3,2,1,0:T(8,128)(2,1)}, u32[]{:S(2)}) copy-start(bf16[3,3,256,256]{3,2,1,0:T(8,128)(2,1)} %new.3) | copy-start | bytes 3538948
  28.6 3.8 %copy-start.3 = (bf16[2,512,512]{2,1,0:T(8,128)(2,1)S(1)}, bf16[2,512,512]{2,1,0:T(8,128)(2,1)}, u32[]{:S(2)}) copy-start(bf16[2,512,512]{2,1,0:T(8,128)(2,1)} %get-tuple-element.15.refs_0_) | copy-start | bytes 3145732
  37.0 34.7 %copy-start.2 = (f32[3,256,256]{2,1,0:T(8,128)S(1)}, f32[3,256,256]{2,1,0:T(8,128)}, u32[]{:S(2)}) copy-start(f32[3,256,256]{2,1,0:T(8,128)} %diag.1) | copy-start | bytes 2359300
  37.0 3.0 %collective-permute-start.9 = (bf16[768,256]{1,0:T(8,128)(2,1)S(1)}, bf16[768,256]{1,0:T(8,128)(2,1)S(1)}, u32[]{:S(2)}, u32[]{:S(2)}) collective-permute-start(bf16[768,256]{1,0:T(8,128)(2,1)S(1)} %get-tuple-element.21), channel_id=1, source_target_pairs={{0,4},{1,5},{2,6},{3,7},{4,0},{5,1},{6,2},{7,3},{8,12},{9,13},{10,... | collective-permute-start | bytes 1179656 | tf_op jit(solution)/shard_map/ppermute | solution.py:20
  37.4 18.2 %collective-permute-start.7 = (bf16[2,3,2,64,256]{4,3,2,1,0:T(8,128)(2,1)S(1)}, bf16[2,3,2,64,256]{4,3,2,1,0:T(8,128)(2,1)S(1)}, u32[]{:S(2)}, u32[]{:S(2)}) collective-permute-start(bf16[2,3,2,64,256]{4,3,2,1,0:T(8,128)(2,1)S(1)} %get-tuple-element.17), channel_id=1, source_target_pairs={{0,1},{1,0},{2,3},{3,2},{4,6},{5,7},{6,4},{7,5},{8,9},{9,8},{10,11... | collective-permute-start | bytes 1179656 | tf_op jit(solution)/shard_map/ppermute | solution.py:20
  40.6 6.2 %collective-permute-start.10 = (bf16[192,256]{1,0:T(8,128)(2,1)S(1)}, bf16[192,256]{1,0:T(8,128)(2,1)S(1)}, u32[]{:S(2)}, u32[]{:S(2)}) collective-permute-start(bf16[192,256]{1,0:T(8,128)(2,1)S(1)} %get-tuple-element.23), channel_id=1, source_target_pairs={{0,8},{1,9},{2,10},{3,11},{4,12},{5,13},{6,14},{7,15},{8,0},{9,1},... | collective-permute-start | bytes 294920 | tf_op jit(solution)/shard_map/ppermute | solution.py:20
  43.6 7.5 %collective-permute-start.11 = (bf16[192,256]{1,0:T(8,128)(2,1)S(1)}, bf16[192,256]{1,0:T(8,128)(2,1)S(1)}, u32[]{:S(2)}, u32[]{:S(2)}) collective-permute-start(bf16[192,256]{1,0:T(8,128)(2,1)S(1)} %get-tuple-element.24), channel_id=1, source_target_pairs={{0,16},{1,17},{2,18},{3,19},{4,20},{5,21},{6,22},{7,23},{8,24},{9,... | collective-permute-start | bytes 294920 | tf_op jit(solution)/shard_map/ppermute | solution.py:20
  44.6 6.5 %collective-permute-start.12 = (bf16[192,256]{1,0:T(8,128)(2,1)S(1)}, bf16[192,256]{1,0:T(8,128)(2,1)S(1)}, u32[]{:S(2)}, u32[]{:S(2)}) collective-permute-start(bf16[192,256]{1,0:T(8,128)(2,1)S(1)} %get-tuple-element.25), channel_id=1, source_target_pairs={{0,24},{1,25},{2,26},{3,27},{4,28},{5,29},{6,30},{7,31},{8,16},{9,... | collective-permute-start | bytes 294920 | tf_op jit(solution)/shard_map/ppermute | solution.py:20
  51.2 6.2 %collective-permute-start.13 = (bf16[192,256]{1,0:T(8,128)(2,1)S(1)}, bf16[192,256]{1,0:T(8,128)(2,1)S(1)}, u32[]{:S(2)}, u32[]{:S(2)}) collective-permute-start(bf16[192,256]{1,0:T(8,128)(2,1)S(1)} %shard_map.101.refs_0_), channel_id=1, source_target_pairs={{0,1},{1,0},{2,3},{3,2},{4,5},{5,4},{6,7},{7,6},{8,9},{9,8},{10,11... | collective-permute-start | bytes 294920 | tf_op jit(solution)/shard_map/ppermute | solution.py:20
  51.9 9.8 %collective-permute-start.14 = (bf16[192,256]{1,0:T(8,128)(2,1)S(1)}, bf16[192,256]{1,0:T(8,128)(2,1)S(1)}, u32[]{:S(2)}, u32[]{:S(2)}) collective-permute-start(bf16[192,256]{1,0:T(8,128)(2,1)S(1)} %shard_map.101.refs_0_), channel_id=1, source_target_pairs={{0,2},{1,3},{2,0},{3,1},{4,6},{5,7},{6,4},{7,5},{8,10},{9,11},{10,... | collective-permute-start | bytes 294920 | tf_op jit(solution)/shard_map/ppermute | solution.py:20
  53.4 9.1 %collective-permute-start.15 = (bf16[192,256]{1,0:T(8,128)(2,1)S(1)}, bf16[192,256]{1,0:T(8,128)(2,1)S(1)}, u32[]{:S(2)}, u32[]{:S(2)}) collective-permute-start(bf16[192,256]{1,0:T(8,128)(2,1)S(1)} %shard_map.101.refs_0_), channel_id=1, source_target_pairs={{0,3},{1,2},{2,1},{3,0},{4,7},{5,6},{6,5},{7,4},{8,11},{9,10},{10,... | collective-permute-start | bytes 294920 | tf_op jit(solution)/shard_map/ppermute | solution.py:20
  56.2 14.2 %collective-permute-start.8 = (bf16[1,3,2,64,256]{4,3,2,1,0:T(8,128)(2,1)S(1)}, bf16[1,3,2,64,256]{4,3,2,1,0:T(8,128)(2,1)S(1)}, u32[]{:S(2)}, u32[]{:S(2)}) collective-permute-start(bf16[1,3,2,64,256]{4,3,2,1,0:T(8,128)(2,1)S(1)} %get-tuple-element.19), channel_id=1, source_target_pairs={{0,2},{1,3},{2,0},{3,1},{4,5},{5,4},{6,7},{7,6},{8,10},{9,11},{10,... | collective-permute-start | bytes 589832 | tf_op jit(solution)/shard_map/ppermute | solution.py:20
  62.5 4.7 %collective-permute-start.16 = (bf16[192,256]{1,0:T(8,128)(2,1)S(1)}, bf16[192,256]{1,0:T(8,128)(2,1)S(1)}, u32[]{:S(2)}, u32[]{:S(2)}) collective-permute-start(bf16[192,256]{1,0:T(8,128)(2,1)S(1)} %shard_map.102.refs_0_), channel_id=1, source_target_pairs={{0,8},{1,9},{2,10},{3,11},{4,12},{5,13},{6,14},{7,15},{8,0},{9,1},... | collective-permute-start | bytes 294920 | tf_op jit(solution)/shard_map/ppermute | solution.py:20
  64.3 4.6 %collective-permute-start.17 = (bf16[192,256]{1,0:T(8,128)(2,1)S(1)}, bf16[192,256]{1,0:T(8,128)(2,1)S(1)}, u32[]{:S(2)}, u32[]{:S(2)}) collective-permute-start(bf16[192,256]{1,0:T(8,128)(2,1)S(1)} %shard_map.102.refs_0_), channel_id=1, source_target_pairs={{0,16},{1,17},{2,18},{3,19},{4,20},{5,21},{6,22},{7,23},{8,24},{9,... | collective-permute-start | bytes 294920 | tf_op jit(solution)/shard_map/ppermute | solution.py:20
  64.9 5.5 %collective-permute-start.18 = (bf16[192,256]{1,0:T(8,128)(2,1)S(1)}, bf16[192,256]{1,0:T(8,128)(2,1)S(1)}, u32[]{:S(2)}, u32[]{:S(2)}) collective-permute-start(bf16[192,256]{1,0:T(8,128)(2,1)S(1)} %shard_map.102.refs_0_), channel_id=1, source_target_pairs={{0,24},{1,25},{2,26},{3,27},{4,28},{5,29},{6,30},{7,31},{8,16},{9,... | collective-permute-start | bytes 294920 | tf_op jit(solution)/shard_map/ppermute | solution.py:20
  66.1 5.1 %collective-permute-start.19 = (bf16[192,256]{1,0:T(8,128)(2,1)S(1)}, bf16[192,256]{1,0:T(8,128)(2,1)S(1)}, u32[]{:S(2)}, u32[]{:S(2)}) collective-permute-start(bf16[192,256]{1,0:T(8,128)(2,1)S(1)} %shard_map.102.refs_0_), channel_id=1, source_target_pairs={{0,4},{1,5},{2,6},{3,7},{4,0},{5,1},{6,2},{7,3},{8,12},{9,13},{10,... | collective-permute-start | bytes 294920 | tf_op jit(solution)/shard_map/ppermute | solution.py:20
  67.2 3.9 %collective-permute-start.20 = (bf16[192,256]{1,0:T(8,128)(2,1)S(1)}, bf16[192,256]{1,0:T(8,128)(2,1)S(1)}, u32[]{:S(2)}, u32[]{:S(2)}) collective-permute-start(bf16[192,256]{1,0:T(8,128)(2,1)S(1)} %collective-permute-done.16.refs_1_), channel_id=1, source_target_pairs={{0,4},{1,5},{2,6},{3,7},{4,0},{5,1},{6,2},{7,3},{8,12},{9,13},{10,... | collective-permute-start | bytes 294920 | tf_op jit(solution)/shard_map/ppermute | solution.py:20
  68.9 2.3 %collective-permute-start.21 = (bf16[192,256]{1,0:T(8,128)(2,1)S(1)}, bf16[192,256]{1,0:T(8,128)(2,1)S(1)}, u32[]{:S(2)}, u32[]{:S(2)}) collective-permute-start(bf16[192,256]{1,0:T(8,128)(2,1)S(1)} %collective-permute-done.17.refs_2_), channel_id=1, source_target_pairs={{0,4},{1,5},{2,6},{3,7},{4,0},{5,1},{6,2},{7,3},{8,12},{9,13},{10,... | collective-permute-start | bytes 294920 | tf_op jit(solution)/shard_map/ppermute | solution.py:20
  70.4 1.3 %collective-permute-start.22 = (bf16[192,256]{1,0:T(8,128)(2,1)S(1)}, bf16[192,256]{1,0:T(8,128)(2,1)S(1)}, u32[]{:S(2)}, u32[]{:S(2)}) collective-permute-start(bf16[192,256]{1,0:T(8,128)(2,1)S(1)} %collective-permute-done.18.refs_3_), channel_id=1, source_target_pairs={{0,4},{1,5},{2,6},{3,7},{4,0},{5,1},{6,2},{7,3},{8,12},{9,13},{10,... | collective-permute-start | bytes 294920 | tf_op jit(solution)/shard_map/ppermute | solution.py:20
where the time goes:
time: 75.2 us; the launch traced here: 74.2 us
  waiting for transfers between devices  29.8 us (40%)
  starting transfers between devices  26 us (35%)
  Pallas kernels  16.8 us (22%)
  between operations  1.43 us (2%)
    ppermute x23, waiting for transfers between devices, permute(): return lax.ppermute(value, ('row', 'col'), pairs)  29.8 us
    ppermute x23, starting transfers between devices, permute(): return lax.ppermute(value, ('row', 'col'), pairs)  26 us
    pallas_call x1, Pallas kernels, per_device(): call(functools.partial(main_kernel, n_high, n_col), (jax.ShapeDtypeStruct...  4.6 us
    pallas_call x1, Pallas kernels, per_device(): call(functools.partial(gather_kernel, n_high, slots), (pltpu.MemorySpace....  3.89 us
    pallas_call x1, Pallas kernels, per_device(): call(own_kernel, jax.ShapeDtypeStruct(p_shape, F32), [SMEM, ANY] + [ANY]...  3.76 us
    pallas_call x1, Pallas kernels, per_device(): call(final_kernel, pltpu.MemorySpace.HBM((t_count, t_count, width, width)...  2.48 us
  transfers between devices with their start and end apart: 23, of which 9 were waited for; matrix products, arithmetic and copies ran while one was open for 0% of the time, Pallas kernels for 13%

commit v1 on v0

--- a/solution.py
+++ b/solution.py
@@ -119,56 +119,57 @@
     return wait
 
 
-def own_kernel(where, w_in, *refs):
-    options, (p_out, w, lo, w_sem, sems) = refs[:-5], refs[-5:]
+def stacked_dot(w, panel):
+    both = jnp.dot(w.reshape(-1, w.shape[-1]), panel, preferred_element_type=F32)
+    return both[: w.shape[1]] + both[w.shape[1] :]
+
+
+def own_kernel(where, w_in, old, *refs):
+    options, (p_out, old_out, w, lo, w_sem, sems) = refs[:-6], refs[-6:]
     w_copy = pltpu.make_async_copy(w_in, w, w_sem)
     w_copy.start()
     wait = fill(where, options, lo, sems)
+    for t in range(lo.shape[0]):
+        old_out[t] = old[t].reshape(lo.shape[1:]).T
     w_copy.wait()
     for t in range(lo.shape[0]):
         wait(t)
-        lo_t = lo[t]
-        running = jnp.dot(w[0], lo_t, preferred_element_type=F32)
-        p_out[t] = running + jnp.dot(w[1], lo_t, preferred_element_type=F32)
+        p_out[t] = stacked_dot(w[...], lo[t])
 
 
 def piece_index(core, value, j, count):
     return jnp.where(core == 0, 2 * j + value, value * count + j)
 
 
-def main_kernel(n_high, n_col, where, p_own, old, new, *refs):
+def main_kernel(n_high, n_col, where, p_own, old_t, new, *refs):
     t_count = new.shape[0]
-    slots = old.shape[1]
+    width = new.shape[-1]
+    slots = old_t.shape[-1] // width
     n_far = n_high - 1
     w_ins, parts = refs[:n_far], refs[n_far:-8]
     u_keep, u_send, g_keep, g_send, lo, u_all, g_all, sems = refs[-8:]
-    width = new.shape[-1]
-    part_rows = slots * width
     cases = len(parts) // max(n_far, 1)
     waits = [
         fill(where, parts[g * cases : (g + 1) * cases], lo.at[g], sems.at[g]) for g in range(n_far)
     ]
-    panels = []
-    index = 0
     for t in range(t_count):
-        running = p_own[t]
-        for g in range(n_high - 1):
-            waits[g](t)
-            lo_t = lo[g, t]
-            running += jnp.dot(w_ins[g][0], lo_t, preferred_element_type=F32)
-            running += jnp.dot(w_ins[g][1], lo_t, preferred_element_type=F32)
-        for s in range(t):
-            running += jnp.dot(panels[s], new[t, s], preferred_element_type=F32)
-        current = -running
-        u_all[t] = current
-        panels.append(current.astype(BF16))
-        own = old[t].reshape(part_rows, width)
-        for s in range(t + 1):
-            left, right = (own, panels[t]) if s == t else (panels[s], own)
-            g_all[pl.ds(index * width, width), :] = lax.dot_general(
-                left, right, (((0,), (0,)), ((), ())), preferred_element_type=F32
-            )
-            index += 1
+        for wait in waits:
+            wait(t)
+    totals = [
+        p_own[t] + sum(stacked_dot(w_ins[g][...], lo[g, t]) for g in range(n_far))
+        for t in range(t_count)
+    ]
+    for s in range(t_count):
+        u_all[s] = -totals[s]
+        panel = (-totals[s]).astype(BF16)
+        for t in range(s + 1, t_count):
+            totals[t] += jnp.dot(panel, new[t, s], preferred_element_type=F32)
+        rest = old_t[s:].reshape(-1, old_t.shape[-1])
+        crossed = jnp.dot(rest, panel, preferred_element_type=F32)
+        for t in range(s, t_count):
+            g_all[pl.ds((t * (t + 1) // 2 + s) * width, width), :] = crossed[
+                (t - s) * width : (t - s + 1) * width
+            ]
     half = g_keep.shape[0]
     g_keep[...] = g_all[pl.ds(pl.multiple_of(where[1] * half, 16), half), :]
     g_send[...] = g_all[pl.ds(pl.multiple_of((1 - where[1]) * half, 16), half), :].astype(BF16)
@@ -213,18 +214,23 @@
 
 
 def wide_dot(left, right, dims):
-    dims = (dims, ((), ()))
+    wide = left if left.dtype == F32 else right
+    high = wide.astype(BF16)
+    low = (wide - high.astype(F32)).astype(BF16)
     if left.dtype == F32:
-        high = left.astype(BF16)
-        low = (left - high.astype(F32)).astype(BF16)
-        return lax.dot_general(high, right, dims, preferred_element_type=F32) + lax.dot_general(
-            low, right, dims, preferred_element_type=F32
+        axis = 1 - dims[0][0]
+        both = lax.dot_general(
+            jnp.concatenate([high, low], axis),
+            right,
+            (dims, ((), ())),
+            preferred_element_type=F32,
         )
-    high = right.astype(BF16)
-    low = (right - high.astype(F32)).astype(BF16)
-    return lax.dot_general(left, high, dims, preferred_element_type=F32) + lax.dot_general(
-        left, low, dims, preferred_element_type=F32
-    )
+        return both[: left.shape[axis]] + both[left.shape[axis] :]
+    parts = [
+        lax.dot_general(left, part, (dims, ((), ())), preferred_element_type=F32)
+        for part in (high, low)
+    ]
+    return parts[0] + parts[1]
 
 
 def final_kernel(where, new, diag, *refs):
@@ -240,7 +246,8 @@
 
     def g(t, s):
         index = t * (t + 1) // 2 + s
-        return g_all[pl.ds(index * width, width), :].astype(F32)
+        value = g_all[pl.ds(index * width, width), :]
+        return (value if s == t else value.T).astype(F32)
 
     def give(source, t, s):
         copy = pltpu.make_async_copy(source, out.at[t, s], sems.at[t, s])
@@ -406,10 +413,13 @@
         ],
     )
     p_shape = (t_count, slots * width, width)
-    p_own = call(
+    p_own, old_t = call(
         own_kernel,
-        jax.ShapeDtypeStruct(p_shape, F32),
-        [SMEM, ANY] + [ANY] * len(own_parts),
+        (
+            jax.ShapeDtypeStruct(p_shape, F32),
+            jax.ShapeDtypeStruct((t_count, width, slots * width), BF16),
+        ),
+        [SMEM, ANY, VMEM] + [ANY] * len(own_parts),
         [
             pltpu.VMEM(w_shape, BF16),
             pltpu.VMEM(p_shape, BF16),
@@ -422,6 +432,7 @@
     )(
         where,
         pltpu.with_memory_space_constraint(ws[0], pltpu.MemorySpace.HBM),
+        lower_old,
         *own_parts,
     )
 
@@ -448,7 +459,7 @@
         flops=2 * block * width * slots * t_count * (2 * n_cand + 4),
         moved=4 * block * t_count * n_cand,
         limit=12 + 2 * n_high,
-    )(where, p_own, lower_old, lower_new, *ws[1:], *far_parts)
+    )(where, p_own, old_t, lower_new, *ws[1:], *far_parts)
 
     def step(index):
         return pairs(

time: 75.2 us -> 74.2 us (0.987)
  Pallas kernels: 16.8 us -> 15.8 us
    pallas_call x1, Pallas kernels: 4.6 us -> 3.66 us  [per_device(): call(functools.partial(main_kernel, n_high, n_col), (jax.ShapeDtypeStruct...]
where the time goes in v1:
time: 74.2 us; the launch traced here: 73.2 us
  waiting for transfers between devices  29.8 us (40%)
  starting transfers between devices  26 us (35%)
  Pallas kernels  15.8 us (21%)
  between operations  1.43 us (2%)
    ppermute x23, waiting for transfers between devices, permute(): return lax.ppermute(value, ('row', 'col'), pairs)  29.8 us
    ppermute x23, starting transfers between devices, permute(): return lax.ppermute(value, ('row', 'col'), pairs)  26 us
    pallas_call x1, Pallas kernels, per_device(): call(functools.partial(gather_kernel, n_high, slots), (pltpu.MemorySpace....  3.88 us
    pallas_call x1, Pallas kernels, per_device(): call(own_kernel, (jax.ShapeDtypeStruct(p_shape, F32), jax.ShapeDtypeStruc...  3.76 us
    pallas_call x1, Pallas kernels, per_device(): call(functools.partial(main_kernel, n_high, n_col), (jax.ShapeDtypeStruct...  3.66 us
    pallas_call x1, Pallas kernels, per_device(): call(final_kernel, pltpu.MemorySpace.HBM((t_count, t_count, width, width)...  2.46 us
  transfers between devices with their start and end apart: 23, of which 9 were waited for; matrix products, arithmetic and copies ran while one was open for 0% of the time, Pallas kernels for 13%

profile of v1, /device:TPU:0, one launch (start us, length us, event | category | flops | bytes accessed | tf_op | source)
XLA Modules:
  0.0 73.2 jit_solution(15011653540361624696)
XLA Ops:
  0.6 0.6 collective-permute-start
  1.2 4.4 %collective-permute-start.1 = (bf16[3,2,256,256]{3,2,1,0:T(8,128)(2,1)}, bf16[3,2,256,256]{3,2,1,0:T(8,128)(2,1)S(1)}, u32[]{:S(2)}, u32[]{:S(2)}) collective-permute-start(bf16[3,2,256,256]{3,2,1,0:T(8,128)(2,1)} %refs_0_.1), channel_id=1, source_target_pairs={{0,8},{5,13},{10,2},{15,7},{16,24},{21,29},{26,18},{31,23},{4,0},{... | collective-permute-start | bytes 2359304 | tf_op jit(solution)/shard_map/ppermute | solution.py:20
  5.6 0.2 collective-permute-start.3
  5.8 0.0 collective-permute-done.refs_1_
  5.8 1.5 %collective-permute-start.5 = (bf16[3,2,256,256]{3,2,1,0:T(8,128)(2,1)S(1)}, bf16[3,2,256,256]{3,2,1,0:T(8,128)(2,1)}, u32[]{:S(2)}, u32[]{:S(2)}) collective-permute-start(bf16[3,2,256,256]{3,2,1,0:T(8,128)(2,1)S(1)} %collective-permute-done.refs_1_), channel_id=1, source_target_pairs={{4,24},{1,29},{14,18},{11,23},{20,8},{17,13},{30,2},{27,7},{0,0},{... | collective-permute-start | bytes 2359304 | tf_op jit(solution)/shard_map/ppermute | solution.py:20
  7.4 13.8 %collective-permute-done.1.refs_2_ = bf16[3,2,256,256]{3,2,1,0:T(8,128)(2,1)S(1)} collective-permute-done((bf16[3,2,256,256]{3,2,1,0:T(8,128)(2,1)}, bf16[3,2,256,256]{3,2,1,0:T(8,128)(2,1)S(1)}, u32[]{:S(2)}, u32[]{:S(2)}) %collective-permute-start.1) | collective-permute-done | bytes 786464 | tf_op jit(solution)/shard_map/ppermute | solution.py:20
  21.2 0.0 collective-permute-start.2
  21.2 0.0 collective-permute-done.3.refs_2_
  21.2 0.5 collective-permute-start.4
  21.7 0.0 collective-permute-done.5.refs_3_
  21.7 2.1 %collective-permute-start.6 = (bf16[3,2,256,256]{3,2,1,0:T(8,128)(2,1)}, bf16[3,2,256,256]{3,2,1,0:T(8,128)(2,1)}, u32[]{:S(2)}, u32[]{:S(2)}) collective-permute-start(bf16[3,2,256,256]{3,2,1,0:T(8,128)(2,1)} %collective-permute-done.5.refs_3_), channel_id=1, source_target_pairs={{0,4},{1,5},{2,6},{3,7},{4,0},{5,1},{6,2},{7,3},{8,12},{9,13},{10,... | collective-permute-start | bytes 2359304 | tf_op jit(solution)/shard_map/ppermute | solution.py:20
  24.5 0.1 stack.39.where
  24.6 0.1 pad_add_fusion.me
  24.6 0.0 copy-start
  24.7 3.9 %shard_map.95 = (bf16[2,512,512]{2,1,0:T(8,128)(2,1)}, bf16[2,512,512]{2,1,0:T(8,128)(2,1)}) custom-call(s32[3]{0:T(128)S(1)} %pad_add_fusion.me, s32[1,1]{1,0:T(1,128)S(6)} %copy.10.count, s32[1,96]{1,0:T(1,128)} %rows_in.1, s32[1,96]{1,0:T(1,128)} %cols_in.1, s32[16]{0:T(128)} %panel_in.1, bf16[96,256,256]{2,1,0:T(8,128)(2,1)} %bitcast.15), custom_call_target="tpu_custom_call" | custom-call | flops 1048576 | bytes 10485760 | tf_op jit(solution)/shard_map/pallas_call | solution.py:387
  28.5 0.0 collective-permute-done.2.refs_3_
  28.6 0.0 copy-done
  28.6 0.0 copy-start.1
  28.6 0.0 copy-start.3
  28.6 3.8 %shard_map.96 = (f32[3,512,256]{2,1,0:T(8,128)S(1)}, bf16[3,256,512]{2,1,0:T(8,128)(2,1)S(1)}) custom-call(s32[6]{0:T(128)S(1)} %stack.39.where, bf16[2,512,512]{2,1,0:T(8,128)(2,1)} %get-tuple-element.16.w_in, bf16[3,2,256,256]{3,2,1,0:T(8,128)(2,1)S(1)} %copy-done, bf16[3,2,256,256]{3,2,1,0:T(8,128)(2,1)S(1)} %copy-done, ...), custom_call_target="tpu_custom_call" | custom-call | flops 805306368 | bytes 3145728 | tf_op jit(solution)/shard_map/pallas_call | solution.py:416
  32.3 0.0 collective-permute-done.4.refs_1_
  32.4 0.0 collective-permute-done.6.refs_4_
  32.4 0.0 copy-done.1
  32.4 0.0 copy-done.3
  32.4 3.7 %shard_map.97 = (f32[2,3,2,64,256]{4,3,2,1,0:T(8,128)S(1)}, bf16[2,3,2,64,256]{4,3,2,1,0:T(8,128)(2,1)S(1)}, f32[768,256]{1,0:T(8,128)S(1)}, bf16[768,256]{1,0:T(8,128)(2,1)S(1)}) custom-call(s32[6]{0:T(128)S(1)} %stack.39.where, f32[3,512,256]{2,1,0:T(8,128)S(1)} %get-tuple-element.17.p_own, bf16[3,256,512]{2,1,0:T(8,128)(2,1)S(1)} %get-tuple-element.18.old_t, ...), custom_call_target="tpu_custom_call" | custom-call | flops 2415919104 | bytes 3145728 | tf_op jit(solution)/shard_map/pallas_call | solution.py:444
  36.1 0.0 copy-start.2
  36.1 0.2 collective-permute-start.9
  36.2 2.8 %collective-permute-start.7 = (bf16[2,3,2,64,256]{4,3,2,1,0:T(8,128)(2,1)S(1)}, bf16[2,3,2,64,256]{4,3,2,1,0:T(8,128)(2,1)S(1)}, u32[]{:S(2)}, u32[]{:S(2)}) collective-permute-start(bf16[2,3,2,64,256]{4,3,2,1,0:T(8,128)(2,1)S(1)} %get-tuple-element.21), channel_id=1, source_target_pairs={{0,1},{1,0},{2,3},{3,2},{4,6},{5,7},{6,4},{7,5},{8,9},{9,8},{10,11... | collective-permute-start | bytes 1179656 | tf_op jit(solution)/shard_map/ppermute | solution.py:20
  39.0 0.0 collective-permute-done.9
  39.0 0.6 shard_map.100
  39.6 3.0 %collective-permute-start.10 = (bf16[192,256]{1,0:T(8,128)(2,1)S(1)}, bf16[192,256]{1,0:T(8,128)(2,1)S(1)}, u32[]{:S(2)}, u32[]{:S(2)}) collective-permute-start(bf16[192,256]{1,0:T(8,128)(2,1)S(1)} %get-tuple-element.27), channel_id=1, source_target_pairs={{0,8},{1,9},{2,10},{3,11},{4,12},{5,13},{6,14},{7,15},{8,0},{9,1},... | collective-permute-start | bytes 294920 | tf_op jit(solution)/shard_map/ppermute | solution.py:20
  42.6 1.0 %collective-permute-start.11 = (bf16[192,256]{1,0:T(8,128)(2,1)S(1)}, bf16[192,256]{1,0:T(8,128)(2,1)S(1)}, u32[]{:S(2)}, u32[]{:S(2)}) collective-permute-start(bf16[192,256]{1,0:T(8,128)(2,1)S(1)} %get-tuple-element.28), channel_id=1, source_target_pairs={{0,16},{1,17},{2,18},{3,19},{4,20},{5,21},{6,22},{7,23},{8,24},{9,... | collective-permute-start | bytes 294920 | tf_op jit(solution)/shard_map/ppermute | solution.py:20
  43.7 0.5 collective-permute-start.12
  44.2 1.6 %collective-permute-done.10.refs_1_ = bf16[192,256]{1,0:T(8,128)(2,1)S(1)} collective-permute-done((bf16[192,256]{1,0:T(8,128)(2,1)S(1)}, bf16[192,256]{1,0:T(8,128)(2,1)S(1)}, u32[]{:S(2)}, u32[]{:S(2)}) %collective-permute-start.10) | collective-permute-done | bytes 98336 | tf_op jit(solution)/shard_map/ppermute | solution.py:20
  45.8 4.4 %collective-permute-done.11.refs_2_ = bf16[192,256]{1,0:T(8,128)(2,1)S(1)} collective-permute-done((bf16[192,256]{1,0:T(8,128)(2,1)S(1)}, bf16[192,256]{1,0:T(8,128)(2,1)S(1)}, u32[]{:S(2)}, u32[]{:S(2)}) %collective-permute-start.11) | collective-permute-done | bytes 98336 | tf_op jit(solution)/shard_map/ppermute | solution.py:20
  50.2 0.0 collective-permute-done.12.refs_3_
  50.2 0.7 collective-permute-start.13
  50.9 1.5 %collective-permute-start.14 = (bf16[192,256]{1,0:T(8,128)(2,1)S(1)}, bf16[192,256]{1,0:T(8,128)(2,1)S(1)}, u32[]{:S(2)}, u32[]{:S(2)}) collective-permute-start(bf16[192,256]{1,0:T(8,128)(2,1)S(1)} %shard_map.101.refs_0_), channel_id=1, source_target_pairs={{0,2},{1,3},{2,0},{3,1},{4,6},{5,7},{6,4},{7,5},{8,10},{9,11},{10,... | collective-permute-start | bytes 294920 | tf_op jit(solution)/shard_map/ppermute | solution.py:20
  52.4 2.2 %collective-permute-start.15 = (bf16[192,256]{1,0:T(8,128)(2,1)S(1)}, bf16[192,256]{1,0:T(8,128)(2,1)S(1)}, u32[]{:S(2)}, u32[]{:S(2)}) collective-permute-start(bf16[192,256]{1,0:T(8,128)(2,1)S(1)} %shard_map.101.refs_0_), channel_id=1, source_target_pairs={{0,3},{1,2},{2,1},{3,0},{4,7},{5,6},{6,5},{7,4},{8,11},{9,10},{10,... | collective-permute-start | bytes 294920 | tf_op jit(solution)/shard_map/ppermute | solution.py:20
  54.7 0.0 collective-permute-done.7.received
  54.7 0.6 shard_map.98
  55.3 1.1 %collective-permute-start.8 = (bf16[1,3,2,64,256]{4,3,2,1,0:T(8,128)(2,1)S(1)}, bf16[1,3,2,64,256]{4,3,2,1,0:T(8,128)(2,1)S(1)}, u32[]{:S(2)}, u32[]{:S(2)}) collective-permute-start(bf16[1,3,2,64,256]{4,3,2,1,0:T(8,128)(2,1)S(1)} %get-tuple-element.23), channel_id=1, source_target_pairs={{0,2},{1,3},{2,0},{3,1},{4,5},{5,4},{6,7},{7,6},{8,10},{9,11},{10,... | collective-permute-start | bytes 589832 | tf_op jit(solution)/shard_map/ppermute | solution.py:20
  56.4 0.0 collective-permute-done.13.refs_1_
  56.4 4.4 %collective-permute-done.14.refs_2_ = bf16[192,256]{1,0:T(8,128)(2,1)S(1)} collective-permute-done((bf16[192,256]{1,0:T(8,128)(2,1)S(1)}, bf16[192,256]{1,0:T(8,128)(2,1)S(1)}, u32[]{:S(2)}, u32[]{:S(2)}) %collective-permute-start.14) | collective-permute-done | bytes 98336 | tf_op jit(solution)/shard_map/ppermute | solution.py:20
  60.7 0.8 %collective-permute-done.15.refs_3_ = bf16[192,256]{1,0:T(8,128)(2,1)S(1)} collective-permute-done((bf16[192,256]{1,0:T(8,128)(2,1)S(1)}, bf16[192,256]{1,0:T(8,128)(2,1)S(1)}, u32[]{:S(2)}, u32[]{:S(2)}) %collective-permute-start.15) | collective-permute-done | bytes 98336 | tf_op jit(solution)/shard_map/ppermute | solution.py:20
  61.5 0.1 shard_map.102.refs_0_
  61.6 1.7 %collective-permute-start.16 = (bf16[192,256]{1,0:T(8,128)(2,1)S(1)}, bf16[192,256]{1,0:T(8,128)(2,1)S(1)}, u32[]{:S(2)}, u32[]{:S(2)}) collective-permute-start(bf16[192,256]{1,0:T(8,128)(2,1)S(1)} %shard_map.102.refs_0_), channel_id=1, source_target_pairs={{0,8},{1,9},{2,10},{3,11},{4,12},{5,13},{6,14},{7,15},{8,0},{9,1},... | collective-permute-start | bytes 294920 | tf_op jit(solution)/shard_map/ppermute | solution.py:20
  63.3 0.6 collective-permute-start.17
  63.9 1.2 %collective-permute-start.18 = (bf16[192,256]{1,0:T(8,128)(2,1)S(1)}, bf16[192,256]{1,0:T(8,128)(2,1)S(1)}, u32[]{:S(2)}, u32[]{:S(2)}) collective-permute-start(bf16[192,256]{1,0:T(8,128)(2,1)S(1)} %shard_map.102.refs_0_), channel_id=1, source_target_pairs={{0,24},{1,25},{2,26},{3,27},{4,28},{5,29},{6,30},{7,31},{8,16},{9,... | collective-permute-start | bytes 294920 | tf_op jit(solution)/shard_map/ppermute | solution.py:20
  65.1 0.0 collective-permute-start.19
  65.1 1.1 %collective-permute-done.16.refs_1_ = bf16[192,256]{1,0:T(8,128)(2,1)S(1)} collective-permute-done((bf16[192,256]{1,0:T(8,128)(2,1)S(1)}, bf16[192,256]{1,0:T(8,128)(2,1)S(1)}, u32[]{:S(2)}, u32[]{:S(2)}) %collective-permute-start.16) | collective-permute-done | bytes 98336 | tf_op jit(solution)/shard_map/ppermute | solution.py:20
  66.3 0.0 collective-permute-start.20
  66.3 1.7 %collective-permute-done.17.refs_2_ = bf16[192,256]{1,0:T(8,128)(2,1)S(1)} collective-permute-done((bf16[192,256]{1,0:T(8,128)(2,1)S(1)}, bf16[192,256]{1,0:T(8,128)(2,1)S(1)}, u32[]{:S(2)}, u32[]{:S(2)}) %collective-permute-start.17) | collective-permute-done | bytes 98336 | tf_op jit(solution)/shard_map/ppermute | solution.py:20
  67.9 0.0 collective-permute-start.21
  67.9 1.5 %collective-permute-done.18.refs_3_ = bf16[192,256]{1,0:T(8,128)(2,1)S(1)} collective-permute-done((bf16[192,256]{1,0:T(8,128)(2,1)S(1)}, bf16[192,256]{1,0:T(8,128)(2,1)S(1)}, u32[]{:S(2)}, u32[]{:S(2)}) %collective-permute-start.18) | collective-permute-done | bytes 98336 | tf_op jit(solution)/shard_map/ppermute | solution.py:20
  69.5 0.0 collective-permute-start.22
  69.5 0.0 collective-permute-done.8.refs_1_
  69.5 0.7 shard_map.99
  70.2 0.0 collective-permute-done.19.refs_4_
  70.2 0.0 collective-permute-done.20.refs_5_
  70.2 0.0 collective-permute-done.21.refs_6_
  70.2 0.6 collective-permute-done.22.refs_7_
  70.8 0.0 copy-done.2
  70.8 2.5 %shard_map.103 = f32[3,3,256,256]{3,2,1,0:T(8,128)} custom-call(s32[6]{0:T(128)S(1)} %stack.39.where, bf16[3,3,256,256]{3,2,1,0:T(8,128)(2,1)S(1)} %copy-done.1, f32[3,256,256]{2,1,0:T(8,128)S(1)} %copy-done.2, bf16[192,256]{1,0:T(8,128)(2,1)S(1)} %shard_map.102.refs_0_, bf16[192,256]{1,0:T(8,128)(2,1)S(1)} %collective-permute-done.16.refs_1_, ...), custom_call_target="tpu_custom_call" | custom-call | flops 536870912 | bytes 3538944 | tf_op jit(solution)/shard_map/pallas_call | solution.py:515
  (1 shorter events, 0.0 us)
Async XLA Ops:
  0.6 5.2 %collective-permute-start = (bf16[3,2,256,256]{3,2,1,0:T(8,128)(2,1)}, bf16[3,2,256,256]{3,2,1,0:T(8,128)(2,1)S(1)}, u32[]{:S(2)}, u32[]{:S(2)}) collective-permute-start(bf16[3,2,256,256]{3,2,1,0:T(8,128)(2,1)} %refs_0_.1), channel_id=1, source_target_pairs={{0,4},{1,5},{2,6},{3,7},{4,0},{5,1},{6,2},{7,3},{8,12},{9,13},{10,... | collective-permute-start | bytes 2359304 | tf_op jit(solution)/shard_map/ppermute | solution.py:20
  1.2 20.0 %collective-permute-start.1 = (bf16[3,2,256,256]{3,2,1,0:T(8,128)(2,1)}, bf16[3,2,256,256]{3,2,1,0:T(8,128)(2,1)S(1)}, u32[]{:S(2)}, u32[]{:S(2)}) collective-permute-start(bf16[3,2,256,256]{3,2,1,0:T(8,128)(2,1)} %refs_0_.1), channel_id=1, source_target_pairs={{0,8},{5,13},{10,2},{15,7},{16,24},{21,29},{26,18},{31,23},{4,0},{... | collective-permute-start | bytes 2359304 | tf_op jit(solution)/shard_map/ppermute | solution.py:20
  5.6 15.6 %collective-permute-start.3 = (bf16[3,2,256,256]{3,2,1,0:T(8,128)(2,1)}, bf16[3,2,256,256]{3,2,1,0:T(8,128)(2,1)S(1)}, u32[]{:S(2)}, u32[]{:S(2)}) collective-permute-start(bf16[3,2,256,256]{3,2,1,0:T(8,128)(2,1)} %refs_0_.1), channel_id=1, source_target_pairs={{0,20},{5,17},{10,30},{15,27},{16,4},{21,1},{26,14},{31,11},{4,0},... | collective-permute-start | bytes 2359304 | tf_op jit(solution)/shard_map/ppermute | solution.py:20
  5.8 15.9 %collective-permute-start.5 = (bf16[3,2,256,256]{3,2,1,0:T(8,128)(2,1)S(1)}, bf16[3,2,256,256]{3,2,1,0:T(8,128)(2,1)}, u32[]{:S(2)}, u32[]{:S(2)}) collective-permute-start(bf16[3,2,256,256]{3,2,1,0:T(8,128)(2,1)S(1)} %collective-permute-done.refs_1_), channel_id=1, source_target_pairs={{4,24},{1,29},{14,18},{11,23},{20,8},{17,13},{30,2},{27,7},{0,0},{... | collective-permute-start | bytes 2359304 | tf_op jit(solution)/shard_map/ppermute | solution.py:20
  21.2 7.4 %collective-permute-start.2 = (bf16[3,2,256,256]{3,2,1,0:T(8,128)(2,1)S(1)}, bf16[3,2,256,256]{3,2,1,0:T(8,128)(2,1)S(1)}, u32[]{:S(2)}, u32[]{:S(2)}) collective-permute-start(bf16[3,2,256,256]{3,2,1,0:T(8,128)(2,1)S(1)} %collective-permute-done.1.refs_2_), channel_id=1, source_target_pairs={{0,4},{1,5},{2,6},{3,7},{4,0},{5,1},{6,2},{7,3},{8,12},{9,13},{10,... | collective-permute-start | bytes 2359304 | tf_op jit(solution)/shard_map/ppermute | solution.py:20
  21.2 11.2 %collective-permute-start.4 = (bf16[3,2,256,256]{3,2,1,0:T(8,128)(2,1)S(1)}, bf16[3,2,256,256]{3,2,1,0:T(8,128)(2,1)}, u32[]{:S(2)}, u32[]{:S(2)}) collective-permute-start(bf16[3,2,256,256]{3,2,1,0:T(8,128)(2,1)S(1)} %collective-permute-done.3.refs_2_), channel_id=1, source_target_pairs={{0,4},{1,5},{2,6},{3,7},{4,0},{5,1},{6,2},{7,3},{8,12},{9,13},{10,... | collective-permute-start | bytes 2359304 | tf_op jit(solution)/shard_map/ppermute | solution.py:20
  21.7 10.7 %collective-permute-start.6 = (bf16[3,2,256,256]{3,2,1,0:T(8,128)(2,1)}, bf16[3,2,256,256]{3,2,1,0:T(8,128)(2,1)}, u32[]{:S(2)}, u32[]{:S(2)}) collective-permute-start(bf16[3,2,256,256]{3,2,1,0:T(8,128)(2,1)} %collective-permute-done.5.refs_3_), channel_id=1, source_target_pairs={{0,4},{1,5},{2,6},{3,7},{4,0},{5,1},{6,2},{7,3},{8,12},{9,13},{10,... | collective-permute-start | bytes 2359304 | tf_op jit(solution)/shard_map/ppermute | solution.py:20
  24.6 3.9 %copy-start = (bf16[3,2,256,256]{3,2,1,0:T(8,128)(2,1)S(1)}, bf16[3,2,256,256]{3,2,1,0:T(8,128)(2,1)}, u32[]{:S(2)}) copy-start(bf16[3,2,256,256]{3,2,1,0:T(8,128)(2,1)} %refs_0_.1) | copy-start | bytes 2359300
  28.6 3.8 %copy-start.1 = (bf16[3,3,256,256]{3,2,1,0:T(8,128)(2,1)S(1)}, bf16[3,3,256,256]{3,2,1,0:T(8,128)(2,1)}, u32[]{:S(2)}) copy-start(bf16[3,3,256,256]{3,2,1,0:T(8,128)(2,1)} %new.3) | copy-start | bytes 3538948
  28.6 3.8 %copy-start.3 = (bf16[2,512,512]{2,1,0:T(8,128)(2,1)S(1)}, bf16[2,512,512]{2,1,0:T(8,128)(2,1)}, u32[]{:S(2)}) copy-start(bf16[2,512,512]{2,1,0:T(8,128)(2,1)} %get-tuple-element.19.refs_0_) | copy-start | bytes 3145732
  36.1 34.7 %copy-start.2 = (f32[3,256,256]{2,1,0:T(8,128)S(1)}, f32[3,256,256]{2,1,0:T(8,128)}, u32[]{:S(2)}) copy-start(f32[3,256,256]{2,1,0:T(8,128)} %diag.1) | copy-start | bytes 2359300
  36.1 3.0 %collective-permute-start.9 = (bf16[768,256]{1,0:T(8,128)(2,1)S(1)}, bf16[768,256]{1,0:T(8,128)(2,1)S(1)}, u32[]{:S(2)}, u32[]{:S(2)}) collective-permute-start(bf16[768,256]{1,0:T(8,128)(2,1)S(1)} %get-tuple-element.25), channel_id=1, source_target_pairs={{0,4},{1,5},{2,6},{3,7},{4,0},{5,1},{6,2},{7,3},{8,12},{9,13},{10,... | collective-permute-start | bytes 1179656 | tf_op jit(solution)/shard_map/ppermute | solution.py:20
  36.2 18.4 %collective-permute-start.7 = (bf16[2,3,2,64,256]{4,3,2,1,0:T(8,128)(2,1)S(1)}, bf16[2,3,2,64,256]{4,3,2,1,0:T(8,128)(2,1)S(1)}, u32[]{:S(2)}, u32[]{:S(2)}) collective-permute-start(bf16[2,3,2,64,256]{4,3,2,1,0:T(8,128)(2,1)S(1)} %get-tuple-element.21), channel_id=1, source_target_pairs={{0,1},{1,0},{2,3},{3,2},{4,6},{5,7},{6,4},{7,5},{8,9},{9,8},{10,11... | collective-permute-start | bytes 1179656 | tf_op jit(solution)/shard_map/ppermute | solution.py:20
  39.6 6.2 %collective-permute-start.10 = (bf16[192,256]{1,0:T(8,128)(2,1)S(1)}, bf16[192,256]{1,0:T(8,128)(2,1)S(1)}, u32[]{:S(2)}, u32[]{:S(2)}) collective-permute-start(bf16[192,256]{1,0:T(8,128)(2,1)S(1)} %get-tuple-element.27), channel_id=1, source_target_pairs={{0,8},{1,9},{2,10},{3,11},{4,12},{5,13},{6,14},{7,15},{8,0},{9,1},... | collective-permute-start | bytes 294920 | tf_op jit(solution)/shard_map/ppermute | solution.py:20
  42.6 7.5 %collective-permute-start.11 = (bf16[192,256]{1,0:T(8,128)(2,1)S(1)}, bf16[192,256]{1,0:T(8,128)(2,1)S(1)}, u32[]{:S(2)}, u32[]{:S(2)}) collective-permute-start(bf16[192,256]{1,0:T(8,128)(2,1)S(1)} %get-tuple-element.28), channel_id=1, source_target_pairs={{0,16},{1,17},{2,18},{3,19},{4,20},{5,21},{6,22},{7,23},{8,24},{9,... | collective-permute-start | bytes 294920 | tf_op jit(solution)/shard_map/ppermute | solution.py:20
  43.7 6.5 %collective-permute-start.12 = (bf16[192,256]{1,0:T(8,128)(2,1)S(1)}, bf16[192,256]{1,0:T(8,128)(2,1)S(1)}, u32[]{:S(2)}, u32[]{:S(2)}) collective-permute-start(bf16[192,256]{1,0:T(8,128)(2,1)S(1)} %get-tuple-element.29), channel_id=1, source_target_pairs={{0,24},{1,25},{2,26},{3,27},{4,28},{5,29},{6,30},{7,31},{8,16},{9,... | collective-permute-start | bytes 294920 | tf_op jit(solution)/shard_map/ppermute | solution.py:20
  50.2 6.2 %collective-permute-start.13 = (bf16[192,256]{1,0:T(8,128)(2,1)S(1)}, bf16[192,256]{1,0:T(8,128)(2,1)S(1)}, u32[]{:S(2)}, u32[]{:S(2)}) collective-permute-start(bf16[192,256]{1,0:T(8,128)(2,1)S(1)} %shard_map.101.refs_0_), channel_id=1, source_target_pairs={{0,1},{1,0},{2,3},{3,2},{4,5},{5,4},{6,7},{7,6},{8,9},{9,8},{10,11... | collective-permute-start | bytes 294920 | tf_op jit(solution)/shard_map/ppermute | solution.py:20
  50.9 9.8 %collective-permute-start.14 = (bf16[192,256]{1,0:T(8,128)(2,1)S(1)}, bf16[192,256]{1,0:T(8,128)(2,1)S(1)}, u32[]{:S(2)}, u32[]{:S(2)}) collective-permute-start(bf16[192,256]{1,0:T(8,128)(2,1)S(1)} %shard_map.101.refs_0_), channel_id=1, source_target_pairs={{0,2},{1,3},{2,0},{3,1},{4,6},{5,7},{6,4},{7,5},{8,10},{9,11},{10,... | collective-permute-start | bytes 294920 | tf_op jit(solution)/shard_map/ppermute | solution.py:20
  52.4 9.1 %collective-permute-start.15 = (bf16[192,256]{1,0:T(8,128)(2,1)S(1)}, bf16[192,256]{1,0:T(8,128)(2,1)S(1)}, u32[]{:S(2)}, u32[]{:S(2)}) collective-permute-start(bf16[192,256]{1,0:T(8,128)(2,1)S(1)} %shard_map.101.refs_0_), channel_id=1, source_target_pairs={{0,3},{1,2},{2,1},{3,0},{4,7},{5,6},{6,5},{7,4},{8,11},{9,10},{10,... | collective-permute-start | bytes 294920 | tf_op jit(solution)/shard_map/ppermute | solution.py:20
  55.3 14.2 %collective-permute-start.8 = (bf16[1,3,2,64,256]{4,3,2,1,0:T(8,128)(2,1)S(1)}, bf16[1,3,2,64,256]{4,3,2,1,0:T(8,128)(2,1)S(1)}, u32[]{:S(2)}, u32[]{:S(2)}) collective-permute-start(bf16[1,3,2,64,256]{4,3,2,1,0:T(8,128)(2,1)S(1)} %get-tuple-element.23), channel_id=1, source_target_pairs={{0,2},{1,3},{2,0},{3,1},{4,5},{5,4},{6,7},{7,6},{8,10},{9,11},{10,... | collective-permute-start | bytes 589832 | tf_op jit(solution)/shard_map/ppermute | solution.py:20
  61.6 4.7 %collective-permute-start.16 = (bf16[192,256]{1,0:T(8,128)(2,1)S(1)}, bf16[192,256]{1,0:T(8,128)(2,1)S(1)}, u32[]{:S(2)}, u32[]{:S(2)}) collective-permute-start(bf16[192,256]{1,0:T(8,128)(2,1)S(1)} %shard_map.102.refs_0_), channel_id=1, source_target_pairs={{0,8},{1,9},{2,10},{3,11},{4,12},{5,13},{6,14},{7,15},{8,0},{9,1},... | collective-permute-start | bytes 294920 | tf_op jit(solution)/shard_map/ppermute | solution.py:20
  63.3 4.6 %collective-permute-start.17 = (bf16[192,256]{1,0:T(8,128)(2,1)S(1)}, bf16[192,256]{1,0:T(8,128)(2,1)S(1)}, u32[]{:S(2)}, u32[]{:S(2)}) collective-permute-start(bf16[192,256]{1,0:T(8,128)(2,1)S(1)} %shard_map.102.refs_0_), channel_id=1, source_target_pairs={{0,16},{1,17},{2,18},{3,19},{4,20},{5,21},{6,22},{7,23},{8,24},{9,... | collective-permute-start | bytes 294920 | tf_op jit(solution)/shard_map/ppermute | solution.py:20
  63.9 5.5 %collective-permute-start.18 = (bf16[192,256]{1,0:T(8,128)(2,1)S(1)}, bf16[192,256]{1,0:T(8,128)(2,1)S(1)}, u32[]{:S(2)}, u32[]{:S(2)}) collective-permute-start(bf16[192,256]{1,0:T(8,128)(2,1)S(1)} %shard_map.102.refs_0_), channel_id=1, source_target_pairs={{0,24},{1,25},{2,26},{3,27},{4,28},{5,29},{6,30},{7,31},{8,16},{9,... | collective-permute-start | bytes 294920 | tf_op jit(solution)/shard_map/ppermute | solution.py:20
  65.1 5.1 %collective-permute-start.19 = (bf16[192,256]{1,0:T(8,128)(2,1)S(1)}, bf16[192,256]{1,0:T(8,128)(2,1)S(1)}, u32[]{:S(2)}, u32[]{:S(2)}) collective-permute-start(bf16[192,256]{1,0:T(8,128)(2,1)S(1)} %shard_map.102.refs_0_), channel_id=1, source_target_pairs={{0,4},{1,5},{2,6},{3,7},{4,0},{5,1},{6,2},{7,3},{8,12},{9,13},{10,... | collective-permute-start | bytes 294920 | tf_op jit(solution)/shard_map/ppermute | solution.py:20
  66.3 3.9 %collective-permute-start.20 = (bf16[192,256]{1,0:T(8,128)(2,1)S(1)}, bf16[192,256]{1,0:T(8,128)(2,1)S(1)}, u32[]{:S(2)}, u32[]{:S(2)}) collective-permute-start(bf16[192,256]{1,0:T(8,128)(2,1)S(1)} %collective-permute-done.16.refs_1_), channel_id=1, source_target_pairs={{0,4},{1,5},{2,6},{3,7},{4,0},{5,1},{6,2},{7,3},{8,12},{9,13},{10,... | collective-permute-start | bytes 294920 | tf_op jit(solution)/shard_map/ppermute | solution.py:20
  67.9 2.3 %collective-permute-start.21 = (bf16[192,256]{1,0:T(8,128)(2,1)S(1)}, bf16[192,256]{1,0:T(8,128)(2,1)S(1)}, u32[]{:S(2)}, u32[]{:S(2)}) collective-permute-start(bf16[192,256]{1,0:T(8,128)(2,1)S(1)} %collective-permute-done.17.refs_2_), channel_id=1, source_target_pairs={{0,4},{1,5},{2,6},{3,7},{4,0},{5,1},{6,2},{7,3},{8,12},{9,13},{10,... | collective-permute-start | bytes 294920 | tf_op jit(solution)/shard_map/ppermute | solution.py:20
  69.5 1.3 %collective-permute-start.22 = (bf16[192,256]{1,0:T(8,128)(2,1)S(1)}, bf16[192,256]{1,0:T(8,128)(2,1)S(1)}, u32[]{:S(2)}, u32[]{:S(2)}) collective-permute-start(bf16[192,256]{1,0:T(8,128)(2,1)S(1)} %collective-permute-done.18.refs_3_), channel_id=1, source_target_pairs={{0,4},{1,5},{2,6},{3,7},{4,0},{5,1},{6,2},{7,3},{8,12},{9,13},{10,... | collective-permute-start | bytes 294920 | tf_op jit(solution)/shard_map/ppermute | solution.py:20

commit v2 on v1

--- a/solution.py
+++ b/solution.py
@@ -373,15 +373,15 @@
         own_parts += [part, core_swap(part)]
     far = {}
     for g in range(1, n_high):
-        far[g, 0] = permute(lower_old, spread(g, 0, 0, 1))
+        far[g, 0] = permute(sibling, spread(g, 0, 1))
     for g in range(1, n_high):
         for o in offsets[1:]:
-            far[g, o] = permute(sibling, spread(g, o, 1))
+            far[g, o] = permute(lower_old, spread(g, o, 0))
     far_parts = []
     for g in range(1, n_high):
         for o in offsets:
             both = [far[g, o], core_swap(far[g, o])]
-            far_parts += both if o else both[::-1]
+            far_parts += both
 
     w_shape = (2, slots * width, slots * width)
     ws = call(

time: 74.2 us -> 73.6 us (level)
  starting transfers between devices: 26 us -> 25 us
  waiting for transfers between devices: 29.8 us -> 30.7 us
    ppermute x23, starting transfers between devices: 26 us -> 25 us  [permute(): return lax.ppermute(value, ('row', 'col'), pairs)]
    ppermute x23, waiting for transfers between devices: 29.8 us -> 30.7 us  [permute(): return lax.ppermute(value, ('row', 'col'), pairs)]
  transfers between devices with their start and end apart: 23 -> 23, of which waited for: 9 -> 10; matrix products, arithmetic and copies ran while one was open for 0% -> 0% of each run, Pallas kernels for 13% -> 13%
where the time goes in v2:
time: 73.6 us; the launch traced here: 73.1 us
  waiting for transfers between devices  30.7 us (42%)
  starting transfers between devices  25 us (34%)
  Pallas kernels  15.8 us (21%)
  between operations  1.46 us (2%)
    ppermute x23, waiting for transfers between devices, permute(): return lax.ppermute(value, ('row', 'col'), pairs)  30.7 us
    ppermute x23, starting transfers between devices, permute(): return lax.ppermute(value, ('row', 'col'), pairs)  25 us
    pallas_call x1, Pallas kernels, per_device(): call(functools.partial(gather_kernel, n_high, slots), (pltpu.MemorySpace....  3.88 us
    pallas_call x1, Pallas kernels, per_device(): call(own_kernel, (jax.ShapeDtypeStruct(p_shape, F32), jax.ShapeDtypeStruc...  3.75 us
    pallas_call x1, Pallas kernels, per_device(): call(functools.partial(main_kernel, n_high, n_col), (jax.ShapeDtypeStruct...  3.66 us
    pallas_call x1, Pallas kernels, per_device(): call(final_kernel, pltpu.MemorySpace.HBM((t_count, t_count, width, width)...  2.46 us
  transfers between devices with their start and end apart: 23, of which 10 were waited for; matrix products, arithmetic and copies ran while one was open for 0% of the time, Pallas kernels for 13%

profile of v2, /device:TPU:0, one launch (start us, length us, event | category | flops | bytes accessed | tf_op | source)
XLA Modules:
  0.0 73.1 jit_solution(5414217111601392536)
XLA Ops:
  0.6 0.6 collective-permute-start
  1.2 4.4 %collective-permute-start.1 = (bf16[3,2,256,256]{3,2,1,0:T(8,128)(2,1)}, bf16[3,2,256,256]{3,2,1,0:T(8,128)(2,1)S(1)}, u32[]{:S(2)}, u32[]{:S(2)}) collective-permute-start(bf16[3,2,256,256]{3,2,1,0:T(8,128)(2,1)} %refs_0_.1), channel_id=1, source_target_pairs={{0,8},{5,13},{10,2},{15,7},{16,24},{21,29},{26,18},{31,23},{4,0},{... | collective-permute-start | bytes 2359304 | tf_op jit(solution)/shard_map/ppermute | solution.py:20
  5.6 3.3 %collective-permute-start.5 = (bf16[3,2,256,256]{3,2,1,0:T(8,128)(2,1)}, bf16[3,2,256,256]{3,2,1,0:T(8,128)(2,1)S(1)}, u32[]{:S(2)}, u32[]{:S(2)}) collective-permute-start(bf16[3,2,256,256]{3,2,1,0:T(8,128)(2,1)} %refs_0_.1), channel_id=1, source_target_pairs={{0,24},{5,29},{10,18},{15,23},{16,8},{21,13},{26,2},{31,7},{4,0},{... | collective-permute-start | bytes 2359304 | tf_op jit(solution)/shard_map/ppermute | solution.py:20
  9.0 0.0 collective-permute-done.refs_1_
  9.0 0.1 collective-permute-start.3
  9.0 6.4 %collective-permute-done.1.refs_2_ = bf16[3,2,256,256]{3,2,1,0:T(8,128)(2,1)S(1)} collective-permute-done((bf16[3,2,256,256]{3,2,1,0:T(8,128)(2,1)}, bf16[3,2,256,256]{3,2,1,0:T(8,128)(2,1)S(1)}, u32[]{:S(2)}, u32[]{:S(2)}) %collective-permute-start.1) | collective-permute-done | bytes 786464 | tf_op jit(solution)/shard_map/ppermute | solution.py:20
  15.4 0.0 collective-permute-start.2
  15.4 8.4 %collective-permute-done.5.refs_3_ = bf16[3,2,256,256]{3,2,1,0:T(8,128)(2,1)S(1)} collective-permute-done((bf16[3,2,256,256]{3,2,1,0:T(8,128)(2,1)}, bf16[3,2,256,256]{3,2,1,0:T(8,128)(2,1)S(1)}, u32[]{:S(2)}, u32[]{:S(2)}) %collective-permute-start.5) | collective-permute-done | bytes 786464 | tf_op jit(solution)/shard_map/ppermute | solution.py:20
  23.8 0.0 collective-permute-start.6
  23.8 0.0 collective-permute-done.3.refs_1_
  23.8 0.5 collective-permute-start.4
  25.0 0.1 stack.39.where
  25.1 0.1 pad_add_fusion.me
  25.2 0.0 copy-start
  25.2 3.9 %shard_map.95 = (bf16[2,512,512]{2,1,0:T(8,128)(2,1)}, bf16[2,512,512]{2,1,0:T(8,128)(2,1)}) custom-call(s32[3]{0:T(128)S(1)} %pad_add_fusion.me, s32[1,1]{1,0:T(1,128)S(6)} %copy.10.count, s32[1,96]{1,0:T(1,128)} %rows_in.1, s32[1,96]{1,0:T(1,128)} %cols_in.1, s32[16]{0:T(128)} %panel_in.1, bf16[96,256,256]{2,1,0:T(8,128)(2,1)} %bitcast.15), custom_call_target="tpu_custom_call" | custom-call | flops 1048576 | bytes 10485760 | tf_op jit(solution)/shard_map/pallas_call | solution.py:387
  29.0 0.0 collective-permute-done.2.refs_3_
  29.1 0.0 copy-done
  29.1 0.0 copy-start.1
  29.1 0.0 copy-start.3
  29.1 3.8 %shard_map.96 = (f32[3,512,256]{2,1,0:T(8,128)S(1)}, bf16[3,256,512]{2,1,0:T(8,128)(2,1)S(1)}) custom-call(s32[6]{0:T(128)S(1)} %stack.39.where, bf16[2,512,512]{2,1,0:T(8,128)(2,1)} %get-tuple-element.16.w_in, bf16[3,2,256,256]{3,2,1,0:T(8,128)(2,1)S(1)} %copy-done, bf16[3,2,256,256]{3,2,1,0:T(8,128)(2,1)S(1)} %copy-done, ...), custom_call_target="tpu_custom_call" | custom-call | flops 805306368 | bytes 3145728 | tf_op jit(solution)/shard_map/pallas_call | solution.py:416
  32.8 0.0 collective-permute-done.6.refs_4_
  32.9 0.0 collective-permute-done.4.refs_2_
  32.9 0.0 copy-done.1
  32.9 0.0 copy-done.3
  32.9 3.7 %shard_map.97 = (f32[2,3,2,64,256]{4,3,2,1,0:T(8,128)S(1)}, bf16[2,3,2,64,256]{4,3,2,1,0:T(8,128)(2,1)S(1)}, f32[768,256]{1,0:T(8,128)S(1)}, bf16[768,256]{1,0:T(8,128)(2,1)S(1)}) custom-call(s32[6]{0:T(128)S(1)} %stack.39.where, f32[3,512,256]{2,1,0:T(8,128)S(1)} %get-tuple-element.17.p_own, bf16[3,256,512]{2,1,0:T(8,128)(2,1)S(1)} %get-tuple-element.18.old_t, ...), custom_call_target="tpu_custom_call" | custom-call | flops 2415919104 | bytes 3145728 | tf_op jit(solution)/shard_map/pallas_call | solution.py:444
  36.6 0.0 copy-start.2
  36.6 0.3 collective-permute-start.9
  36.9 2.3 %collective-permute-start.7 = (bf16[2,3,2,64,256]{4,3,2,1,0:T(8,128)(2,1)S(1)}, bf16[2,3,2,64,256]{4,3,2,1,0:T(8,128)(2,1)S(1)}, u32[]{:S(2)}, u32[]{:S(2)}) collective-permute-start(bf16[2,3,2,64,256]{4,3,2,1,0:T(8,128)(2,1)S(1)} %get-tuple-element.21), channel_id=1, source_target_pairs={{0,1},{1,0},{2,3},{3,2},{4,6},{5,7},{6,4},{7,5},{8,9},{9,8},{10,11... | collective-permute-start | bytes 1179656 | tf_op jit(solution)/shard_map/ppermute | solution.py:20
  39.2 0.0 collective-permute-done.9
  39.2 0.6 shard_map.100
  39.9 2.8 %collective-permute-start.10 = (bf16[192,256]{1,0:T(8,128)(2,1)S(1)}, bf16[192,256]{1,0:T(8,128)(2,1)S(1)}, u32[]{:S(2)}, u32[]{:S(2)}) collective-permute-start(bf16[192,256]{1,0:T(8,128)(2,1)S(1)} %get-tuple-element.27), channel_id=1, source_target_pairs={{0,8},{1,9},{2,10},{3,11},{4,12},{5,13},{6,14},{7,15},{8,0},{9,1},... | collective-permute-start | bytes 294920 | tf_op jit(solution)/shard_map/ppermute | solution.py:20
  42.6 0.9 %collective-permute-start.11 = (bf16[192,256]{1,0:T(8,128)(2,1)S(1)}, bf16[192,256]{1,0:T(8,128)(2,1)S(1)}, u32[]{:S(2)}, u32[]{:S(2)}) collective-permute-start(bf16[192,256]{1,0:T(8,128)(2,1)S(1)} %get-tuple-element.28), channel_id=1, source_target_pairs={{0,16},{1,17},{2,18},{3,19},{4,20},{5,21},{6,22},{7,23},{8,24},{9,... | collective-permute-start | bytes 294920 | tf_op jit(solution)/shard_map/ppermute | solution.py:20
  43.6 0.6 collective-permute-start.12
  44.2 1.5 %collective-permute-done.10.refs_1_ = bf16[192,256]{1,0:T(8,128)(2,1)S(1)} collective-permute-done((bf16[192,256]{1,0:T(8,128)(2,1)S(1)}, bf16[192,256]{1,0:T(8,128)(2,1)S(1)}, u32[]{:S(2)}, u32[]{:S(2)}) %collective-permute-start.10) | collective-permute-done | bytes 98336 | tf_op jit(solution)/shard_map/ppermute | solution.py:20
  45.7 4.4 %collective-permute-done.11.refs_2_ = bf16[192,256]{1,0:T(8,128)(2,1)S(1)} collective-permute-done((bf16[192,256]{1,0:T(8,128)(2,1)S(1)}, bf16[192,256]{1,0:T(8,128)(2,1)S(1)}, u32[]{:S(2)}, u32[]{:S(2)}) %collective-permute-start.11) | collective-permute-done | bytes 98336 | tf_op jit(solution)/shard_map/ppermute | solution.py:20
  50.1 0.0 collective-permute-done.12.refs_3_
  50.1 0.7 collective-permute-start.13
  50.8 1.5 %collective-permute-start.14 = (bf16[192,256]{1,0:T(8,128)(2,1)S(1)}, bf16[192,256]{1,0:T(8,128)(2,1)S(1)}, u32[]{:S(2)}, u32[]{:S(2)}) collective-permute-start(bf16[192,256]{1,0:T(8,128)(2,1)S(1)} %shard_map.101.refs_0_), channel_id=1, source_target_pairs={{0,2},{1,3},{2,0},{3,1},{4,6},{5,7},{6,4},{7,5},{8,10},{9,11},{10,... | collective-permute-start | bytes 294920 | tf_op jit(solution)/shard_map/ppermute | solution.py:20
  52.3 2.2 %collective-permute-start.15 = (bf16[192,256]{1,0:T(8,128)(2,1)S(1)}, bf16[192,256]{1,0:T(8,128)(2,1)S(1)}, u32[]{:S(2)}, u32[]{:S(2)}) collective-permute-start(bf16[192,256]{1,0:T(8,128)(2,1)S(1)} %shard_map.101.refs_0_), channel_id=1, source_target_pairs={{0,3},{1,2},{2,1},{3,0},{4,7},{5,6},{6,5},{7,4},{8,11},{9,10},{10,... | collective-permute-start | bytes 294920 | tf_op jit(solution)/shard_map/ppermute | solution.py:20
  54.6 0.0 collective-permute-done.7.received
  54.6 0.6 shard_map.98
  55.2 1.1 %collective-permute-start.8 = (bf16[1,3,2,64,256]{4,3,2,1,0:T(8,128)(2,1)S(1)}, bf16[1,3,2,64,256]{4,3,2,1,0:T(8,128)(2,1)S(1)}, u32[]{:S(2)}, u32[]{:S(2)}) collective-permute-start(bf16[1,3,2,64,256]{4,3,2,1,0:T(8,128)(2,1)S(1)} %get-tuple-element.23), channel_id=1, source_target_pairs={{0,2},{1,3},{2,0},{3,1},{4,5},{5,4},{6,7},{7,6},{8,10},{9,11},{10,... | collective-permute-start | bytes 589832 | tf_op jit(solution)/shard_map/ppermute | solution.py:20
  56.3 0.0 collective-permute-done.13.refs_1_
  56.3 4.2 %collective-permute-done.14.refs_2_ = bf16[192,256]{1,0:T(8,128)(2,1)S(1)} collective-permute-done((bf16[192,256]{1,0:T(8,128)(2,1)S(1)}, bf16[192,256]{1,0:T(8,128)(2,1)S(1)}, u32[]{:S(2)}, u32[]{:S(2)}) %collective-permute-start.14) | collective-permute-done | bytes 98336 | tf_op jit(solution)/shard_map/ppermute | solution.py:20
  60.5 0.9 %collective-permute-done.15.refs_3_ = bf16[192,256]{1,0:T(8,128)(2,1)S(1)} collective-permute-done((bf16[192,256]{1,0:T(8,128)(2,1)S(1)}, bf16[192,256]{1,0:T(8,128)(2,1)S(1)}, u32[]{:S(2)}, u32[]{:S(2)}) %collective-permute-start.15) | collective-permute-done | bytes 98336 | tf_op jit(solution)/shard_map/ppermute | solution.py:20
  61.4 0.1 shard_map.102.refs_0_
  61.5 1.6 %collective-permute-start.16 = (bf16[192,256]{1,0:T(8,128)(2,1)S(1)}, bf16[192,256]{1,0:T(8,128)(2,1)S(1)}, u32[]{:S(2)}, u32[]{:S(2)}) collective-permute-start(bf16[192,256]{1,0:T(8,128)(2,1)S(1)} %shard_map.102.refs_0_), channel_id=1, source_target_pairs={{0,8},{1,9},{2,10},{3,11},{4,12},{5,13},{6,14},{7,15},{8,0},{9,1},... | collective-permute-start | bytes 294920 | tf_op jit(solution)/shard_map/ppermute | solution.py:20
  63.1 0.7 collective-permute-start.17
  63.8 1.2 %collective-permute-start.18 = (bf16[192,256]{1,0:T(8,128)(2,1)S(1)}, bf16[192,256]{1,0:T(8,128)(2,1)S(1)}, u32[]{:S(2)}, u32[]{:S(2)}) collective-permute-start(bf16[192,256]{1,0:T(8,128)(2,1)S(1)} %shard_map.102.refs_0_), channel_id=1, source_target_pairs={{0,24},{1,25},{2,26},{3,27},{4,28},{5,29},{6,30},{7,31},{8,16},{9,... | collective-permute-start | bytes 294920 | tf_op jit(solution)/shard_map/ppermute | solution.py:20
  65.0 0.0 collective-permute-start.19
  65.0 1.1 %collective-permute-done.16.refs_1_ = bf16[192,256]{1,0:T(8,128)(2,1)S(1)} collective-permute-done((bf16[192,256]{1,0:T(8,128)(2,1)S(1)}, bf16[192,256]{1,0:T(8,128)(2,1)S(1)}, u32[]{:S(2)}, u32[]{:S(2)}) %collective-permute-start.16) | collective-permute-done | bytes 98336 | tf_op jit(solution)/shard_map/ppermute | solution.py:20
  66.2 0.0 collective-permute-start.20
  66.2 1.6 %collective-permute-done.17.refs_2_ = bf16[192,256]{1,0:T(8,128)(2,1)S(1)} collective-permute-done((bf16[192,256]{1,0:T(8,128)(2,1)S(1)}, bf16[192,256]{1,0:T(8,128)(2,1)S(1)}, u32[]{:S(2)}, u32[]{:S(2)}) %collective-permute-start.17) | collective-permute-done | bytes 98336 | tf_op jit(solution)/shard_map/ppermute | solution.py:20
  67.7 0.0 collective-permute-start.21
  67.7 1.6 %collective-permute-done.18.refs_3_ = bf16[192,256]{1,0:T(8,128)(2,1)S(1)} collective-permute-done((bf16[192,256]{1,0:T(8,128)(2,1)S(1)}, bf16[192,256]{1,0:T(8,128)(2,1)S(1)}, u32[]{:S(2)}, u32[]{:S(2)}) %collective-permute-start.18) | collective-permute-done | bytes 98336 | tf_op jit(solution)/shard_map/ppermute | solution.py:20
  69.4 0.0 collective-permute-start.22
  69.4 0.0 collective-permute-done.8.refs_1_
  69.4 0.7 shard_map.99
  70.1 0.0 collective-permute-done.19.refs_4_
  70.1 0.0 collective-permute-done.20.refs_5_
  70.1 0.0 collective-permute-done.21.refs_6_
  70.1 0.6 collective-permute-done.22.refs_7_
  70.7 0.0 copy-done.2
  70.7 2.5 %shard_map.103 = f32[3,3,256,256]{3,2,1,0:T(8,128)} custom-call(s32[6]{0:T(128)S(1)} %stack.39.where, bf16[3,3,256,256]{3,2,1,0:T(8,128)(2,1)S(1)} %copy-done.1, f32[3,256,256]{2,1,0:T(8,128)S(1)} %copy-done.2, bf16[192,256]{1,0:T(8,128)(2,1)S(1)} %shard_map.102.refs_0_, bf16[192,256]{1,0:T(8,128)(2,1)S(1)} %collective-permute-done.16.refs_1_, ...), custom_call_target="tpu_custom_call" | custom-call | flops 536870912 | bytes 3538944 | tf_op jit(solution)/shard_map/pallas_call | solution.py:515
  (1 shorter events, 0.0 us)
Async XLA Ops:
  0.6 8.3 %collective-permute-start = (bf16[3,2,256,256]{3,2,1,0:T(8,128)(2,1)}, bf16[3,2,256,256]{3,2,1,0:T(8,128)(2,1)S(1)}, u32[]{:S(2)}, u32[]{:S(2)}) collective-permute-start(bf16[3,2,256,256]{3,2,1,0:T(8,128)(2,1)} %refs_0_.1), channel_id=1, source_target_pairs={{0,4},{1,5},{2,6},{3,7},{4,0},{5,1},{6,2},{7,3},{8,12},{9,13},{10,... | collective-permute-start | bytes 2359304 | tf_op jit(solution)/shard_map/ppermute | solution.py:20
  1.2 14.2 %collective-permute-start.1 = (bf16[3,2,256,256]{3,2,1,0:T(8,128)(2,1)}, bf16[3,2,256,256]{3,2,1,0:T(8,128)(2,1)S(1)}, u32[]{:S(2)}, u32[]{:S(2)}) collective-permute-start(bf16[3,2,256,256]{3,2,1,0:T(8,128)(2,1)} %refs_0_.1), channel_id=1, source_target_pairs={{0,8},{5,13},{10,2},{15,7},{16,24},{21,29},{26,18},{31,23},{4,0},{... | collective-permute-start | bytes 2359304 | tf_op jit(solution)/shard_map/ppermute | solution.py:20
  5.6 18.2 %collective-permute-start.5 = (bf16[3,2,256,256]{3,2,1,0:T(8,128)(2,1)}, bf16[3,2,256,256]{3,2,1,0:T(8,128)(2,1)S(1)}, u32[]{:S(2)}, u32[]{:S(2)}) collective-permute-start(bf16[3,2,256,256]{3,2,1,0:T(8,128)(2,1)} %refs_0_.1), channel_id=1, source_target_pairs={{0,24},{5,29},{10,18},{15,23},{16,8},{21,13},{26,2},{31,7},{4,0},{... | collective-permute-start | bytes 2359304 | tf_op jit(solution)/shard_map/ppermute | solution.py:20
  9.0 14.9 %collective-permute-start.3 = (bf16[3,2,256,256]{3,2,1,0:T(8,128)(2,1)S(1)}, bf16[3,2,256,256]{3,2,1,0:T(8,128)(2,1)}, u32[]{:S(2)}, u32[]{:S(2)}) collective-permute-start(bf16[3,2,256,256]{3,2,1,0:T(8,128)(2,1)S(1)} %collective-permute-done.refs_1_), channel_id=1, source_target_pairs={{4,16},{1,21},{14,26},{11,31},{20,0},{17,5},{30,10},{27,15},{0,4},... | collective-permute-start | bytes 2359304 | tf_op jit(solution)/shard_map/ppermute | solution.py:20
  15.4 13.7 %collective-permute-start.2 = (bf16[3,2,256,256]{3,2,1,0:T(8,128)(2,1)S(1)}, bf16[3,2,256,256]{3,2,1,0:T(8,128)(2,1)S(1)}, u32[]{:S(2)}, u32[]{:S(2)}) collective-permute-start(bf16[3,2,256,256]{3,2,1,0:T(8,128)(2,1)S(1)} %collective-permute-done.1.refs_2_), channel_id=1, source_target_pairs={{0,4},{1,5},{2,6},{3,7},{4,0},{5,1},{6,2},{7,3},{8,12},{9,13},{10,... | collective-permute-start | bytes 2359304 | tf_op jit(solution)/shard_map/ppermute | solution.py:20
  23.8 9.0 %collective-permute-start.6 = (bf16[3,2,256,256]{3,2,1,0:T(8,128)(2,1)S(1)}, bf16[3,2,256,256]{3,2,1,0:T(8,128)(2,1)}, u32[]{:S(2)}, u32[]{:S(2)}) collective-permute-start(bf16[3,2,256,256]{3,2,1,0:T(8,128)(2,1)S(1)} %collective-permute-done.5.refs_3_), channel_id=1, source_target_pairs={{0,4},{1,5},{2,6},{3,7},{4,0},{5,1},{6,2},{7,3},{8,12},{9,13},{10,... | collective-permute-start | bytes 2359304 | tf_op jit(solution)/shard_map/ppermute | solution.py:20
  23.8 9.0 %collective-permute-start.4 = (bf16[3,2,256,256]{3,2,1,0:T(8,128)(2,1)}, bf16[3,2,256,256]{3,2,1,0:T(8,128)(2,1)}, u32[]{:S(2)}, u32[]{:S(2)}) collective-permute-start(bf16[3,2,256,256]{3,2,1,0:T(8,128)(2,1)} %collective-permute-done.3.refs_1_), channel_id=1, source_target_pairs={{0,4},{1,5},{2,6},{3,7},{4,0},{5,1},{6,2},{7,3},{8,12},{9,13},{10,... | collective-permute-start | bytes 2359304 | tf_op jit(solution)/shard_map/ppermute | solution.py:20
  25.2 3.9 %copy-start = (bf16[3,2,256,256]{3,2,1,0:T(8,128)(2,1)S(1)}, bf16[3,2,256,256]{3,2,1,0:T(8,128)(2,1)}, u32[]{:S(2)}) copy-start(bf16[3,2,256,256]{3,2,1,0:T(8,128)(2,1)} %refs_0_.1) | copy-start | bytes 2359300
  29.1 3.8 %copy-start.1 = (bf16[3,3,256,256]{3,2,1,0:T(8,128)(2,1)S(1)}, bf16[3,3,256,256]{3,2,1,0:T(8,128)(2,1)}, u32[]{:S(2)}) copy-start(bf16[3,3,256,256]{3,2,1,0:T(8,128)(2,1)} %new.3) | copy-start | bytes 3538948
  29.1 3.8 %copy-start.3 = (bf16[2,512,512]{2,1,0:T(8,128)(2,1)S(1)}, bf16[2,512,512]{2,1,0:T(8,128)(2,1)}, u32[]{:S(2)}) copy-start(bf16[2,512,512]{2,1,0:T(8,128)(2,1)} %get-tuple-element.19.refs_0_) | copy-start | bytes 3145732
  36.6 34.1 %copy-start.2 = (f32[3,256,256]{2,1,0:T(8,128)S(1)}, f32[3,256,256]{2,1,0:T(8,128)}, u32[]{:S(2)}) copy-start(f32[3,256,256]{2,1,0:T(8,128)} %diag.1) | copy-start | bytes 2359300
  36.6 2.7 %collective-permute-start.9 = (bf16[768,256]{1,0:T(8,128)(2,1)S(1)}, bf16[768,256]{1,0:T(8,128)(2,1)S(1)}, u32[]{:S(2)}, u32[]{:S(2)}) collective-permute-start(bf16[768,256]{1,0:T(8,128)(2,1)S(1)} %get-tuple-element.25), channel_id=1, source_target_pairs={{0,4},{1,5},{2,6},{3,7},{4,0},{5,1},{6,2},{7,3},{8,12},{9,13},{10,... | collective-permute-start | bytes 1179656 | tf_op jit(solution)/shard_map/ppermute | solution.py:20
  36.9 17.7 %collective-permute-start.7 = (bf16[2,3,2,64,256]{4,3,2,1,0:T(8,128)(2,1)S(1)}, bf16[2,3,2,64,256]{4,3,2,1,0:T(8,128)(2,1)S(1)}, u32[]{:S(2)}, u32[]{:S(2)}) collective-permute-start(bf16[2,3,2,64,256]{4,3,2,1,0:T(8,128)(2,1)S(1)} %get-tuple-element.21), channel_id=1, source_target_pairs={{0,1},{1,0},{2,3},{3,2},{4,6},{5,7},{6,4},{7,5},{8,9},{9,8},{10,11... | collective-permute-start | bytes 1179656 | tf_op jit(solution)/shard_map/ppermute | solution.py:20
  39.9 5.8 %collective-permute-start.10 = (bf16[192,256]{1,0:T(8,128)(2,1)S(1)}, bf16[192,256]{1,0:T(8,128)(2,1)S(1)}, u32[]{:S(2)}, u32[]{:S(2)}) collective-permute-start(bf16[192,256]{1,0:T(8,128)(2,1)S(1)} %get-tuple-element.27), channel_id=1, source_target_pairs={{0,8},{1,9},{2,10},{3,11},{4,12},{5,13},{6,14},{7,15},{8,0},{9,1},... | collective-permute-start | bytes 294920 | tf_op jit(solution)/shard_map/ppermute | solution.py:20
  42.6 7.4 %collective-permute-start.11 = (bf16[192,256]{1,0:T(8,128)(2,1)S(1)}, bf16[192,256]{1,0:T(8,128)(2,1)S(1)}, u32[]{:S(2)}, u32[]{:S(2)}) collective-permute-start(bf16[192,256]{1,0:T(8,128)(2,1)S(1)} %get-tuple-element.28), channel_id=1, source_target_pairs={{0,16},{1,17},{2,18},{3,19},{4,20},{5,21},{6,22},{7,23},{8,24},{9,... | collective-permute-start | bytes 294920 | tf_op jit(solution)/shard_map/ppermute | solution.py:20
  43.6 6.5 %collective-permute-start.12 = (bf16[192,256]{1,0:T(8,128)(2,1)S(1)}, bf16[192,256]{1,0:T(8,128)(2,1)S(1)}, u32[]{:S(2)}, u32[]{:S(2)}) collective-permute-start(bf16[192,256]{1,0:T(8,128)(2,1)S(1)} %get-tuple-element.29), channel_id=1, source_target_pairs={{0,24},{1,25},{2,26},{3,27},{4,28},{5,29},{6,30},{7,31},{8,16},{9,... | collective-permute-start | bytes 294920 | tf_op jit(solution)/shard_map/ppermute | solution.py:20
  50.1 6.2 %collective-permute-start.13 = (bf16[192,256]{1,0:T(8,128)(2,1)S(1)}, bf16[192,256]{1,0:T(8,128)(2,1)S(1)}, u32[]{:S(2)}, u32[]{:S(2)}) collective-permute-start(bf16[192,256]{1,0:T(8,128)(2,1)S(1)} %shard_map.101.refs_0_), channel_id=1, source_target_pairs={{0,1},{1,0},{2,3},{3,2},{4,5},{5,4},{6,7},{7,6},{8,9},{9,8},{10,11... | collective-permute-start | bytes 294920 | tf_op jit(solution)/shard_map/ppermute | solution.py:20
  50.8 9.6 %collective-permute-start.14 = (bf16[192,256]{1,0:T(8,128)(2,1)S(1)}, bf16[192,256]{1,0:T(8,128)(2,1)S(1)}, u32[]{:S(2)}, u32[]{:S(2)}) collective-permute-start(bf16[192,256]{1,0:T(8,128)(2,1)S(1)} %shard_map.101.refs_0_), channel_id=1, source_target_pairs={{0,2},{1,3},{2,0},{3,1},{4,6},{5,7},{6,4},{7,5},{8,10},{9,11},{10,... | collective-permute-start | bytes 294920 | tf_op jit(solution)/shard_map/ppermute | solution.py:20
  52.3 9.1 %collective-permute-start.15 = (bf16[192,256]{1,0:T(8,128)(2,1)S(1)}, bf16[192,256]{1,0:T(8,128)(2,1)S(1)}, u32[]{:S(2)}, u32[]{:S(2)}) collective-permute-start(bf16[192,256]{1,0:T(8,128)(2,1)S(1)} %shard_map.101.refs_0_), channel_id=1, source_target_pairs={{0,3},{1,2},{2,1},{3,0},{4,7},{5,6},{6,5},{7,4},{8,11},{9,10},{10,... | collective-permute-start | bytes 294920 | tf_op jit(solution)/shard_map/ppermute | solution.py:20
  55.2 14.2 %collective-permute-start.8 = (bf16[1,3,2,64,256]{4,3,2,1,0:T(8,128)(2,1)S(1)}, bf16[1,3,2,64,256]{4,3,2,1,0:T(8,128)(2,1)S(1)}, u32[]{:S(2)}, u32[]{:S(2)}) collective-permute-start(bf16[1,3,2,64,256]{4,3,2,1,0:T(8,128)(2,1)S(1)} %get-tuple-element.23), channel_id=1, source_target_pairs={{0,2},{1,3},{2,0},{3,1},{4,5},{5,4},{6,7},{7,6},{8,10},{9,11},{10,... | collective-permute-start | bytes 589832 | tf_op jit(solution)/shard_map/ppermute | solution.py:20
  61.5 4.7 %collective-permute-start.16 = (bf16[192,256]{1,0:T(8,128)(2,1)S(1)}, bf16[192,256]{1,0:T(8,128)(2,1)S(1)}, u32[]{:S(2)}, u32[]{:S(2)}) collective-permute-start(bf16[192,256]{1,0:T(8,128)(2,1)S(1)} %shard_map.102.refs_0_), channel_id=1, source_target_pairs={{0,8},{1,9},{2,10},{3,11},{4,12},{5,13},{6,14},{7,15},{8,0},{9,1},... | collective-permute-start | bytes 294920 | tf_op jit(solution)/shard_map/ppermute | solution.py:20
  63.1 4.6 %collective-permute-start.17 = (bf16[192,256]{1,0:T(8,128)(2,1)S(1)}, bf16[192,256]{1,0:T(8,128)(2,1)S(1)}, u32[]{:S(2)}, u32[]{:S(2)}) collective-permute-start(bf16[192,256]{1,0:T(8,128)(2,1)S(1)} %shard_map.102.refs_0_), channel_id=1, source_target_pairs={{0,16},{1,17},{2,18},{3,19},{4,20},{5,21},{6,22},{7,23},{8,24},{9,... | collective-permute-start | bytes 294920 | tf_op jit(solution)/shard_map/ppermute | solution.py:20
  63.8 5.5 %collective-permute-start.18 = (bf16[192,256]{1,0:T(8,128)(2,1)S(1)}, bf16[192,256]{1,0:T(8,128)(2,1)S(1)}, u32[]{:S(2)}, u32[]{:S(2)}) collective-permute-start(bf16[192,256]{1,0:T(8,128)(2,1)S(1)} %shard_map.102.refs_0_), channel_id=1, source_target_pairs={{0,24},{1,25},{2,26},{3,27},{4,28},{5,29},{6,30},{7,31},{8,16},{9,... | collective-permute-start | bytes 294920 | tf_op jit(solution)/shard_map/ppermute | solution.py:20
  65.0 5.1 %collective-permute-start.19 = (bf16[192,256]{1,0:T(8,128)(2,1)S(1)}, bf16[192,256]{1,0:T(8,128)(2,1)S(1)}, u32[]{:S(2)}, u32[]{:S(2)}) collective-permute-start(bf16[192,256]{1,0:T(8,128)(2,1)S(1)} %shard_map.102.refs_0_), channel_id=1, source_target_pairs={{0,4},{1,5},{2,6},{3,7},{4,0},{5,1},{6,2},{7,3},{8,12},{9,13},{10,... | collective-permute-start | bytes 294920 | tf_op jit(solution)/shard_map/ppermute | solution.py:20
  66.2 3.9 %collective-permute-start.20 = (bf16[192,256]{1,0:T(8,128)(2,1)S(1)}, bf16[192,256]{1,0:T(8,128)(2,1)S(1)}, u32[]{:S(2)}, u32[]{:S(2)}) collective-permute-start(bf16[192,256]{1,0:T(8,128)(2,1)S(1)} %collective-permute-done.16.refs_1_), channel_id=1, source_target_pairs={{0,4},{1,5},{2,6},{3,7},{4,0},{5,1},{6,2},{7,3},{8,12},{9,13},{10,... | collective-permute-start | bytes 294920 | tf_op jit(solution)/shard_map/ppermute | solution.py:20
  67.7 2.4 %collective-permute-start.21 = (bf16[192,256]{1,0:T(8,128)(2,1)S(1)}, bf16[192,256]{1,0:T(8,128)(2,1)S(1)}, u32[]{:S(2)}, u32[]{:S(2)}) collective-permute-start(bf16[192,256]{1,0:T(8,128)(2,1)S(1)} %collective-permute-done.17.refs_2_), channel_id=1, source_target_pairs={{0,4},{1,5},{2,6},{3,7},{4,0},{5,1},{6,2},{7,3},{8,12},{9,13},{10,... | collective-permute-start | bytes 294920 | tf_op jit(solution)/shard_map/ppermute | solution.py:20
  69.4 1.3 %collective-permute-start.22 = (bf16[192,256]{1,0:T(8,128)(2,1)S(1)}, bf16[192,256]{1,0:T(8,128)(2,1)S(1)}, u32[]{:S(2)}, u32[]{:S(2)}) collective-permute-start(bf16[192,256]{1,0:T(8,128)(2,1)S(1)} %collective-permute-done.18.refs_3_), channel_id=1, source_target_pairs={{0,4},{1,5},{2,6},{3,7},{4,0},{5,1},{6,2},{7,3},{8,12},{9,13},{10,... | collective-permute-start | bytes 294920 | tf_op jit(solution)/shard_map/ppermute | solution.py:20

commit v3 on v1

--- a/solution.py
+++ b/solution.py
@@ -124,13 +124,15 @@
     return both[: w.shape[1]] + both[w.shape[1] :]
 
 
-def own_kernel(where, w_in, old, *refs):
-    options, (p_out, old_out, w, lo, w_sem, sems) = refs[:-6], refs[-6:]
+def own_kernel(where, w_in, old, new, *refs):
+    options, (p_out, old_out, new_out, w, lo, w_sem, sems) = refs[:-7], refs[-7:]
     w_copy = pltpu.make_async_copy(w_in, w, w_sem)
     w_copy.start()
     wait = fill(where, options, lo, sems)
     for t in range(lo.shape[0]):
         old_out[t] = old[t].reshape(lo.shape[1:]).T
+        for s in range(t):
+            new_out[t * (t - 1) // 2 + s] = new[t, s].T
     w_copy.wait()
     for t in range(lo.shape[0]):
         wait(t)
@@ -146,8 +148,8 @@
     width = new.shape[-1]
     slots = old_t.shape[-1] // width
     n_far = n_high - 1
-    w_ins, parts = refs[:n_far], refs[n_far:-8]
-    u_keep, u_send, g_keep, g_send, lo, u_all, g_all, sems = refs[-8:]
+    w_ins, parts = refs[:n_far], refs[n_far:-7]
+    u_keep, u_send, g_all, g_send, lo, u_all, sems = refs[-7:]
     cases = len(parts) // max(n_far, 1)
     waits = [
         fill(where, parts[g * cases : (g + 1) * cases], lo.at[g], sems.at[g]) for g in range(n_far)
@@ -155,6 +157,8 @@
     for t in range(t_count):
         for wait in waits:
             wait(t)
+    share = width // n_col
+    count = n_col // 2
     totals = [
         p_own[t] + sum(stacked_dot(w_ins[g][...], lo[g, t]) for g in range(n_far))
         for t in range(t_count)
@@ -162,6 +166,12 @@
     for s in range(t_count):
         u_all[s] = -totals[s]
         panel = (-totals[s]).astype(BF16)
+        for value, out in ((where[4], u_keep), (1 - where[4], u_send)):
+            for j in range(count):
+                start = piece_index(where[1], value, j, count) * share
+                for p in range(slots):
+                    window = pl.ds(pl.multiple_of(p * width + start, 16), share)
+                    out[j, s, p] = u_all[s, window, :].astype(out.dtype)
         for t in range(s + 1, t_count):
             totals[t] += jnp.dot(panel, new[t, s], preferred_element_type=F32)
         rest = old_t[s:].reshape(-1, old_t.shape[-1])
@@ -170,18 +180,8 @@
             g_all[pl.ds((t * (t + 1) // 2 + s) * width, width), :] = crossed[
                 (t - s) * width : (t - s + 1) * width
             ]
-    half = g_keep.shape[0]
-    g_keep[...] = g_all[pl.ds(pl.multiple_of(where[1] * half, 16), half), :]
+    half = g_send.shape[0]
     g_send[...] = g_all[pl.ds(pl.multiple_of((1 - where[1]) * half, 16), half), :].astype(BF16)
-    share = width // n_col
-    count = n_col // 2
-    for value, out in ((where[4], u_keep), (1 - where[4], u_send)):
-        for j in range(count):
-            start = piece_index(where[1], value, j, count) * share
-            for t in range(t_count):
-                for s in range(slots):
-                    window = pl.ds(pl.multiple_of(s * width + start, 16), share)
-                    out[j, t, s] = u_all[t, window, :].astype(out.dtype)
 
 
 def halving_kernel(bit, where, keep, received, keep_out, send_out):
@@ -195,7 +195,8 @@
 def split_kernel(where, keep, received, own, *sends):
     def piece(m):
         index = where[3] ^ m
-        return keep[index] + received[index].astype(F32)
+        kept = keep[where[1] * received.shape[0] + index]
+        return kept + received[index].astype(F32)
 
     own[...] = piece(0)
     for m, send in enumerate(sends):
@@ -233,7 +234,7 @@
     return parts[0] + parts[1]
 
 
-def final_kernel(where, new, diag, *refs):
+def final_kernel(where, new, new_t, diag, *refs):
     pieces, (out, g_all, y, zero, sems) = refs[:-5], refs[-5:]
     t_count = new.shape[0]
     width = new.shape[-1]
@@ -273,7 +274,7 @@
             give(y.at[t, s], t, s)
         diagonal = diag[t] - g(t, t)
         for s in range(t):
-            diagonal -= wide_dot(new[t, s], blocks[t, s], ((0,), (0,)))
+            diagonal -= wide_dot(new_t[t * (t - 1) // 2 + s], blocks[t, s], ((1,), (0,)))
         blocks[t, t] = diagonal
         y[t, t] = diagonal
         give(y.at[t, t], t, t)
@@ -413,13 +414,14 @@
         ],
     )
     p_shape = (t_count, slots * width, width)
-    p_own, old_t = call(
+    p_own, old_t, new_t = call(
         own_kernel,
         (
             jax.ShapeDtypeStruct(p_shape, F32),
             jax.ShapeDtypeStruct((t_count, width, slots * width), BF16),
+            jax.ShapeDtypeStruct((max(t_count * (t_count - 1) // 2, 1), width, width), BF16),
         ),
-        [SMEM, ANY, VMEM] + [ANY] * len(own_parts),
+        [SMEM, ANY, VMEM, VMEM] + [ANY] * len(own_parts),
         [
             pltpu.VMEM(w_shape, BF16),
             pltpu.VMEM(p_shape, BF16),
@@ -433,6 +435,7 @@
         where,
         pltpu.with_memory_space_constraint(ws[0], pltpu.MemorySpace.HBM),
         lower_old,
+        lower_new,
         *own_parts,
     )
 
@@ -441,19 +444,18 @@
     half = n_blocks * width // 2
     piece = half // n_plane
     u_shape = (n_col // 2, t_count, slots, share, width)
-    u_keep, u_send, g_keep, g_send = call(
+    u_keep, u_send, g_all, g_send = call(
         functools.partial(main_kernel, n_high, n_col),
         (
             jax.ShapeDtypeStruct(u_shape, F32),
             jax.ShapeDtypeStruct(u_shape, BF16),
-            jax.ShapeDtypeStruct((half, width), F32),
+            jax.ShapeDtypeStruct((2 * half, width), F32),
             jax.ShapeDtypeStruct((half, width), BF16),
         ),
         [SMEM, VMEM, VMEM, VMEM] + [VMEM] * (n_high - 1) + [ANY] * len(far_parts),
         [
             pltpu.VMEM((n_high - 1, t_count, slots * width, width), BF16),
             pltpu.VMEM((t_count, slots * width, width), F32),
-            pltpu.VMEM((n_blocks * width, width), F32),
             pltpu.SemaphoreType.DMA((n_high - 1, t_count, slots)),
         ],
         flops=2 * block * width * slots * t_count * (2 * n_cand + 4),
@@ -485,7 +487,7 @@
             moved=values[0].size * 2 * len(values),
         )(*values)
 
-    keep = g_keep.reshape(n_plane, piece, width)
+    keep = g_all.reshape(2 * n_plane, piece, width)
     received = core_swap(g_send)
     u_received = permute(u_send, step(0))
     shape = (piece, width)
@@ -495,7 +497,7 @@
         [SMEM, VMEM, VMEM],
         flops=half * width,
         moved=half * width * 8,
-    )(where, keep, received.reshape(keep.shape))
+    )(where, keep, received.reshape(n_plane, piece, width))
     arrived = [
         permute(send, pairs(anyone, lambda r, c: (r ^ 2 * (m + 1), c)))
         for m, send in enumerate(sends)
@@ -515,7 +517,7 @@
     supernode_inverse = call(
         final_kernel,
         pltpu.MemorySpace.HBM((t_count, t_count, width, width), F32),
-        [SMEM] + [VMEM] * (2 + len(pieces)),
+        [SMEM] + [VMEM] * (3 + len(pieces)),
         [
             pltpu.VMEM((n_blocks * width, width), BF16),
             pltpu.VMEM((t_count, t_count, width, width), F32),
@@ -524,7 +526,7 @@
         ],
         flops=2 * block * width * 16,
         moved=block * t_count * t_count * 6,
-    )(where, lower_new, diag_inverse, *pieces)
+    )(where, lower_new, new_t, diag_inverse, *pieces)
     panel_inverse = add(BF16, [u_keep, u_received])[0]
     return (panel_inverse, supernode_inverse)
 

time: 74.2 us -> 74.3 us (level)
  no operation moved by 1% of the time
where the time goes in v3:
time: 74.3 us; the launch traced here: 73.3 us
  waiting for transfers between devices  29.8 us (40%)
  starting transfers between devices  26 us (35%)
  Pallas kernels  15.9 us (21%)
  between operations  1.43 us (2%)
    ppermute x23, waiting for transfers between devices, permute(): return lax.ppermute(value, ('row', 'col'), pairs)  29.8 us
    ppermute x23, starting transfers between devices, permute(): return lax.ppermute(value, ('row', 'col'), pairs)  26 us
    pallas_call x1, Pallas kernels, per_device(): call(functools.partial(gather_kernel, n_high, slots), (pltpu.MemorySpace....  4.01 us
    pallas_call x1, Pallas kernels, per_device(): call(own_kernel, (jax.ShapeDtypeStruct(p_shape, F32), jax.ShapeDtypeStruc...  3.83 us
    pallas_call x1, Pallas kernels, per_device(): call(functools.partial(main_kernel, n_high, n_col), (jax.ShapeDtypeStruct...  3.55 us
    pallas_call x1, Pallas kernels, per_device(): call(final_kernel, pltpu.MemorySpace.HBM((t_count, t_count, width, width)...  2.47 us
  transfers between devices with their start and end apart: 23, of which 9 were waited for; matrix products, arithmetic and copies ran while one was open for 0% of the time, Pallas kernels for 13%

profile of v3, /device:TPU:0, one launch (start us, length us, event | category | flops | bytes accessed | tf_op | source)
XLA Modules:
  0.0 73.3 jit_solution(14100305336788716104)
XLA Ops:
  0.6 0.6 collective-permute-start
  1.2 4.4 %collective-permute-start.1 = (bf16[3,2,256,256]{3,2,1,0:T(8,128)(2,1)}, bf16[3,2,256,256]{3,2,1,0:T(8,128)(2,1)S(1)}, u32[]{:S(2)}, u32[]{:S(2)}) collective-permute-start(bf16[3,2,256,256]{3,2,1,0:T(8,128)(2,1)} %refs_0_.1), channel_id=1, source_target_pairs={{0,8},{5,13},{10,2},{15,7},{16,24},{21,29},{26,18},{31,23},{4,0},{... | collective-permute-start | bytes 2359304 | tf_op jit(solution)/shard_map/ppermute | solution.py:20
  5.6 0.2 collective-permute-start.3
  5.8 0.0 collective-permute-done.refs_1_
  5.8 1.5 %collective-permute-start.5 = (bf16[3,2,256,256]{3,2,1,0:T(8,128)(2,1)S(1)}, bf16[3,2,256,256]{3,2,1,0:T(8,128)(2,1)}, u32[]{:S(2)}, u32[]{:S(2)}) collective-permute-start(bf16[3,2,256,256]{3,2,1,0:T(8,128)(2,1)S(1)} %collective-permute-done.refs_1_), channel_id=1, source_target_pairs={{4,24},{1,29},{14,18},{11,23},{20,8},{17,13},{30,2},{27,7},{0,0},{... | collective-permute-start | bytes 2359304 | tf_op jit(solution)/shard_map/ppermute | solution.py:20
  7.4 13.8 %collective-permute-done.1.refs_2_ = bf16[3,2,256,256]{3,2,1,0:T(8,128)(2,1)S(1)} collective-permute-done((bf16[3,2,256,256]{3,2,1,0:T(8,128)(2,1)}, bf16[3,2,256,256]{3,2,1,0:T(8,128)(2,1)S(1)}, u32[]{:S(2)}, u32[]{:S(2)}) %collective-permute-start.1) | collective-permute-done | bytes 786464 | tf_op jit(solution)/shard_map/ppermute | solution.py:20
  21.2 0.0 collective-permute-start.2
  21.2 0.0 collective-permute-done.3.refs_2_
  21.2 0.5 collective-permute-start.4
  21.7 0.0 collective-permute-done.5.refs_3_
  21.7 2.1 %collective-permute-start.6 = (bf16[3,2,256,256]{3,2,1,0:T(8,128)(2,1)}, bf16[3,2,256,256]{3,2,1,0:T(8,128)(2,1)}, u32[]{:S(2)}, u32[]{:S(2)}) collective-permute-start(bf16[3,2,256,256]{3,2,1,0:T(8,128)(2,1)} %collective-permute-done.5.refs_3_), channel_id=1, source_target_pairs={{0,4},{1,5},{2,6},{3,7},{4,0},{5,1},{6,2},{7,3},{8,12},{9,13},{10,... | collective-permute-start | bytes 2359304 | tf_op jit(solution)/shard_map/ppermute | solution.py:20
  24.5 0.1 stack.39.where
  24.6 0.1 pad_add_fusion.me
  24.6 0.0 copy-start
  24.7 0.0 copy-start.1
  24.7 4.0 %shard_map.95 = (bf16[2,512,512]{2,1,0:T(8,128)(2,1)}, bf16[2,512,512]{2,1,0:T(8,128)(2,1)}) custom-call(s32[3]{0:T(128)S(1)} %pad_add_fusion.me, s32[1,1]{1,0:T(1,128)S(6)} %copy.10.count, s32[1,96]{1,0:T(1,128)} %rows_in.1, s32[1,96]{1,0:T(1,128)} %cols_in.1, s32[16]{0:T(128)} %panel_in.1, bf16[96,256,256]{2,1,0:T(8,128)(2,1)} %bitcast.15), custom_call_target="tpu_custom_call" | custom-call | flops 1048576 | bytes 10485760 | tf_op jit(solution)/shard_map/pallas_call | solution.py:388
  28.7 0.0 collective-permute-done.2.refs_3_
  28.7 0.0 copy-done
  28.7 0.0 copy-done.1
  28.7 0.0 copy-start.3
  28.7 3.8 %shard_map.96 = (f32[3,512,256]{2,1,0:T(8,128)S(1)}, bf16[3,256,512]{2,1,0:T(8,128)(2,1)S(1)}, bf16[3,256,256]{2,1,0:T(8,128)(2,1)S(1)}) custom-call(s32[6]{0:T(128)S(1)} %stack.39.where, bf16[2,512,512]{2,1,0:T(8,128)(2,1)} %get-tuple-element.17.w_in, bf16[3,2,256,256]{3,2,1,0:T(8,128)(2,1)S(1)} %copy-done.1, bf16[3,3,256,256]{3,2,1,0:T(8,128)(2,1)S(1)} %copy-done, ...), custom_call_target="tpu_custom_call" | custom-call | flops 805306368 | bytes 3145728 | tf_op jit(solution)/shard_map/pallas_call | solution.py:417
  32.6 0.0 collective-permute-done.4.refs_1_
  32.6 0.0 collective-permute-done.6.refs_4_
  32.6 0.0 copy-done.3
  32.6 3.5 %shard_map.97 = (f32[2,3,2,64,256]{4,3,2,1,0:T(8,128)S(1)}, bf16[2,3,2,64,256]{4,3,2,1,0:T(8,128)(2,1)S(1)}, f32[1536,256]{1,0:T(8,128)S(1)}, bf16[768,256]{1,0:T(8,128)(2,1)S(1)}) custom-call(s32[6]{0:T(128)S(1)} %stack.39.where, f32[3,512,256]{2,1,0:T(8,128)S(1)} %get-tuple-element.18.p_own, bf16[3,256,512]{2,1,0:T(8,128)(2,1)S(1)} %get-tuple-element.19.old_t, ...), custom_call_target="tpu_custom_call" | custom-call | flops 2415919104 | bytes 3145728 | tf_op jit(solution)/shard_map/pallas_call | solution.py:447
  36.1 0.2 collective-permute-start.9
  36.3 2.8 %collective-permute-start.7 = (bf16[2,3,2,64,256]{4,3,2,1,0:T(8,128)(2,1)S(1)}, bf16[2,3,2,64,256]{4,3,2,1,0:T(8,128)(2,1)S(1)}, u32[]{:S(2)}, u32[]{:S(2)}) collective-permute-start(bf16[2,3,2,64,256]{4,3,2,1,0:T(8,128)(2,1)S(1)} %get-tuple-element.22), channel_id=1, source_target_pairs={{0,1},{1,0},{2,3},{3,2},{4,6},{5,7},{6,4},{7,5},{8,9},{9,8},{10,11... | collective-permute-start | bytes 1179656 | tf_op jit(solution)/shard_map/ppermute | solution.py:20
  39.1 0.0 collective-permute-done.9
  39.1 0.6 shard_map.100
  39.7 0.0 copy-start.2
  39.7 3.0 %collective-permute-start.10 = (bf16[192,256]{1,0:T(8,128)(2,1)S(1)}, bf16[192,256]{1,0:T(8,128)(2,1)S(1)}, u32[]{:S(2)}, u32[]{:S(2)}) collective-permute-start(bf16[192,256]{1,0:T(8,128)(2,1)S(1)} %get-tuple-element.29), channel_id=1, source_target_pairs={{0,8},{1,9},{2,10},{3,11},{4,12},{5,13},{6,14},{7,15},{8,0},{9,1},... | collective-permute-start | bytes 294920 | tf_op jit(solution)/shard_map/ppermute | solution.py:20
  42.7 1.0 %collective-permute-start.11 = (bf16[192,256]{1,0:T(8,128)(2,1)S(1)}, bf16[192,256]{1,0:T(8,128)(2,1)S(1)}, u32[]{:S(2)}, u32[]{:S(2)}) collective-permute-start(bf16[192,256]{1,0:T(8,128)(2,1)S(1)} %get-tuple-element.30), channel_id=1, source_target_pairs={{0,16},{1,17},{2,18},{3,19},{4,20},{5,21},{6,22},{7,23},{8,24},{9,... | collective-permute-start | bytes 294920 | tf_op jit(solution)/shard_map/ppermute | solution.py:20
  43.7 0.5 collective-permute-start.12
  44.2 1.6 %collective-permute-done.10.refs_1_ = bf16[192,256]{1,0:T(8,128)(2,1)S(1)} collective-permute-done((bf16[192,256]{1,0:T(8,128)(2,1)S(1)}, bf16[192,256]{1,0:T(8,128)(2,1)S(1)}, u32[]{:S(2)}, u32[]{:S(2)}) %collective-permute-start.10) | collective-permute-done | bytes 98336 | tf_op jit(solution)/shard_map/ppermute | solution.py:20
  45.9 4.4 %collective-permute-done.11.refs_2_ = bf16[192,256]{1,0:T(8,128)(2,1)S(1)} collective-permute-done((bf16[192,256]{1,0:T(8,128)(2,1)S(1)}, bf16[192,256]{1,0:T(8,128)(2,1)S(1)}, u32[]{:S(2)}, u32[]{:S(2)}) %collective-permute-start.11) | collective-permute-done | bytes 98336 | tf_op jit(solution)/shard_map/ppermute | solution.py:20
  50.2 0.0 collective-permute-done.12.refs_3_
  50.3 0.7 collective-permute-start.13
  51.0 1.5 %collective-permute-start.14 = (bf16[192,256]{1,0:T(8,128)(2,1)S(1)}, bf16[192,256]{1,0:T(8,128)(2,1)S(1)}, u32[]{:S(2)}, u32[]{:S(2)}) collective-permute-start(bf16[192,256]{1,0:T(8,128)(2,1)S(1)} %shard_map.101.refs_0_), channel_id=1, source_target_pairs={{0,2},{1,3},{2,0},{3,1},{4,6},{5,7},{6,4},{7,5},{8,10},{9,11},{10,... | collective-permute-start | bytes 294920 | tf_op jit(solution)/shard_map/ppermute | solution.py:20
  52.5 2.2 %collective-permute-start.15 = (bf16[192,256]{1,0:T(8,128)(2,1)S(1)}, bf16[192,256]{1,0:T(8,128)(2,1)S(1)}, u32[]{:S(2)}, u32[]{:S(2)}) collective-permute-start(bf16[192,256]{1,0:T(8,128)(2,1)S(1)} %shard_map.101.refs_0_), channel_id=1, source_target_pairs={{0,3},{1,2},{2,1},{3,0},{4,7},{5,6},{6,5},{7,4},{8,11},{9,10},{10,... | collective-permute-start | bytes 294920 | tf_op jit(solution)/shard_map/ppermute | solution.py:20
  54.7 0.0 collective-permute-done.7.received
  54.8 0.6 shard_map.98
  55.4 1.1 %collective-permute-start.8 = (bf16[1,3,2,64,256]{4,3,2,1,0:T(8,128)(2,1)S(1)}, bf16[1,3,2,64,256]{4,3,2,1,0:T(8,128)(2,1)S(1)}, u32[]{:S(2)}, u32[]{:S(2)}) collective-permute-start(bf16[1,3,2,64,256]{4,3,2,1,0:T(8,128)(2,1)S(1)} %get-tuple-element.24), channel_id=1, source_target_pairs={{0,2},{1,3},{2,0},{3,1},{4,5},{5,4},{6,7},{7,6},{8,10},{9,11},{10,... | collective-permute-start | bytes 589832 | tf_op jit(solution)/shard_map/ppermute | solution.py:20
  56.5 0.0 collective-permute-done.13.refs_1_
  56.5 4.4 %collective-permute-done.14.refs_2_ = bf16[192,256]{1,0:T(8,128)(2,1)S(1)} collective-permute-done((bf16[192,256]{1,0:T(8,128)(2,1)S(1)}, bf16[192,256]{1,0:T(8,128)(2,1)S(1)}, u32[]{:S(2)}, u32[]{:S(2)}) %collective-permute-start.14) | collective-permute-done | bytes 98336 | tf_op jit(solution)/shard_map/ppermute | solution.py:20
  60.8 0.8 %collective-permute-done.15.refs_3_ = bf16[192,256]{1,0:T(8,128)(2,1)S(1)} collective-permute-done((bf16[192,256]{1,0:T(8,128)(2,1)S(1)}, bf16[192,256]{1,0:T(8,128)(2,1)S(1)}, u32[]{:S(2)}, u32[]{:S(2)}) %collective-permute-start.15) | collective-permute-done | bytes 98336 | tf_op jit(solution)/shard_map/ppermute | solution.py:20
  61.6 0.1 shard_map.102.refs_0_
  61.7 1.7 %collective-permute-start.16 = (bf16[192,256]{1,0:T(8,128)(2,1)S(1)}, bf16[192,256]{1,0:T(8,128)(2,1)S(1)}, u32[]{:S(2)}, u32[]{:S(2)}) collective-permute-start(bf16[192,256]{1,0:T(8,128)(2,1)S(1)} %shard_map.102.refs_0_), channel_id=1, source_target_pairs={{0,8},{1,9},{2,10},{3,11},{4,12},{5,13},{6,14},{7,15},{8,0},{9,1},... | collective-permute-start | bytes 294920 | tf_op jit(solution)/shard_map/ppermute | solution.py:20
  63.4 0.6 collective-permute-start.17
  64.0 1.2 %collective-permute-start.18 = (bf16[192,256]{1,0:T(8,128)(2,1)S(1)}, bf16[192,256]{1,0:T(8,128)(2,1)S(1)}, u32[]{:S(2)}, u32[]{:S(2)}) collective-permute-start(bf16[192,256]{1,0:T(8,128)(2,1)S(1)} %shard_map.102.refs_0_), channel_id=1, source_target_pairs={{0,24},{1,25},{2,26},{3,27},{4,28},{5,29},{6,30},{7,31},{8,16},{9,... | collective-permute-start | bytes 294920 | tf_op jit(solution)/shard_map/ppermute | solution.py:20
  65.2 0.0 collective-permute-start.19
  65.2 1.1 %collective-permute-done.16.refs_1_ = bf16[192,256]{1,0:T(8,128)(2,1)S(1)} collective-permute-done((bf16[192,256]{1,0:T(8,128)(2,1)S(1)}, bf16[192,256]{1,0:T(8,128)(2,1)S(1)}, u32[]{:S(2)}, u32[]{:S(2)}) %collective-permute-start.16) | collective-permute-done | bytes 98336 | tf_op jit(solution)/shard_map/ppermute | solution.py:20
  66.3 0.0 collective-permute-start.20
  66.3 1.7 %collective-permute-done.17.refs_2_ = bf16[192,256]{1,0:T(8,128)(2,1)S(1)} collective-permute-done((bf16[192,256]{1,0:T(8,128)(2,1)S(1)}, bf16[192,256]{1,0:T(8,128)(2,1)S(1)}, u32[]{:S(2)}, u32[]{:S(2)}) %collective-permute-start.17) | collective-permute-done | bytes 98336 | tf_op jit(solution)/shard_map/ppermute | solution.py:20
  68.0 0.0 collective-permute-start.21
  68.0 1.5 %collective-permute-done.18.refs_3_ = bf16[192,256]{1,0:T(8,128)(2,1)S(1)} collective-permute-done((bf16[192,256]{1,0:T(8,128)(2,1)S(1)}, bf16[192,256]{1,0:T(8,128)(2,1)S(1)}, u32[]{:S(2)}, u32[]{:S(2)}) %collective-permute-start.18) | collective-permute-done | bytes 98336 | tf_op jit(solution)/shard_map/ppermute | solution.py:20
  69.5 0.0 collective-permute-start.22
  69.5 0.0 collective-permute-done.8.refs_1_
  69.5 0.7 shard_map.99
  70.3 0.0 collective-permute-done.19.refs_4_
  70.3 0.0 collective-permute-done.20.refs_5_
  70.3 0.0 collective-permute-done.21.refs_6_
  70.3 0.6 collective-permute-done.22.refs_7_
  70.8 0.0 copy-done.2
  70.8 2.5 %shard_map.103 = f32[3,3,256,256]{3,2,1,0:T(8,128)} custom-call(s32[6]{0:T(128)S(1)} %stack.39.where, bf16[3,3,256,256]{3,2,1,0:T(8,128)(2,1)S(1)} %copy-done, bf16[3,256,256]{2,1,0:T(8,128)(2,1)S(1)} %get-tuple-element.25.new_t, f32[3,256,256]{2,1,0:T(8,128)S(1)} %copy-done.2, bf16[192,256]{1,0:T(8,128)(2,1)S(1)} %shard_map.102.refs_0_, ...), custom_call_target="tpu_custom_call" | custom-call | flops 536870912 | bytes 3538944 | tf_op jit(solution)/shard_map/pallas_call | solution.py:517
  (1 shorter events, 0.0 us)
Async XLA Ops:
  0.6 5.2 %collective-permute-start = (bf16[3,2,256,256]{3,2,1,0:T(8,128)(2,1)}, bf16[3,2,256,256]{3,2,1,0:T(8,128)(2,1)S(1)}, u32[]{:S(2)}, u32[]{:S(2)}) collective-permute-start(bf16[3,2,256,256]{3,2,1,0:T(8,128)(2,1)} %refs_0_.1), channel_id=1, source_target_pairs={{0,4},{1,5},{2,6},{3,7},{4,0},{5,1},{6,2},{7,3},{8,12},{9,13},{10,... | collective-permute-start | bytes 2359304 | tf_op jit(solution)/shard_map/ppermute | solution.py:20
  1.2 20.0 %collective-permute-start.1 = (bf16[3,2,256,256]{3,2,1,0:T(8,128)(2,1)}, bf16[3,2,256,256]{3,2,1,0:T(8,128)(2,1)S(1)}, u32[]{:S(2)}, u32[]{:S(2)}) collective-permute-start(bf16[3,2,256,256]{3,2,1,0:T(8,128)(2,1)} %refs_0_.1), channel_id=1, source_target_pairs={{0,8},{5,13},{10,2},{15,7},{16,24},{21,29},{26,18},{31,23},{4,0},{... | collective-permute-start | bytes 2359304 | tf_op jit(solution)/shard_map/ppermute | solution.py:20
  5.6 15.6 %collective-permute-start.3 = (bf16[3,2,256,256]{3,2,1,0:T(8,128)(2,1)}, bf16[3,2,256,256]{3,2,1,0:T(8,128)(2,1)S(1)}, u32[]{:S(2)}, u32[]{:S(2)}) collective-permute-start(bf16[3,2,256,256]{3,2,1,0:T(8,128)(2,1)} %refs_0_.1), channel_id=1, source_target_pairs={{0,20},{5,17},{10,30},{15,27},{16,4},{21,1},{26,14},{31,11},{4,0},... | collective-permute-start | bytes 2359304 | tf_op jit(solution)/shard_map/ppermute | solution.py:20
  5.8 15.9 %collective-permute-start.5 = (bf16[3,2,256,256]{3,2,1,0:T(8,128)(2,1)S(1)}, bf16[3,2,256,256]{3,2,1,0:T(8,128)(2,1)}, u32[]{:S(2)}, u32[]{:S(2)}) collective-permute-start(bf16[3,2,256,256]{3,2,1,0:T(8,128)(2,1)S(1)} %collective-permute-done.refs_1_), channel_id=1, source_target_pairs={{4,24},{1,29},{14,18},{11,23},{20,8},{17,13},{30,2},{27,7},{0,0},{... | collective-permute-start | bytes 2359304 | tf_op jit(solution)/shard_map/ppermute | solution.py:20
  21.2 7.5 %collective-permute-start.2 = (bf16[3,2,256,256]{3,2,1,0:T(8,128)(2,1)S(1)}, bf16[3,2,256,256]{3,2,1,0:T(8,128)(2,1)S(1)}, u32[]{:S(2)}, u32[]{:S(2)}) collective-permute-start(bf16[3,2,256,256]{3,2,1,0:T(8,128)(2,1)S(1)} %collective-permute-done.1.refs_2_), channel_id=1, source_target_pairs={{0,4},{1,5},{2,6},{3,7},{4,0},{5,1},{6,2},{7,3},{8,12},{9,13},{10,... | collective-permute-start | bytes 2359304 | tf_op jit(solution)/shard_map/ppermute | solution.py:20
  21.2 11.4 %collective-permute-start.4 = (bf16[3,2,256,256]{3,2,1,0:T(8,128)(2,1)S(1)}, bf16[3,2,256,256]{3,2,1,0:T(8,128)(2,1)}, u32[]{:S(2)}, u32[]{:S(2)}) collective-permute-start(bf16[3,2,256,256]{3,2,1,0:T(8,128)(2,1)S(1)} %collective-permute-done.3.refs_2_), channel_id=1, source_target_pairs={{0,4},{1,5},{2,6},{3,7},{4,0},{5,1},{6,2},{7,3},{8,12},{9,13},{10,... | collective-permute-start | bytes 2359304 | tf_op jit(solution)/shard_map/ppermute | solution.py:20
  21.7 10.9 %collective-permute-start.6 = (bf16[3,2,256,256]{3,2,1,0:T(8,128)(2,1)}, bf16[3,2,256,256]{3,2,1,0:T(8,128)(2,1)}, u32[]{:S(2)}, u32[]{:S(2)}) collective-permute-start(bf16[3,2,256,256]{3,2,1,0:T(8,128)(2,1)} %collective-permute-done.5.refs_3_), channel_id=1, source_target_pairs={{0,4},{1,5},{2,6},{3,7},{4,0},{5,1},{6,2},{7,3},{8,12},{9,13},{10,... | collective-permute-start | bytes 2359304 | tf_op jit(solution)/shard_map/ppermute | solution.py:20
  24.6 4.0 %copy-start = (bf16[3,3,256,256]{3,2,1,0:T(8,128)(2,1)S(1)}, bf16[3,3,256,256]{3,2,1,0:T(8,128)(2,1)}, u32[]{:S(2)}) copy-start(bf16[3,3,256,256]{3,2,1,0:T(8,128)(2,1)} %new.5) | copy-start | bytes 3538948
  24.7 4.0 %copy-start.1 = (bf16[3,2,256,256]{3,2,1,0:T(8,128)(2,1)S(1)}, bf16[3,2,256,256]{3,2,1,0:T(8,128)(2,1)}, u32[]{:S(2)}) copy-start(bf16[3,2,256,256]{3,2,1,0:T(8,128)(2,1)} %refs_0_.1) | copy-start | bytes 2359300
  28.7 3.9 %copy-start.3 = (bf16[2,512,512]{2,1,0:T(8,128)(2,1)S(1)}, bf16[2,512,512]{2,1,0:T(8,128)(2,1)}, u32[]{:S(2)}) copy-start(bf16[2,512,512]{2,1,0:T(8,128)(2,1)} %get-tuple-element.20.refs_0_) | copy-start | bytes 3145732
  36.1 2.9 %collective-permute-start.9 = (bf16[768,256]{1,0:T(8,128)(2,1)S(1)}, bf16[768,256]{1,0:T(8,128)(2,1)S(1)}, u32[]{:S(2)}, u32[]{:S(2)}) collective-permute-start(bf16[768,256]{1,0:T(8,128)(2,1)S(1)} %get-tuple-element.27), channel_id=1, source_target_pairs={{0,4},{1,5},{2,6},{3,7},{4,0},{5,1},{6,2},{7,3},{8,12},{9,13},{10,... | collective-permute-start | bytes 1179656 | tf_op jit(solution)/shard_map/ppermute | solution.py:20
  36.3 18.4 %collective-permute-start.7 = (bf16[2,3,2,64,256]{4,3,2,1,0:T(8,128)(2,1)S(1)}, bf16[2,3,2,64,256]{4,3,2,1,0:T(8,128)(2,1)S(1)}, u32[]{:S(2)}, u32[]{:S(2)}) collective-permute-start(bf16[2,3,2,64,256]{4,3,2,1,0:T(8,128)(2,1)S(1)} %get-tuple-element.22), channel_id=1, source_target_pairs={{0,1},{1,0},{2,3},{3,2},{4,6},{5,7},{6,4},{7,5},{8,9},{9,8},{10,11... | collective-permute-start | bytes 1179656 | tf_op jit(solution)/shard_map/ppermute | solution.py:20
  39.7 31.1 %copy-start.2 = (f32[3,256,256]{2,1,0:T(8,128)S(1)}, f32[3,256,256]{2,1,0:T(8,128)}, u32[]{:S(2)}) copy-start(f32[3,256,256]{2,1,0:T(8,128)} %diag.1) | copy-start | bytes 2359300
  39.7 6.2 %collective-permute-start.10 = (bf16[192,256]{1,0:T(8,128)(2,1)S(1)}, bf16[192,256]{1,0:T(8,128)(2,1)S(1)}, u32[]{:S(2)}, u32[]{:S(2)}) collective-permute-start(bf16[192,256]{1,0:T(8,128)(2,1)S(1)} %get-tuple-element.29), channel_id=1, source_target_pairs={{0,8},{1,9},{2,10},{3,11},{4,12},{5,13},{6,14},{7,15},{8,0},{9,1},... | collective-permute-start | bytes 294920 | tf_op jit(solution)/shard_map/ppermute | solution.py:20
  42.7 7.5 %collective-permute-start.11 = (bf16[192,256]{1,0:T(8,128)(2,1)S(1)}, bf16[192,256]{1,0:T(8,128)(2,1)S(1)}, u32[]{:S(2)}, u32[]{:S(2)}) collective-permute-start(bf16[192,256]{1,0:T(8,128)(2,1)S(1)} %get-tuple-element.30), channel_id=1, source_target_pairs={{0,16},{1,17},{2,18},{3,19},{4,20},{5,21},{6,22},{7,23},{8,24},{9,... | collective-permute-start | bytes 294920 | tf_op jit(solution)/shard_map/ppermute | solution.py:20
  43.7 6.5 %collective-permute-start.12 = (bf16[192,256]{1,0:T(8,128)(2,1)S(1)}, bf16[192,256]{1,0:T(8,128)(2,1)S(1)}, u32[]{:S(2)}, u32[]{:S(2)}) collective-permute-start(bf16[192,256]{1,0:T(8,128)(2,1)S(1)} %get-tuple-element.31), channel_id=1, source_target_pairs={{0,24},{1,25},{2,26},{3,27},{4,28},{5,29},{6,30},{7,31},{8,16},{9,... | collective-permute-start | bytes 294920 | tf_op jit(solution)/shard_map/ppermute | solution.py:20
  50.3 6.2 %collective-permute-start.13 = (bf16[192,256]{1,0:T(8,128)(2,1)S(1)}, bf16[192,256]{1,0:T(8,128)(2,1)S(1)}, u32[]{:S(2)}, u32[]{:S(2)}) collective-permute-start(bf16[192,256]{1,0:T(8,128)(2,1)S(1)} %shard_map.101.refs_0_), channel_id=1, source_target_pairs={{0,1},{1,0},{2,3},{3,2},{4,5},{5,4},{6,7},{7,6},{8,9},{9,8},{10,11... | collective-permute-start | bytes 294920 | tf_op jit(solution)/shard_map/ppermute | solution.py:20
  51.0 9.8 %collective-permute-start.14 = (bf16[192,256]{1,0:T(8,128)(2,1)S(1)}, bf16[192,256]{1,0:T(8,128)(2,1)S(1)}, u32[]{:S(2)}, u32[]{:S(2)}) collective-permute-start(bf16[192,256]{1,0:T(8,128)(2,1)S(1)} %shard_map.101.refs_0_), channel_id=1, source_target_pairs={{0,2},{1,3},{2,0},{3,1},{4,6},{5,7},{6,4},{7,5},{8,10},{9,11},{10,... | collective-permute-start | bytes 294920 | tf_op jit(solution)/shard_map/ppermute | solution.py:20
  52.5 9.1 %collective-permute-start.15 = (bf16[192,256]{1,0:T(8,128)(2,1)S(1)}, bf16[192,256]{1,0:T(8,128)(2,1)S(1)}, u32[]{:S(2)}, u32[]{:S(2)}) collective-permute-start(bf16[192,256]{1,0:T(8,128)(2,1)S(1)} %shard_map.101.refs_0_), channel_id=1, source_target_pairs={{0,3},{1,2},{2,1},{3,0},{4,7},{5,6},{6,5},{7,4},{8,11},{9,10},{10,... | collective-permute-start | bytes 294920 | tf_op jit(solution)/shard_map/ppermute | solution.py:20
  55.4 14.2 %collective-permute-start.8 = (bf16[1,3,2,64,256]{4,3,2,1,0:T(8,128)(2,1)S(1)}, bf16[1,3,2,64,256]{4,3,2,1,0:T(8,128)(2,1)S(1)}, u32[]{:S(2)}, u32[]{:S(2)}) collective-permute-start(bf16[1,3,2,64,256]{4,3,2,1,0:T(8,128)(2,1)S(1)} %get-tuple-element.24), channel_id=1, source_target_pairs={{0,2},{1,3},{2,0},{3,1},{4,5},{5,4},{6,7},{7,6},{8,10},{9,11},{10,... | collective-permute-start | bytes 589832 | tf_op jit(solution)/shard_map/ppermute | solution.py:20
  61.7 4.7 %collective-permute-start.16 = (bf16[192,256]{1,0:T(8,128)(2,1)S(1)}, bf16[192,256]{1,0:T(8,128)(2,1)S(1)}, u32[]{:S(2)}, u32[]{:S(2)}) collective-permute-start(bf16[192,256]{1,0:T(8,128)(2,1)S(1)} %shard_map.102.refs_0_), channel_id=1, source_target_pairs={{0,8},{1,9},{2,10},{3,11},{4,12},{5,13},{6,14},{7,15},{8,0},{9,1},... | collective-permute-start | bytes 294920 | tf_op jit(solution)/shard_map/ppermute | solution.py:20
  63.4 4.6 %collective-permute-start.17 = (bf16[192,256]{1,0:T(8,128)(2,1)S(1)}, bf16[192,256]{1,0:T(8,128)(2,1)S(1)}, u32[]{:S(2)}, u32[]{:S(2)}) collective-permute-start(bf16[192,256]{1,0:T(8,128)(2,1)S(1)} %shard_map.102.refs_0_), channel_id=1, source_target_pairs={{0,16},{1,17},{2,18},{3,19},{4,20},{5,21},{6,22},{7,23},{8,24},{9,... | collective-permute-start | bytes 294920 | tf_op jit(solution)/shard_map/ppermute | solution.py:20
  64.0 5.5 %collective-permute-start.18 = (bf16[192,256]{1,0:T(8,128)(2,1)S(1)}, bf16[192,256]{1,0:T(8,128)(2,1)S(1)}, u32[]{:S(2)}, u32[]{:S(2)}) collective-permute-start(bf16[192,256]{1,0:T(8,128)(2,1)S(1)} %shard_map.102.refs_0_), channel_id=1, source_target_pairs={{0,24},{1,25},{2,26},{3,27},{4,28},{5,29},{6,30},{7,31},{8,16},{9,... | collective-permute-start | bytes 294920 | tf_op jit(solution)/shard_map/ppermute | solution.py:20
  65.2 5.1 %collective-permute-start.19 = (bf16[192,256]{1,0:T(8,128)(2,1)S(1)}, bf16[192,256]{1,0:T(8,128)(2,1)S(1)}, u32[]{:S(2)}, u32[]{:S(2)}) collective-permute-start(bf16[192,256]{1,0:T(8,128)(2,1)S(1)} %shard_map.102.refs_0_), channel_id=1, source_target_pairs={{0,4},{1,5},{2,6},{3,7},{4,0},{5,1},{6,2},{7,3},{8,12},{9,13},{10,... | collective-permute-start | bytes 294920 | tf_op jit(solution)/shard_map/ppermute | solution.py:20
  66.3 3.9 %collective-permute-start.20 = (bf16[192,256]{1,0:T(8,128)(2,1)S(1)}, bf16[192,256]{1,0:T(8,128)(2,1)S(1)}, u32[]{:S(2)}, u32[]{:S(2)}) collective-permute-start(bf16[192,256]{1,0:T(8,128)(2,1)S(1)} %collective-permute-done.16.refs_1_), channel_id=1, source_target_pairs={{0,4},{1,5},{2,6},{3,7},{4,0},{5,1},{6,2},{7,3},{8,12},{9,13},{10,... | collective-permute-start | bytes 294920 | tf_op jit(solution)/shard_map/ppermute | solution.py:20
  68.0 2.3 %collective-permute-start.21 = (bf16[192,256]{1,0:T(8,128)(2,1)S(1)}, bf16[192,256]{1,0:T(8,128)(2,1)S(1)}, u32[]{:S(2)}, u32[]{:S(2)}) collective-permute-start(bf16[192,256]{1,0:T(8,128)(2,1)S(1)} %collective-permute-done.17.refs_2_), channel_id=1, source_target_pairs={{0,4},{1,5},{2,6},{3,7},{4,0},{5,1},{6,2},{7,3},{8,12},{9,13},{10,... | collective-permute-start | bytes 294920 | tf_op jit(solution)/shard_map/ppermute | solution.py:20
  69.5 1.3 %collective-permute-start.22 = (bf16[192,256]{1,0:T(8,128)(2,1)S(1)}, bf16[192,256]{1,0:T(8,128)(2,1)S(1)}, u32[]{:S(2)}, u32[]{:S(2)}) collective-permute-start(bf16[192,256]{1,0:T(8,128)(2,1)S(1)} %collective-permute-done.18.refs_3_), channel_id=1, source_target_pairs={{0,4},{1,5},{2,6},{3,7},{4,0},{5,1},{6,2},{7,3},{8,12},{9,13},{10,... | collective-permute-start | bytes 294920 | tf_op jit(solution)/shard_map/ppermute | solution.py:20

commit v4 on v1

--- a/solution.py
+++ b/solution.py
@@ -13,7 +13,7 @@
 VMEM = pl.BlockSpec(memory_space=pltpu.VMEM)
 ANY = pl.BlockSpec(memory_space=pl.ANY)
 SMEM = pl.BlockSpec(memory_space=pltpu.SMEM)
-DEPTH = 8
+DEPTH = 16
 
 
 def permute(value, pairs):
@@ -44,12 +44,12 @@
             where = jnp.int32(-1)
             for p in range(n_cand):
                 where = jnp.where(col == cand[p], p, where)
-            slot = jnp.int32(-1)
-            for s in range(slots):
+            slot = jnp.int32(0)
+            for s in range(1, slots):
                 slot = jnp.where(row == own[s], s, slot)
             order[n] = k
             code[n] = slot * n_cand + where
-            used = (where >= 0) & (slot >= 0) & (k < count[0, 0])
+            used = (where >= 0) & (k < count[0, 0])
             n = n + used.astype(jnp.int32)
         return n
 

time: 74.2 us -> 73.4 us (0.989)
  no operation moved by 1% of the time
where the time goes in v4:
time: 73.4 us; the launch traced here: 72.6 us
  waiting for transfers between devices  29.2 us (40%)
  starting transfers between devices  25.9 us (35%)
  Pallas kernels  15.9 us (22%)
  between operations  1.43 us (2%)
    ppermute x23, waiting for transfers between devices, permute(): return lax.ppermute(value, ('row', 'col'), pairs)  29.2 us
    ppermute x23, starting transfers between devices, permute(): return lax.ppermute(value, ('row', 'col'), pairs)  25.9 us
    pallas_call x1, Pallas kernels, per_device(): call(functools.partial(gather_kernel, n_high, slots), (pltpu.MemorySpace....  3.93 us
    pallas_call x1, Pallas kernels, per_device(): call(own_kernel, (jax.ShapeDtypeStruct(p_shape, F32), jax.ShapeDtypeStruc...  3.75 us
    pallas_call x1, Pallas kernels, per_device(): call(functools.partial(main_kernel, n_high, n_col), (jax.ShapeDtypeStruct...  3.66 us
    pallas_call x1, Pallas kernels, per_device(): call(final_kernel, pltpu.MemorySpace.HBM((t_count, t_count, width, width)...  2.46 us
  transfers between devices with their start and end apart: 23, of which 9 were waited for; matrix products, arithmetic and copies ran while one was open for 0% of the time, Pallas kernels for 13%

profile of v4, /device:TPU:0, one launch (start us, length us, event | category | flops | bytes accessed | tf_op | source)
XLA Modules:
  0.0 72.6 jit_solution(7911726500296271690)
XLA Ops:
  0.6 0.6 collective-permute-start
  1.2 4.4 %collective-permute-start.1 = (bf16[3,2,256,256]{3,2,1,0:T(8,128)(2,1)}, bf16[3,2,256,256]{3,2,1,0:T(8,128)(2,1)S(1)}, u32[]{:S(2)}, u32[]{:S(2)}) collective-permute-start(bf16[3,2,256,256]{3,2,1,0:T(8,128)(2,1)} %refs_0_.1), channel_id=1, source_target_pairs={{0,8},{5,13},{10,2},{15,7},{16,24},{21,29},{26,18},{31,23},{4,0},{... | collective-permute-start | bytes 2359304 | tf_op jit(solution)/shard_map/ppermute | solution.py:20
  5.6 0.2 collective-permute-start.3
  5.8 0.0 collective-permute-done.refs_1_
  5.8 1.5 %collective-permute-start.5 = (bf16[3,2,256,256]{3,2,1,0:T(8,128)(2,1)S(1)}, bf16[3,2,256,256]{3,2,1,0:T(8,128)(2,1)}, u32[]{:S(2)}, u32[]{:S(2)}) collective-permute-start(bf16[3,2,256,256]{3,2,1,0:T(8,128)(2,1)S(1)} %collective-permute-done.refs_1_), channel_id=1, source_target_pairs={{4,24},{1,29},{14,18},{11,23},{20,8},{17,13},{30,2},{27,7},{0,0},{... | collective-permute-start | bytes 2359304 | tf_op jit(solution)/shard_map/ppermute | solution.py:20
  7.4 13.8 %collective-permute-done.1.refs_2_ = bf16[3,2,256,256]{3,2,1,0:T(8,128)(2,1)S(1)} collective-permute-done((bf16[3,2,256,256]{3,2,1,0:T(8,128)(2,1)}, bf16[3,2,256,256]{3,2,1,0:T(8,128)(2,1)S(1)}, u32[]{:S(2)}, u32[]{:S(2)}) %collective-permute-start.1) | collective-permute-done | bytes 786464 | tf_op jit(solution)/shard_map/ppermute | solution.py:20
  21.2 0.0 collective-permute-start.2
  21.2 0.0 collective-permute-done.3.refs_2_
  21.2 0.5 collective-permute-start.4
  21.7 0.0 collective-permute-done.5.refs_3_
  21.7 2.1 %collective-permute-start.6 = (bf16[3,2,256,256]{3,2,1,0:T(8,128)(2,1)}, bf16[3,2,256,256]{3,2,1,0:T(8,128)(2,1)}, u32[]{:S(2)}, u32[]{:S(2)}) collective-permute-start(bf16[3,2,256,256]{3,2,1,0:T(8,128)(2,1)} %collective-permute-done.5.refs_3_), channel_id=1, source_target_pairs={{0,4},{1,5},{2,6},{3,7},{4,0},{5,1},{6,2},{7,3},{8,12},{9,13},{10,... | collective-permute-start | bytes 2359304 | tf_op jit(solution)/shard_map/ppermute | solution.py:20
  24.5 0.1 stack.39.where
  24.6 0.1 pad_add_fusion.me
  24.6 0.0 copy-start
  24.7 3.9 %shard_map.95 = (bf16[2,512,512]{2,1,0:T(8,128)(2,1)}, bf16[2,512,512]{2,1,0:T(8,128)(2,1)}) custom-call(s32[3]{0:T(128)S(1)} %pad_add_fusion.me, s32[1,1]{1,0:T(1,128)S(6)} %copy.10.count, s32[1,96]{1,0:T(1,128)} %rows_in.1, s32[1,96]{1,0:T(1,128)} %cols_in.1, s32[16]{0:T(128)} %panel_in.1, bf16[96,256,256]{2,1,0:T(8,128)(2,1)} %bitcast.15), custom_call_target="tpu_custom_call" | custom-call | flops 1048576 | bytes 10485760 | tf_op jit(solution)/shard_map/pallas_call | solution.py:387
  28.6 0.0 collective-permute-done.2.refs_3_
  28.6 0.0 copy-done
  28.6 0.0 copy-start.1
  28.6 0.0 copy-start.3
  28.6 3.8 %shard_map.96 = (f32[3,512,256]{2,1,0:T(8,128)S(1)}, bf16[3,256,512]{2,1,0:T(8,128)(2,1)S(1)}) custom-call(s32[6]{0:T(128)S(1)} %stack.39.where, bf16[2,512,512]{2,1,0:T(8,128)(2,1)} %get-tuple-element.16.w_in, bf16[3,2,256,256]{3,2,1,0:T(8,128)(2,1)S(1)} %copy-done, bf16[3,2,256,256]{3,2,1,0:T(8,128)(2,1)S(1)} %copy-done, ...), custom_call_target="tpu_custom_call" | custom-call | flops 805306368 | bytes 3145728 | tf_op jit(solution)/shard_map/pallas_call | solution.py:416
  32.4 0.0 collective-permute-done.4.refs_1_
  32.4 0.0 collective-permute-done.6.refs_4_
  32.4 0.0 copy-done.1
  32.4 0.0 copy-done.3
  32.4 3.7 %shard_map.97 = (f32[2,3,2,64,256]{4,3,2,1,0:T(8,128)S(1)}, bf16[2,3,2,64,256]{4,3,2,1,0:T(8,128)(2,1)S(1)}, f32[768,256]{1,0:T(8,128)S(1)}, bf16[768,256]{1,0:T(8,128)(2,1)S(1)}) custom-call(s32[6]{0:T(128)S(1)} %stack.39.where, f32[3,512,256]{2,1,0:T(8,128)S(1)} %get-tuple-element.17.p_own, bf16[3,256,512]{2,1,0:T(8,128)(2,1)S(1)} %get-tuple-element.18.old_t, ...), custom_call_target="tpu_custom_call" | custom-call | flops 2415919104 | bytes 3145728 | tf_op jit(solution)/shard_map/pallas_call | solution.py:444
  36.1 0.0 copy-start.2
  36.1 0.2 collective-permute-start.9
  36.3 2.1 %collective-permute-start.7 = (bf16[2,3,2,64,256]{4,3,2,1,0:T(8,128)(2,1)S(1)}, bf16[2,3,2,64,256]{4,3,2,1,0:T(8,128)(2,1)S(1)}, u32[]{:S(2)}, u32[]{:S(2)}) collective-permute-start(bf16[2,3,2,64,256]{4,3,2,1,0:T(8,128)(2,1)S(1)} %get-tuple-element.21), channel_id=1, source_target_pairs={{0,1},{1,0},{2,3},{3,2},{4,6},{5,7},{6,4},{7,5},{8,9},{9,8},{10,11... | collective-permute-start | bytes 1179656 | tf_op jit(solution)/shard_map/ppermute | solution.py:20
  38.4 0.0 collective-permute-done.9
  38.4 0.6 shard_map.100
  39.0 3.6 %collective-permute-start.10 = (bf16[192,256]{1,0:T(8,128)(2,1)S(1)}, bf16[192,256]{1,0:T(8,128)(2,1)S(1)}, u32[]{:S(2)}, u32[]{:S(2)}) collective-permute-start(bf16[192,256]{1,0:T(8,128)(2,1)S(1)} %get-tuple-element.27), channel_id=1, source_target_pairs={{0,8},{1,9},{2,10},{3,11},{4,12},{5,13},{6,14},{7,15},{8,0},{9,1},... | collective-permute-start | bytes 294920 | tf_op jit(solution)/shard_map/ppermute | solution.py:20
  42.6 0.6 collective-permute-start.11
  43.2 1.0 %collective-permute-start.12 = (bf16[192,256]{1,0:T(8,128)(2,1)S(1)}, bf16[192,256]{1,0:T(8,128)(2,1)S(1)}, u32[]{:S(2)}, u32[]{:S(2)}) collective-permute-start(bf16[192,256]{1,0:T(8,128)(2,1)S(1)} %get-tuple-element.29), channel_id=1, source_target_pairs={{0,24},{1,25},{2,26},{3,27},{4,28},{5,29},{6,30},{7,31},{8,16},{9,... | collective-permute-start | bytes 294920 | tf_op jit(solution)/shard_map/ppermute | solution.py:20
  44.1 1.1 %collective-permute-done.10.refs_1_ = bf16[192,256]{1,0:T(8,128)(2,1)S(1)} collective-permute-done((bf16[192,256]{1,0:T(8,128)(2,1)S(1)}, bf16[192,256]{1,0:T(8,128)(2,1)S(1)}, u32[]{:S(2)}, u32[]{:S(2)}) %collective-permute-start.10) | collective-permute-done | bytes 98336 | tf_op jit(solution)/shard_map/ppermute | solution.py:20
  45.2 4.3 %collective-permute-done.11.refs_2_ = bf16[192,256]{1,0:T(8,128)(2,1)S(1)} collective-permute-done((bf16[192,256]{1,0:T(8,128)(2,1)S(1)}, bf16[192,256]{1,0:T(8,128)(2,1)S(1)}, u32[]{:S(2)}, u32[]{:S(2)}) %collective-permute-start.11) | collective-permute-done | bytes 98336 | tf_op jit(solution)/shard_map/ppermute | solution.py:20
  49.5 0.0 collective-permute-done.12.refs_3_
  49.6 0.7 collective-permute-start.13
  50.2 1.6 %collective-permute-start.14 = (bf16[192,256]{1,0:T(8,128)(2,1)S(1)}, bf16[192,256]{1,0:T(8,128)(2,1)S(1)}, u32[]{:S(2)}, u32[]{:S(2)}) collective-permute-start(bf16[192,256]{1,0:T(8,128)(2,1)S(1)} %shard_map.101.refs_0_), channel_id=1, source_target_pairs={{0,2},{1,3},{2,0},{3,1},{4,6},{5,7},{6,4},{7,5},{8,10},{9,11},{10,... | collective-permute-start | bytes 294920 | tf_op jit(solution)/shard_map/ppermute | solution.py:20
  51.8 2.2 %collective-permute-start.15 = (bf16[192,256]{1,0:T(8,128)(2,1)S(1)}, bf16[192,256]{1,0:T(8,128)(2,1)S(1)}, u32[]{:S(2)}, u32[]{:S(2)}) collective-permute-start(bf16[192,256]{1,0:T(8,128)(2,1)S(1)} %shard_map.101.refs_0_), channel_id=1, source_target_pairs={{0,3},{1,2},{2,1},{3,0},{4,7},{5,6},{6,5},{7,4},{8,11},{9,10},{10,... | collective-permute-start | bytes 294920 | tf_op jit(solution)/shard_map/ppermute | solution.py:20
  54.0 0.0 collective-permute-done.7.received
  54.0 0.6 shard_map.98
  54.6 1.1 %collective-permute-start.8 = (bf16[1,3,2,64,256]{4,3,2,1,0:T(8,128)(2,1)S(1)}, bf16[1,3,2,64,256]{4,3,2,1,0:T(8,128)(2,1)S(1)}, u32[]{:S(2)}, u32[]{:S(2)}) collective-permute-start(bf16[1,3,2,64,256]{4,3,2,1,0:T(8,128)(2,1)S(1)} %get-tuple-element.23), channel_id=1, source_target_pairs={{0,2},{1,3},{2,0},{3,1},{4,5},{5,4},{6,7},{7,6},{8,10},{9,11},{10,... | collective-permute-start | bytes 589832 | tf_op jit(solution)/shard_map/ppermute | solution.py:20
  55.7 0.0 collective-permute-done.13.refs_1_
  55.7 3.6 %collective-permute-done.14.refs_2_ = bf16[192,256]{1,0:T(8,128)(2,1)S(1)} collective-permute-done((bf16[192,256]{1,0:T(8,128)(2,1)S(1)}, bf16[192,256]{1,0:T(8,128)(2,1)S(1)}, u32[]{:S(2)}, u32[]{:S(2)}) %collective-permute-start.14) | collective-permute-done | bytes 98336 | tf_op jit(solution)/shard_map/ppermute | solution.py:20
  59.3 1.5 %collective-permute-done.15.refs_3_ = bf16[192,256]{1,0:T(8,128)(2,1)S(1)} collective-permute-done((bf16[192,256]{1,0:T(8,128)(2,1)S(1)}, bf16[192,256]{1,0:T(8,128)(2,1)S(1)}, u32[]{:S(2)}, u32[]{:S(2)}) %collective-permute-start.15) | collective-permute-done | bytes 98336 | tf_op jit(solution)/shard_map/ppermute | solution.py:20
  60.8 0.1 shard_map.102.refs_0_
  60.9 1.7 %collective-permute-start.16 = (bf16[192,256]{1,0:T(8,128)(2,1)S(1)}, bf16[192,256]{1,0:T(8,128)(2,1)S(1)}, u32[]{:S(2)}, u32[]{:S(2)}) collective-permute-start(bf16[192,256]{1,0:T(8,128)(2,1)S(1)} %shard_map.102.refs_0_), channel_id=1, source_target_pairs={{0,8},{1,9},{2,10},{3,11},{4,12},{5,13},{6,14},{7,15},{8,0},{9,1},... | collective-permute-start | bytes 294920 | tf_op jit(solution)/shard_map/ppermute | solution.py:20
  62.6 0.7 collective-permute-start.17
  63.3 1.2 %collective-permute-start.18 = (bf16[192,256]{1,0:T(8,128)(2,1)S(1)}, bf16[192,256]{1,0:T(8,128)(2,1)S(1)}, u32[]{:S(2)}, u32[]{:S(2)}) collective-permute-start(bf16[192,256]{1,0:T(8,128)(2,1)S(1)} %shard_map.102.refs_0_), channel_id=1, source_target_pairs={{0,24},{1,25},{2,26},{3,27},{4,28},{5,29},{6,30},{7,31},{8,16},{9,... | collective-permute-start | bytes 294920 | tf_op jit(solution)/shard_map/ppermute | solution.py:20
  64.5 0.0 collective-permute-start.19
  64.5 1.1 %collective-permute-done.16.refs_1_ = bf16[192,256]{1,0:T(8,128)(2,1)S(1)} collective-permute-done((bf16[192,256]{1,0:T(8,128)(2,1)S(1)}, bf16[192,256]{1,0:T(8,128)(2,1)S(1)}, u32[]{:S(2)}, u32[]{:S(2)}) %collective-permute-start.16) | collective-permute-done | bytes 98336 | tf_op jit(solution)/shard_map/ppermute | solution.py:20
  65.6 0.0 collective-permute-start.20
  65.6 1.7 %collective-permute-done.17.refs_2_ = bf16[192,256]{1,0:T(8,128)(2,1)S(1)} collective-permute-done((bf16[192,256]{1,0:T(8,128)(2,1)S(1)}, bf16[192,256]{1,0:T(8,128)(2,1)S(1)}, u32[]{:S(2)}, u32[]{:S(2)}) %collective-permute-start.17) | collective-permute-done | bytes 98336 | tf_op jit(solution)/shard_map/ppermute | solution.py:20
  67.3 0.0 collective-permute-start.21
  67.3 1.6 %collective-permute-done.18.refs_3_ = bf16[192,256]{1,0:T(8,128)(2,1)S(1)} collective-permute-done((bf16[192,256]{1,0:T(8,128)(2,1)S(1)}, bf16[192,256]{1,0:T(8,128)(2,1)S(1)}, u32[]{:S(2)}, u32[]{:S(2)}) %collective-permute-start.18) | collective-permute-done | bytes 98336 | tf_op jit(solution)/shard_map/ppermute | solution.py:20
  68.8 0.0 collective-permute-start.22
  68.8 0.0 collective-permute-done.8.refs_1_
  68.8 0.7 shard_map.99
  69.5 0.0 collective-permute-done.19.refs_4_
  69.5 0.0 collective-permute-done.20.refs_5_
  69.5 0.0 collective-permute-done.21.refs_6_
  69.6 0.6 collective-permute-done.22.refs_7_
  70.1 0.0 copy-done.2
  70.1 2.5 %shard_map.103 = f32[3,3,256,256]{3,2,1,0:T(8,128)} custom-call(s32[6]{0:T(128)S(1)} %stack.39.where, bf16[3,3,256,256]{3,2,1,0:T(8,128)(2,1)S(1)} %copy-done.1, f32[3,256,256]{2,1,0:T(8,128)S(1)} %copy-done.2, bf16[192,256]{1,0:T(8,128)(2,1)S(1)} %shard_map.102.refs_0_, bf16[192,256]{1,0:T(8,128)(2,1)S(1)} %collective-permute-done.16.refs_1_, ...), custom_call_target="tpu_custom_call" | custom-call | flops 536870912 | bytes 3538944 | tf_op jit(solution)/shard_map/pallas_call | solution.py:515
  (1 shorter events, 0.0 us)
Async XLA Ops:
  0.6 5.2 %collective-permute-start = (bf16[3,2,256,256]{3,2,1,0:T(8,128)(2,1)}, bf16[3,2,256,256]{3,2,1,0:T(8,128)(2,1)S(1)}, u32[]{:S(2)}, u32[]{:S(2)}) collective-permute-start(bf16[3,2,256,256]{3,2,1,0:T(8,128)(2,1)} %refs_0_.1), channel_id=1, source_target_pairs={{0,4},{1,5},{2,6},{3,7},{4,0},{5,1},{6,2},{7,3},{8,12},{9,13},{10,... | collective-permute-start | bytes 2359304 | tf_op jit(solution)/shard_map/ppermute | solution.py:20
  1.2 20.0 %collective-permute-start.1 = (bf16[3,2,256,256]{3,2,1,0:T(8,128)(2,1)}, bf16[3,2,256,256]{3,2,1,0:T(8,128)(2,1)S(1)}, u32[]{:S(2)}, u32[]{:S(2)}) collective-permute-start(bf16[3,2,256,256]{3,2,1,0:T(8,128)(2,1)} %refs_0_.1), channel_id=1, source_target_pairs={{0,8},{5,13},{10,2},{15,7},{16,24},{21,29},{26,18},{31,23},{4,0},{... | collective-permute-start | bytes 2359304 | tf_op jit(solution)/shard_map/ppermute | solution.py:20
  5.6 15.6 %collective-permute-start.3 = (bf16[3,2,256,256]{3,2,1,0:T(8,128)(2,1)}, bf16[3,2,256,256]{3,2,1,0:T(8,128)(2,1)S(1)}, u32[]{:S(2)}, u32[]{:S(2)}) collective-permute-start(bf16[3,2,256,256]{3,2,1,0:T(8,128)(2,1)} %refs_0_.1), channel_id=1, source_target_pairs={{0,20},{5,17},{10,30},{15,27},{16,4},{21,1},{26,14},{31,11},{4,0},... | collective-permute-start | bytes 2359304 | tf_op jit(solution)/shard_map/ppermute | solution.py:20
  5.8 15.9 %collective-permute-start.5 = (bf16[3,2,256,256]{3,2,1,0:T(8,128)(2,1)S(1)}, bf16[3,2,256,256]{3,2,1,0:T(8,128)(2,1)}, u32[]{:S(2)}, u32[]{:S(2)}) collective-permute-start(bf16[3,2,256,256]{3,2,1,0:T(8,128)(2,1)S(1)} %collective-permute-done.refs_1_), channel_id=1, source_target_pairs={{4,24},{1,29},{14,18},{11,23},{20,8},{17,13},{30,2},{27,7},{0,0},{... | collective-permute-start | bytes 2359304 | tf_op jit(solution)/shard_map/ppermute | solution.py:20
  21.2 7.4 %collective-permute-start.2 = (bf16[3,2,256,256]{3,2,1,0:T(8,128)(2,1)S(1)}, bf16[3,2,256,256]{3,2,1,0:T(8,128)(2,1)S(1)}, u32[]{:S(2)}, u32[]{:S(2)}) collective-permute-start(bf16[3,2,256,256]{3,2,1,0:T(8,128)(2,1)S(1)} %collective-permute-done.1.refs_2_), channel_id=1, source_target_pairs={{0,4},{1,5},{2,6},{3,7},{4,0},{5,1},{6,2},{7,3},{8,12},{9,13},{10,... | collective-permute-start | bytes 2359304 | tf_op jit(solution)/shard_map/ppermute | solution.py:20
  21.2 11.2 %collective-permute-start.4 = (bf16[3,2,256,256]{3,2,1,0:T(8,128)(2,1)S(1)}, bf16[3,2,256,256]{3,2,1,0:T(8,128)(2,1)}, u32[]{:S(2)}, u32[]{:S(2)}) collective-permute-start(bf16[3,2,256,256]{3,2,1,0:T(8,128)(2,1)S(1)} %collective-permute-done.3.refs_2_), channel_id=1, source_target_pairs={{0,4},{1,5},{2,6},{3,7},{4,0},{5,1},{6,2},{7,3},{8,12},{9,13},{10,... | collective-permute-start | bytes 2359304 | tf_op jit(solution)/shard_map/ppermute | solution.py:20
  21.7 10.7 %collective-permute-start.6 = (bf16[3,2,256,256]{3,2,1,0:T(8,128)(2,1)}, bf16[3,2,256,256]{3,2,1,0:T(8,128)(2,1)}, u32[]{:S(2)}, u32[]{:S(2)}) collective-permute-start(bf16[3,2,256,256]{3,2,1,0:T(8,128)(2,1)} %collective-permute-done.5.refs_3_), channel_id=1, source_target_pairs={{0,4},{1,5},{2,6},{3,7},{4,0},{5,1},{6,2},{7,3},{8,12},{9,13},{10,... | collective-permute-start | bytes 2359304 | tf_op jit(solution)/shard_map/ppermute | solution.py:20
  24.6 4.0 %copy-start = (bf16[3,2,256,256]{3,2,1,0:T(8,128)(2,1)S(1)}, bf16[3,2,256,256]{3,2,1,0:T(8,128)(2,1)}, u32[]{:S(2)}) copy-start(bf16[3,2,256,256]{3,2,1,0:T(8,128)(2,1)} %refs_0_.1) | copy-start | bytes 2359300
  28.6 3.8 %copy-start.1 = (bf16[3,3,256,256]{3,2,1,0:T(8,128)(2,1)S(1)}, bf16[3,3,256,256]{3,2,1,0:T(8,128)(2,1)}, u32[]{:S(2)}) copy-start(bf16[3,3,256,256]{3,2,1,0:T(8,128)(2,1)} %new.3) | copy-start | bytes 3538948
  28.6 3.8 %copy-start.3 = (bf16[2,512,512]{2,1,0:T(8,128)(2,1)S(1)}, bf16[2,512,512]{2,1,0:T(8,128)(2,1)}, u32[]{:S(2)}) copy-start(bf16[2,512,512]{2,1,0:T(8,128)(2,1)} %get-tuple-element.19.refs_0_) | copy-start | bytes 3145732
  36.1 34.0 %copy-start.2 = (f32[3,256,256]{2,1,0:T(8,128)S(1)}, f32[3,256,256]{2,1,0:T(8,128)}, u32[]{:S(2)}) copy-start(f32[3,256,256]{2,1,0:T(8,128)} %diag.1) | copy-start | bytes 2359300
  36.1 2.3 %collective-permute-start.9 = (bf16[768,256]{1,0:T(8,128)(2,1)S(1)}, bf16[768,256]{1,0:T(8,128)(2,1)S(1)}, u32[]{:S(2)}, u32[]{:S(2)}) collective-permute-start(bf16[768,256]{1,0:T(8,128)(2,1)S(1)} %get-tuple-element.25), channel_id=1, source_target_pairs={{0,4},{1,5},{2,6},{3,7},{4,0},{5,1},{6,2},{7,3},{8,12},{9,13},{10,... | collective-permute-start | bytes 1179656 | tf_op jit(solution)/shard_map/ppermute | solution.py:20
  36.3 17.7 %collective-permute-start.7 = (bf16[2,3,2,64,256]{4,3,2,1,0:T(8,128)(2,1)S(1)}, bf16[2,3,2,64,256]{4,3,2,1,0:T(8,128)(2,1)S(1)}, u32[]{:S(2)}, u32[]{:S(2)}) collective-permute-start(bf16[2,3,2,64,256]{4,3,2,1,0:T(8,128)(2,1)S(1)} %get-tuple-element.21), channel_id=1, source_target_pairs={{0,1},{1,0},{2,3},{3,2},{4,6},{5,7},{6,4},{7,5},{8,9},{9,8},{10,11... | collective-permute-start | bytes 1179656 | tf_op jit(solution)/shard_map/ppermute | solution.py:20
  39.0 6.2 %collective-permute-start.10 = (bf16[192,256]{1,0:T(8,128)(2,1)S(1)}, bf16[192,256]{1,0:T(8,128)(2,1)S(1)}, u32[]{:S(2)}, u32[]{:S(2)}) collective-permute-start(bf16[192,256]{1,0:T(8,128)(2,1)S(1)} %get-tuple-element.27), channel_id=1, source_target_pairs={{0,8},{1,9},{2,10},{3,11},{4,12},{5,13},{6,14},{7,15},{8,0},{9,1},... | collective-permute-start | bytes 294920 | tf_op jit(solution)/shard_map/ppermute | solution.py:20
  42.6 6.9 %collective-permute-start.11 = (bf16[192,256]{1,0:T(8,128)(2,1)S(1)}, bf16[192,256]{1,0:T(8,128)(2,1)S(1)}, u32[]{:S(2)}, u32[]{:S(2)}) collective-permute-start(bf16[192,256]{1,0:T(8,128)(2,1)S(1)} %get-tuple-element.28), channel_id=1, source_target_pairs={{0,16},{1,17},{2,18},{3,19},{4,20},{5,21},{6,22},{7,23},{8,24},{9,... | collective-permute-start | bytes 294920 | tf_op jit(solution)/shard_map/ppermute | solution.py:20
  43.2 6.4 %collective-permute-start.12 = (bf16[192,256]{1,0:T(8,128)(2,1)S(1)}, bf16[192,256]{1,0:T(8,128)(2,1)S(1)}, u32[]{:S(2)}, u32[]{:S(2)}) collective-permute-start(bf16[192,256]{1,0:T(8,128)(2,1)S(1)} %get-tuple-element.29), channel_id=1, source_target_pairs={{0,24},{1,25},{2,26},{3,27},{4,28},{5,29},{6,30},{7,31},{8,16},{9,... | collective-permute-start | bytes 294920 | tf_op jit(solution)/shard_map/ppermute | solution.py:20
  49.6 6.1 %collective-permute-start.13 = (bf16[192,256]{1,0:T(8,128)(2,1)S(1)}, bf16[192,256]{1,0:T(8,128)(2,1)S(1)}, u32[]{:S(2)}, u32[]{:S(2)}) collective-permute-start(bf16[192,256]{1,0:T(8,128)(2,1)S(1)} %shard_map.101.refs_0_), channel_id=1, source_target_pairs={{0,1},{1,0},{2,3},{3,2},{4,5},{5,4},{6,7},{7,6},{8,9},{9,8},{10,11... | collective-permute-start | bytes 294920 | tf_op jit(solution)/shard_map/ppermute | solution.py:20
  50.2 9.1 %collective-permute-start.14 = (bf16[192,256]{1,0:T(8,128)(2,1)S(1)}, bf16[192,256]{1,0:T(8,128)(2,1)S(1)}, u32[]{:S(2)}, u32[]{:S(2)}) collective-permute-start(bf16[192,256]{1,0:T(8,128)(2,1)S(1)} %shard_map.101.refs_0_), channel_id=1, source_target_pairs={{0,2},{1,3},{2,0},{3,1},{4,6},{5,7},{6,4},{7,5},{8,10},{9,11},{10,... | collective-permute-start | bytes 294920 | tf_op jit(solution)/shard_map/ppermute | solution.py:20
  51.8 9.0 %collective-permute-start.15 = (bf16[192,256]{1,0:T(8,128)(2,1)S(1)}, bf16[192,256]{1,0:T(8,128)(2,1)S(1)}, u32[]{:S(2)}, u32[]{:S(2)}) collective-permute-start(bf16[192,256]{1,0:T(8,128)(2,1)S(1)} %shard_map.101.refs_0_), channel_id=1, source_target_pairs={{0,3},{1,2},{2,1},{3,0},{4,7},{5,6},{6,5},{7,4},{8,11},{9,10},{10,... | collective-permute-start | bytes 294920 | tf_op jit(solution)/shard_map/ppermute | solution.py:20
  54.6 14.2 %collective-permute-start.8 = (bf16[1,3,2,64,256]{4,3,2,1,0:T(8,128)(2,1)S(1)}, bf16[1,3,2,64,256]{4,3,2,1,0:T(8,128)(2,1)S(1)}, u32[]{:S(2)}, u32[]{:S(2)}) collective-permute-start(bf16[1,3,2,64,256]{4,3,2,1,0:T(8,128)(2,1)S(1)} %get-tuple-element.23), channel_id=1, source_target_pairs={{0,2},{1,3},{2,0},{3,1},{4,5},{5,4},{6,7},{7,6},{8,10},{9,11},{10,... | collective-permute-start | bytes 589832 | tf_op jit(solution)/shard_map/ppermute | solution.py:20
  60.9 4.7 %collective-permute-start.16 = (bf16[192,256]{1,0:T(8,128)(2,1)S(1)}, bf16[192,256]{1,0:T(8,128)(2,1)S(1)}, u32[]{:S(2)}, u32[]{:S(2)}) collective-permute-start(bf16[192,256]{1,0:T(8,128)(2,1)S(1)} %shard_map.102.refs_0_), channel_id=1, source_target_pairs={{0,8},{1,9},{2,10},{3,11},{4,12},{5,13},{6,14},{7,15},{8,0},{9,1},... | collective-permute-start | bytes 294920 | tf_op jit(solution)/shard_map/ppermute | solution.py:20
  62.6 4.6 %collective-permute-start.17 = (bf16[192,256]{1,0:T(8,128)(2,1)S(1)}, bf16[192,256]{1,0:T(8,128)(2,1)S(1)}, u32[]{:S(2)}, u32[]{:S(2)}) collective-permute-start(bf16[192,256]{1,0:T(8,128)(2,1)S(1)} %shard_map.102.refs_0_), channel_id=1, source_target_pairs={{0,16},{1,17},{2,18},{3,19},{4,20},{5,21},{6,22},{7,23},{8,24},{9,... | collective-permute-start | bytes 294920 | tf_op jit(solution)/shard_map/ppermute | solution.py:20
  63.3 5.5 %collective-permute-start.18 = (bf16[192,256]{1,0:T(8,128)(2,1)S(1)}, bf16[192,256]{1,0:T(8,128)(2,1)S(1)}, u32[]{:S(2)}, u32[]{:S(2)}) collective-permute-start(bf16[192,256]{1,0:T(8,128)(2,1)S(1)} %shard_map.102.refs_0_), channel_id=1, source_target_pairs={{0,24},{1,25},{2,26},{3,27},{4,28},{5,29},{6,30},{7,31},{8,16},{9,... | collective-permute-start | bytes 294920 | tf_op jit(solution)/shard_map/ppermute | solution.py:20
  64.5 5.1 %collective-permute-start.19 = (bf16[192,256]{1,0:T(8,128)(2,1)S(1)}, bf16[192,256]{1,0:T(8,128)(2,1)S(1)}, u32[]{:S(2)}, u32[]{:S(2)}) collective-permute-start(bf16[192,256]{1,0:T(8,128)(2,1)S(1)} %shard_map.102.refs_0_), channel_id=1, source_target_pairs={{0,4},{1,5},{2,6},{3,7},{4,0},{5,1},{6,2},{7,3},{8,12},{9,13},{10,... | collective-permute-start | bytes 294920 | tf_op jit(solution)/shard_map/ppermute | solution.py:20
  65.6 4.0 %collective-permute-start.20 = (bf16[192,256]{1,0:T(8,128)(2,1)S(1)}, bf16[192,256]{1,0:T(8,128)(2,1)S(1)}, u32[]{:S(2)}, u32[]{:S(2)}) collective-permute-start(bf16[192,256]{1,0:T(8,128)(2,1)S(1)} %collective-permute-done.16.refs_1_), channel_id=1, source_target_pairs={{0,4},{1,5},{2,6},{3,7},{4,0},{5,1},{6,2},{7,3},{8,12},{9,13},{10,... | collective-permute-start | bytes 294920 | tf_op jit(solution)/shard_map/ppermute | solution.py:20
  67.3 2.3 %collective-permute-start.21 = (bf16[192,256]{1,0:T(8,128)(2,1)S(1)}, bf16[192,256]{1,0:T(8,128)(2,1)S(1)}, u32[]{:S(2)}, u32[]{:S(2)}) collective-permute-start(bf16[192,256]{1,0:T(8,128)(2,1)S(1)} %collective-permute-done.17.refs_2_), channel_id=1, source_target_pairs={{0,4},{1,5},{2,6},{3,7},{4,0},{5,1},{6,2},{7,3},{8,12},{9,13},{10,... | collective-permute-start | bytes 294920 | tf_op jit(solution)/shard_map/ppermute | solution.py:20
  68.8 1.3 %collective-permute-start.22 = (bf16[192,256]{1,0:T(8,128)(2,1)S(1)}, bf16[192,256]{1,0:T(8,128)(2,1)S(1)}, u32[]{:S(2)}, u32[]{:S(2)}) collective-permute-start(bf16[192,256]{1,0:T(8,128)(2,1)S(1)} %collective-permute-done.18.refs_3_), channel_id=1, source_target_pairs={{0,4},{1,5},{2,6},{3,7},{4,0},{5,1},{6,2},{7,3},{8,12},{9,13},{10,... | collective-permute-start | bytes 294920 | tf_op jit(solution)/shard_map/ppermute | solution.py:20
